TPU v7x, 512 devices: a whole 4x8x8 slice. The times are simulated.
512 devices in a mesh: blk: 512 (over x, z, y, core).
Axes of the slice: x: 4, y: 8, z: 8, core: 2. Of those that a mesh axis runs over, the one named last changes fastest.
Arguments:
- positive_row: float32 [256, 131072], P(None, 'blk'), may hold values from -6 to 160, as said below
- negative_row: float32 [256, 131072], P(None, 'blk'), may hold values from -5 to 5
Outputs:
- positive_out: float32 [256, 131072], P(None, 'blk')
- negative_out: float32 [256, 131072], P(None, 'blk')
Inputs may be any that keep to these rules, and one draw needn't show every extreme that they name: `positive_row`: the first 256 columns form an upper triangular block whose diagonal lies between 80 and 160.
All inputs are finite; a program needn't handle non-finite values.
Results may differ from a plain program's by a relative error of at most 0.00017.
Values sent between devices are 32-bit elements; how exact they have to be, the bound alone decides.
No kernel may reach another device: no remote copies, remote signals or barrier semaphores. Data moves between devices by JAX's collectives and lax.ppermute only.
A program may use at most 64 MiB of HBM per device.

v0:
```python
import jax
import jax.numpy as jnp
from jax import lax
from jax.sharding import PartitionSpec as P

STEPS = 2
NEWTON = 4


HIGHEST = lax.Precision.HIGHEST


def broadcast(array, axis, root):
    mine = lax.axis_index(axis) == root
    return lax.psum(jnp.where(mine, array, jnp.zeros_like(array)), axis)


def shifted(block, axis, distance):
    devices = range(lax.axis_size(axis))
    route = [(i - distance, i) for i in devices if i - distance in devices]
    return lax.ppermute(block, axis, route)


def identity_of(size):
    rows_index = lax.broadcasted_iota(jnp.int32, (size, size), 0)
    cols_index = lax.broadcasted_iota(jnp.int32, (size, size), 1)
    return jnp.where(rows_index == cols_index, 1.0, 0.0).astype(jnp.float32)


def root_series(gram_part, identity):
    inner = 0.3125 * identity + 0.2734375 * gram_part
    inner = 0.375 * identity + jnp.dot(gram_part, inner, precision=HIGHEST)
    inner = 0.5 * identity + jnp.dot(gram_part, inner, precision=HIGHEST)
    return identity + jnp.dot(gram_part, inner, precision=HIGHEST)


def solve_coupling(lead_p, lead_n):
    identity = identity_of(lead_p.shape[0])
    diag_values = jnp.sum(lead_p * identity, axis=1)
    approx = identity * (1.0 / diag_values)[:, None]
    lead_t = lead_p.T
    for newton_index in range(NEWTON):
        product = jnp.dot(lead_t, approx, precision=HIGHEST)
        approx = jnp.dot(approx, 2.0 * identity - product, precision=HIGHEST)
    return jnp.dot(approx, lead_n.T, precision=HIGHEST)


def roots_from(coupling_t):
    identity = identity_of(coupling_t.shape[0])
    gram_top = jnp.dot(coupling_t, coupling_t.T, precision=HIGHEST)
    gram_bottom = jnp.dot(coupling_t.T, coupling_t, precision=HIGHEST)
    return (root_series(gram_top, identity), root_series(gram_bottom, identity))


def build_reflector(lead_p, lead_n):
    coupling_t = solve_coupling(lead_p, lead_n)
    root_top, root_bottom = roots_from(coupling_t)
    return (coupling_t, root_top, root_bottom)


def empty_factors(lead_p, lead_n):
    zeros_block = jnp.zeros_like(lead_p)
    return (zeros_block, zeros_block, zeros_block)


def apply_reflector(coupling_t, root_top, root_bottom, positive, negative):
    wide_p = positive - jnp.dot(coupling_t, negative, precision=HIGHEST)
    wide_n = negative - jnp.dot(coupling_t.T, positive, precision=HIGHEST)
    new_p = jnp.dot(root_top, wide_p, precision=HIGHEST)
    new_n = jnp.dot(root_bottom, wide_n, precision=HIGHEST)
    return (new_p, new_n)


def on_device(positive_row, negative_row):
    my_index = lax.axis_index("blk")
    positive = positive_row
    negative = negative_row
    for step_index in range(STEPS):
        is_owner = my_index == step_index
        factors = lax.cond(is_owner, build_reflector, empty_factors, positive, negative)
        coupling_t, root_top, root_bottom = (
            broadcast(factors[0], "blk", step_index),
            broadcast(factors[1], "blk", step_index),
            broadcast(factors[2], "blk", step_index),
        )
        new_p, new_n = apply_reflector(coupling_t, root_top, root_bottom, positive, negative)
        positive = shifted(new_p, "blk", 1)
        negative = new_n
    return (positive, negative)


def solution(mesh):
    in_specs = (P(None, "blk"), P(None, "blk"))
    out_specs = (P(None, "blk"), P(None, "blk"))
    return jax.shard_map(
        on_device, mesh=mesh, in_specs=in_specs, out_specs=out_specs, check_vma=False
    )
```

profile of v0, /device:TPU:6, one launch (start us, length us, event | category | flops | bytes accessed | tf_op | source)
XLA Modules:
  0.0 598.3 jit_solution(224445151067089374)
XLA Ops:
  7.2 0.0 all-reduce.7.cloned.1.call-start
  7.2 0.1 conditional.2
  7.3 0.7 broadcast_select_fusion.5
  8.0 0.7 broadcast_select_fusion.4
  8.8 0.7 broadcast_select_fusion.3
  9.5 0.0 all-reduce.7.cloned.1.call-update
  9.5 0.0 all-reduce.5.cloned.1.call-start
  9.6 283.2 %all-reduce.7.cloned.1.call-done = (f32[256,256]{1,0:T(8,128)}, f32[256,256]{1,0:T(8,128)}, f32[256,256]{1,0:T(8,128)}) async-done(((f32[256,256]{1,0:T(8,128)}, f32[256,256]{1,0:T(8,128)}, f32[256,256]{1,0:T(8,128)}), (f32[256,256]{1,0:T(8,128)}, f32[256,256]{1,0:T(8,128)}, f32[256,256]{1,0:T(8,128)})) %all-reduce.7.cloned.1.call-update) | async-done | bytes 786448 | tf_op jit(solution)/shard_map/psum | solution.py:15
  292.7 0.0 copy-done
  292.7 0.0 copy-done.6
  292.7 1.4 convolution_subtract_fusion.3
  294.1 0.4 fusion.88
  294.5 2.8 collective-permute-start
  297.3 0.6 convolution_subtract_fusion.2
  297.9 0.4 fusion.89
  298.3 8.2 %collective-permute-done = f32[256,256]{1,0:T(8,128)S(1)} collective-permute-done((f32[256,256]{1,0:T(8,128)S(1)}, f32[256,256]{1,0:T(8,128)S(1)}, u32[]{:S(2)}, u32[]{:S(2)}) %collective-permute-start) | collective-permute-done | bytes 262176 | tf_op jit(solution)/shard_map/ppermute | solution.py:21
  306.6 0.3 conditional.3
  306.8 0.7 broadcast_select_fusion.2
  307.6 0.8 broadcast_select_fusion
  308.4 0.0 all-reduce.5.cloned.1.call-update
  308.4 268.5 %all-reduce.5.cloned.1.call-done = (f32[256,256]{1,0:T(8,128)}, f32[256,256]{1,0:T(8,128)}, f32[256,256]{1,0:T(8,128)}) async-done(((f32[256,256]{1,0:T(8,128)}, f32[256,256]{1,0:T(8,128)}, f32[256,256]{1,0:T(8,128)}), (f32[256,256]{1,0:T(8,128)}, f32[256,256]{1,0:T(8,128)}, f32[256,256]{1,0:T(8,128)})) %all-reduce.5.cloned.1.call-update) | async-done | bytes 786448 | tf_op jit(solution)/shard_map/psum | solution.py:15
  576.9 1.4 convolution_subtract_fusion.1
  578.3 0.0 copy-done.13
  578.3 0.0 copy-start.9
  578.3 0.4 fusion.90
  578.7 0.0 copy-start.11
  578.7 2.8 collective-permute-start.1
  581.5 0.6 convolution_subtract_fusion
  582.1 0.0 copy-done.11
  582.1 1.1 fusion.91
  583.2 7.5 %collective-permute-done.1 = f32[256,256]{1,0:T(8,128)S(1)} collective-permute-done((f32[256,256]{1,0:T(8,128)S(1)}, f32[256,256]{1,0:T(8,128)S(1)}, u32[]{:S(2)}, u32[]{:S(2)}) %collective-permute-start.1) | collective-permute-done | bytes 262176 | tf_op jit(solution)/shard_map/ppermute | solution.py:21
  590.7 0.7 copy.23
  (16 shorter events, 0.1 us)
Async XLA Ops:
  7.2 285.6 %all-reduce.7.cloned.1.call-start = ((), (), s32[]{:S(2)}) async-start(), calls=%async_computation.1 | async-start | bytes 1572864 | tf_op jit(solution)/shard_map/psum | solution.py:15
  9.5 283.2 %copy-start = (f32[256,256]{1,0:T(8,128)S(1)}, f32[256,256]{1,0:T(8,128)}, u32[]{:S(2)}) copy-start(f32[256,256]{1,0:T(8,128)} %param.6) | copy-start | bytes 786436
  9.5 283.2 %copy-start.6 = (f32[256,256]{1,0:T(8,128)S(1)}, f32[256,256]{1,0:T(8,128)}, u32[]{:S(2)}) copy-start(f32[256,256]{1,0:T(8,128)} %param.7) | copy-start | bytes 786436
  9.5 567.4 %all-reduce.5.cloned.1.call-start = ((), (), s32[]{:S(2)}) async-start(), calls=%async_computation | async-start | bytes 1572864 | tf_op jit(solution)/shard_map/psum | solution.py:15
  292.7 1.4 copy-start.12
  294.1 3.2 copy-start.8
  294.5 3.4 copy-start.10
  294.5 12.0 %collective-permute-start = (f32[256,256]{1,0:T(8,128)S(1)}, f32[256,256]{1,0:T(8,128)S(1)}, u32[]{:S(2)}, u32[]{:S(2)}) collective-permute-start(f32[256,256]{1,0:T(8,128)S(1)} %fusion.88), channel_id=1, source_target_pairs={{0,1},{1,2},{2,3},{3,4},{4,5},{5,6},{6,7},{7,8},{8,9},{9,10},{10,1... | collective-permute-start | bytes 786440 | tf_op jit(solution)/shard_map/ppermute | solution.py:21
  576.9 1.4 copy-start.13
  578.3 3.2 copy-start.9
  578.7 3.4 copy-start.11
  578.7 12.0 %collective-permute-start.1 = (f32[256,256]{1,0:T(8,128)S(1)}, f32[256,256]{1,0:T(8,128)S(1)}, u32[]{:S(2)}, u32[]{:S(2)}) collective-permute-start(f32[256,256]{1,0:T(8,128)S(1)} %fusion.90), channel_id=1, source_target_pairs={{0,1},{1,2},{2,3},{3,4},{4,5},{5,6},{6,7},{7,8},{8,9},{9,10},{10,1... | collective-permute-start | bytes 786440 | tf_op jit(solution)/shard_map/ppermute | solution.py:21
Sparse Core Ops, SparseCore 0:
  14.0 278.6 all-reduce.6
  308.5 268.3 all-reduce.4
where the time goes:
time: 599 us; the launch traced here: 598 us
  waiting for transfers between devices  567 us (95%)
  between operations  14.2 us (2%)
  matrix products  6.16 us (1%)
    psum x2, waiting for transfers between devices, broadcast(): return lax.psum(jnp.where(mine, array, jnp.zeros_like(array)), axis)  552 us
    ppermute x2, waiting for transfers between devices, shifted(): return lax.ppermute(block, axis, route)  15.8 us
  transfers between devices with their start and end apart: 4, of which 4 were waited for; matrix products, arithmetic and copies ran while one was open for 0% of the time, Pallas kernels for 0%

commit v1 on v0

v1 whole, which is shorter than its diff:
```python
import jax
import jax.numpy as jnp
from jax import lax
from jax.experimental import pallas as pl
from jax.experimental.pallas import tpu as pltpu
from jax.sharding import PartitionSpec as P

B = 256
AXIS = "blk"

XS, ZS, YS = 4, 8, 8


def position(x, z, y, core):
    return (((x % XS) * ZS + z % ZS) * YS + y % YS) * 2 + core


TREE = (
    (
        ((2, 0, 0), (-1, 0, 0), (1, 0, 0)),
        ((0, 4, 0), (0, -2, 0), (0, 2, 0)),
        ((0, 0, 4), (0, 0, -2), (0, 0, 2)),
        ((0, 1, 1), (0, 1, 0), (0, 0, 1)),
    ),
    (
        ((0, 4, 0), (0, -2, 0), (0, 2, 0)),
        ((0, 0, 4), (0, 0, -2), (0, 0, 2)),
        ((2, 0, 0), (-1, 0, 0), (1, 0, 0)),
        ((0, -1, -1), (0, -1, 0), (0, 0, -1)),
    ),
)


def tree_rounds():
    holders = [[(0, 0, 0)], [(0, 0, 0)]]
    rounds = []
    for r in range(len(TREE[0])):
        permutes = []
        fresh = [[], []]
        for k in range(len(TREE[0][r])):
            pairs = []
            for core in range(2):
                dx, dz, dy = TREE[core][r][k]
                for x, z, y in holders[core]:
                    to = ((x + dx) % XS, (z + dz) % ZS, (y + dy) % YS)
                    fresh[core].append(to)
                    pairs.append((position(x, z, y, core), position(*to, core)))
            permutes.append(pairs)
        for core in range(2):
            holders[core] += fresh[core]
        rounds.append(permutes)
    return rounds


def halves(a):
    high = a.astype(jnp.bfloat16)
    low = (a - high.astype(jnp.float32)).astype(jnp.bfloat16)
    return high, low


def dot(a, b):
    left = jnp.concatenate([a[0], a[0], a[1]], axis=1)
    right = jnp.concatenate([b[0], b[1], b[0]], axis=0)
    return jnp.dot(left, right, preferred_element_type=jnp.float32)


def eye():
    rows = lax.broadcasted_iota(jnp.int32, (B, B), 0)
    cols = lax.broadcasted_iota(jnp.int32, (B, B), 1)
    return jnp.where(rows == cols, 1.0, 0.0).astype(jnp.float32)


def coupling_of(lead_p, lead_n, identity):
    diag = jnp.sum(lead_p * identity, axis=1, keepdims=True)
    w1 = identity - lead_p * (1.0 / diag)
    h1 = halves(w1)
    w2 = dot(h1, h1)
    m1 = lead_n + dot(halves(lead_n), h1)
    h2 = halves(w2)
    w4 = dot(h2, h2)
    m2 = m1 + dot(halves(m1), h2)
    h4 = halves(w4)
    w8 = dot(h4, h4)
    m3 = m2 + dot(halves(m2), h4)
    m4 = m3 + dot(halves(m3), halves(w8))
    diag_row = jnp.sum(lead_p * identity, axis=0, keepdims=True)
    return m4 * (1.0 / diag_row)


def root_of(gram, identity):
    e = halves(gram)
    square = dot(e, e)
    inner = 0.375 * identity + 0.3125 * gram + 0.2734375 * square
    return identity + 0.5 * gram + dot(halves(square), halves(inner))


def roots_of(k, kt, identity):
    top = root_of(dot(kt, k), identity)
    bottom = root_of(dot(k, kt), identity)
    return halves(top), halves(bottom)


def factor_kernel(me_ref, own_ref, partner_ref, out_ref):
    me = me_ref[0]

    @pl.when(me >= 2)
    def _():
        out_ref[...] = jnp.zeros_like(out_ref)

    @pl.when(me < 2)
    def _():
        identity = eye()
        mine, other = own_ref[...], partner_ref[...]
        first, second = jnp.where(me == 0, mine, other), jnp.where(me == 0, other, mine)
        p0, n0, p1, n1 = first[:B, :], first[B:, :], second[:B, :], second[B:, :]
        k0 = coupling_of(p0, n0, identity)
        k, kt = halves(k0), halves(k0.T)
        top, bottom = roots_of(k, kt, identity)
        lead_p = dot(top, halves(p0 - dot(kt, halves(n0))))
        lead_n = dot(bottom, halves(n1 - dot(k, halves(p1))))
        k1 = coupling_of(lead_p, lead_n, identity)
        out_ref[...] = jnp.where(me == 0, k0, k1)


def apply_kernel(k_ref, back2_ref, back1_ref, own_ref, p_ref, n_ref):
    identity = eye()
    k0, k1 = k_ref[0], k_ref[1]
    h0, t0 = halves(k0), halves(k0.T)
    h1, t1 = halves(k1), halves(k1.T)
    top0, bottom0 = roots_of(h0, t0, identity)
    top1, bottom1 = roots_of(h1, t1, identity)
    p2, n2 = back2_ref[:B, :], back2_ref[B:, :]
    p1, n1 = back1_ref[:B, :], back1_ref[B:, :]
    p0, n0 = own_ref[:B, :], own_ref[B:, :]
    cat = lambda a, b: jnp.concatenate([a, b], axis=1)
    first_p = dot(top0, halves(cat(p2, p1) - dot(t0, halves(cat(n2, n1)))))
    first_n = dot(bottom0, halves(cat(n1, n0) - dot(h0, halves(cat(p1, p0)))))
    p_ref[...] = dot(top1, halves(first_p[:, :B] - dot(t1, halves(first_n[:, :B]))))
    n_ref[...] = dot(bottom1, halves(first_n[:, B:] - dot(h1, halves(first_p[:, B:]))))


VMEM = pl.BlockSpec(memory_space=pltpu.VMEM)
SMEM = pl.BlockSpec(memory_space=pltpu.SMEM)


def on_device(positive_row, negative_row):
    me = lax.axis_index(AXIS)
    devices = lax.axis_size(AXIS)
    cores = [[i, i + 1] for i in range(0, devices, 2)]
    own = jnp.concatenate([positive_row, negative_row], axis=0)
    odd = me % 2 == 1
    swap = [(i, i ^ 1) for i in range(devices)]
    partner = lax.ppermute(own, AXIS, swap)

    route = [(i, i + (1 if i % 2 else 3)) for i in range(devices)]
    crossed = lax.ppermute(own, AXIS, [(i, j) for i, j in route if j < devices])

    factor = pl.pallas_call(
        factor_kernel,
        out_shape=jax.ShapeDtypeStruct((B, B), jnp.float32),
        in_specs=[SMEM, VMEM, VMEM],
        out_specs=VMEM,
    )(jnp.reshape(me, (1,)).astype(jnp.int32), own, partner)

    held = factor
    rounds = tree_rounds()
    for number, permutes in enumerate(rounds):
        if number == len(rounds) - 1:
            held, crossed = lax.optimization_barrier((held, crossed))
            back2 = lax.ppermute(crossed, AXIS, swap)
        arrived = [lax.ppermute(held, AXIS, pairs) for pairs in permutes]
        for block in arrived:
            held = held + block
    back1 = jnp.where(odd, partner, crossed)

    both = lax.all_gather(held, AXIS, axis=0, axis_index_groups=cores)
    return pl.pallas_call(
        apply_kernel,
        out_shape=[jax.ShapeDtypeStruct((B, B), jnp.float32)] * 2,
        in_specs=[VMEM] * 4,
        out_specs=[VMEM] * 2,
    )(both, back2, back1, own)


def solution(mesh):
    spec = P(None, AXIS)
    return jax.shard_map(
        on_device, mesh=mesh, in_specs=(spec, spec), out_specs=(spec, spec), check_vma=False
    )
```

time: 599 us -> 86.2 us (0.14)
  the two profiles are of different devices: /device:TPU:6 before, /device:TPU:221 now
where the time goes in v1:
time: 86.2 us; the launch traced here: 85.7 us
  waiting for transfers between devices  50.6 us (59%)
  starting transfers between devices  18.7 us (22%)
  Pallas kernels  8.35 us (10%)
  local copies, waits for them, and re-layouts  2.66 us (3%)
  blocking collectives  2.31 us (3%)
  other arithmetic  2.13 us (2%)
  between operations  0.92 us (1%)
    ppermute x12, waiting for transfers between devices, on_device(): arrived = [lax.ppermute(held, AXIS, pairs) for pairs in permutes]  40 us
    ppermute x1, waiting for transfers between devices, on_device(): crossed = lax.ppermute(own, AXIS, [(i, j) for i, j in route if j < devices])  9.11 us
    ppermute x12, starting transfers between devices, on_device(): arrived = [lax.ppermute(held, AXIS, pairs) for pairs in permutes]  8.85 us
    pallas_call x1, Pallas kernels, on_device(): pl.pallas_call(apply_kernel, out_shape=[jax.ShapeDtypeStruct((B, B), jnp....  6.43 us
    ppermute x1, starting transfers between devices, on_device(): crossed = lax.ppermute(own, AXIS, [(i, j) for i, j in route if j < devices])  4.67 us
    unnamed x13, local copies, waits for them, and re-layouts  2.64 us
    ppermute x1, starting transfers between devices, on_device(): back2 = lax.ppermute(crossed, AXIS, swap)  2.62 us
    ppermute x1, starting transfers between devices, on_device(): partner = lax.ppermute(own, AXIS, swap)  2.58 us
  transfers between devices with their start and end apart: 15, of which 3 were waited for; matrix products, arithmetic and copies ran while one was open for 1% of the time, Pallas kernels for 0%

profile of v1, /device:TPU:221, one launch (start us, length us, event | category | flops | bytes accessed | tf_op | source)
XLA Modules:
  0.0 85.7 jit_solution(18369405996686620651)
XLA Ops:
  0.6 1.0 %constant_dynamic-update-slice_fusion.1 = f32[512,256]{1,0:T(8,128)S(1)} fusion(f32[256,256]{1,0:T(8,128)} %param.2), kind=kLoop, calls=%fused_computation.6 | loop fusion | bytes 524288
  1.7 0.0 copy-done.5
  1.7 2.6 %collective-permute-start = (f32[512,256]{1,0:T(8,128)S(1)}, f32[512,256]{1,0:T(8,128)S(1)}, u32[]{:S(2)}, u32[]{:S(2)}) collective-permute-start(f32[512,256]{1,0:T(8,128)S(1)} %constant_dynamic-update-slice_fusion.own_ref), channel_id=1, source_target_pairs={{0,1},{1,0},{2,3},{3,2},{4,5},{5,4},{6,7},{7,6},{8,9},{9,8},{10,11... | collective-permute-start | bytes 1572872 | tf_op jit(solution)/shard_map/ppermute | solution.py:153
  4.3 1.5 %collective-permute-done.partner_ref = f32[512,256]{1,0:T(8,128)S(1)} collective-permute-done((f32[512,256]{1,0:T(8,128)S(1)}, f32[512,256]{1,0:T(8,128)S(1)}, u32[]{:S(2)}, u32[]{:S(2)}) %collective-permute-start) | collective-permute-done | bytes 524320 | tf_op jit(solution)/shard_map/ppermute | solution.py:153
  5.8 0.8 copy-done.2
  6.6 1.9 %shard_map.41 = f32[256,256]{1,0:T(8,128)} custom-call(s32[1]{0:T(128)} %bitcast.me_ref, f32[512,256]{1,0:T(8,128)} %copy-done, f32[512,256]{1,0:T(8,128)} %copy-done.2), custom_call_target="tpu_custom_call" | custom-call | tf_op jit(solution)/shard_map/pallas_call | solution.py:158
  8.5 0.8 collective-permute-start.3
  9.3 0.7 collective-permute-start.2
  10.0 0.7 collective-permute-start.1
  10.7 0.0 collective-permute-done.3
  10.7 0.0 collective-permute-done.1
  10.7 1.0 %add_add_fusion.3 = f32[256,256]{1,0:T(8,128)S(1)} fusion(f32[256,256]{1,0:T(8,128)S(1)} %collective-permute-done.3, f32[256,256]{1,0:T(8,128)S(1)} %collective-permute-done.2, f32[256,256]{1,0:T(8,128)} %shard_map.41, f32[256,256]{1,0:T(8,128)S(1)} %collective-permute-done.1), kind=kLoop, calls=%fused_computation.3 | loop fusion | flops 196608 | bytes 1310720 | tf_op jit(solution)/shard_map/add | solution.py:173
  11.8 0.7 collective-permute-start.6
  12.4 0.7 collective-permute-start.5
  13.1 0.7 collective-permute-start.4
  13.8 4.7 %collective-permute-start.10 = (f32[512,256]{1,0:T(8,128)S(1)}, f32[512,256]{1,0:T(8,128)S(1)}, u32[]{:S(2)}, u32[]{:S(2)}) collective-permute-start(f32[512,256]{1,0:T(8,128)S(1)} %copy-done.1), channel_id=1, source_target_pairs={{0,3},{1,2},{2,5},{3,4},{4,7},{5,6},{6,9},{7,8},{8,11},{9,10},{10,... | collective-permute-start | bytes 1572872 | tf_op jit(solution)/shard_map/ppermute | solution.py:156
  18.5 0.1 add_add_fusion.2
  18.6 0.7 collective-permute-start.9
  19.3 0.7 collective-permute-start.8
  20.0 0.7 collective-permute-start.7
  20.7 0.1 add_add_fusion.1
  20.8 9.1 %collective-permute-done.10 = f32[512,256]{1,0:T(8,128)S(1)} collective-permute-done((f32[512,256]{1,0:T(8,128)S(1)}, f32[512,256]{1,0:T(8,128)S(1)}, u32[]{:S(2)}, u32[]{:S(2)}) %collective-permute-start.10) | collective-permute-done | bytes 524320 | tf_op jit(solution)/shard_map/ppermute | solution.py:156
  29.9 0.7 collective-permute-start.13
  30.6 0.7 collective-permute-start.12
  31.3 1.3 %collective-permute-start.11 = (f32[256,256]{1,0:T(8,128)S(1)}, f32[256,256]{1,0:T(8,128)S(1)}, u32[]{:S(2)}, u32[]{:S(2)}) collective-permute-start(f32[256,256]{1,0:T(8,128)S(1)} %add_add_fusion.1), channel_id=1, source_target_pairs={{0,18},{256,274},{384,402},{128,146},{64,82},{320,338},{448,466},{... | collective-permute-start | bytes 786440 | tf_op jit(solution)/shard_map/ppermute | solution.py:171
  32.6 2.6 %collective-permute-start.14 = (f32[512,256]{1,0:T(8,128)S(1)}, f32[512,256]{1,0:T(8,128)S(1)}, u32[]{:S(2)}, u32[]{:S(2)}) collective-permute-start(f32[512,256]{1,0:T(8,128)S(1)} %collective-permute-done.10), channel_id=1, source_target_pairs={{0,1},{1,0},{2,3},{3,2},{4,5},{5,4},{6,7},{7,6},{8,9},{9,8},{10,11... | collective-permute-start | bytes 1572872 | tf_op jit(solution)/shard_map/ppermute | solution.py:170
  35.2 0.9 %broadcast_select_fusion.back1_ref = f32[512,256]{1,0:T(8,128)} fusion(f32[512,256]{1,0:T(8,128)S(1)} %copy-done.3, f32[512,256]{1,0:T(8,128)S(1)} %collective-permute-done.10, pred[]{:T(512)S(6)} %eq.5), kind=kLoop, calls=%fused_computation.4 | loop fusion | flops 131072 | bytes 1572865 | tf_op jit(solution)/shard_map/jit(_where)/select_n | solution.py:174
  36.1 40.0 %collective-permute-done.11 = f32[256,256]{1,0:T(8,128)S(1)} collective-permute-done((f32[256,256]{1,0:T(8,128)S(1)}, f32[256,256]{1,0:T(8,128)S(1)}, u32[]{:S(2)}, u32[]{:S(2)}) %collective-permute-start.11) | collective-permute-done | bytes 262176 | tf_op jit(solution)/shard_map/ppermute | solution.py:171
  76.1 0.1 add_add_fusion
  76.2 2.3 %all-gather = f32[512,256]{1,0:T(8,128)} all-gather(f32[256,256]{1,0:T(8,128)S(1)} %add_add_fusion), channel_id=2, replica_groups={{0,1},{2,3},{4,5},{6,7},{8,9},{10,11},{12,13},{14,15},{16,17},{18,19},{..., dimensions={0}, use_global_device_ids=true | all-gather | bytes 786432 | tf_op jit(solution)/shard_map/all_gather | solution.py:176
  78.5 0.8 copy-done.4
  79.3 6.4 %shard_map.42 = (f32[256,256]{1,0:T(8,128)}, f32[256,256]{1,0:T(8,128)}) custom-call(f32[2,256,256]{2,1,0:T(8,128)} %bitcast.2, f32[512,256]{1,0:T(8,128)} %copy-done.4, f32[512,256]{1,0:T(8,128)} %broadcast_select_fusion.back1_ref, f32[512,256]{1,0:T(8,128)} %copy-done), custom_call_target="tpu_custom_call" | custom-call | tf_op jit(solution)/shard_map/pallas_call | solution.py:177
  (20 shorter events, 0.1 us)
Async XLA Ops:
  0.6 1.0 %copy-start.5 = (f32[256,256]{1,0:T(8,128)S(1)}, f32[256,256]{1,0:T(8,128)}, u32[]{:S(2)}) copy-start(f32[256,256]{1,0:T(8,128)} %param.3) | copy-start | bytes 786436
  1.7 4.1 %copy-start = (f32[512,256]{1,0:T(8,128)}, f32[512,256]{1,0:T(8,128)S(1)}, u32[]{:S(2)}) copy-start(f32[512,256]{1,0:T(8,128)S(1)} %constant_dynamic-update-slice_fusion.own_ref) | copy-start | bytes 1572868
  1.7 4.1 %collective-permute-start = (f32[512,256]{1,0:T(8,128)S(1)}, f32[512,256]{1,0:T(8,128)S(1)}, u32[]{:S(2)}, u32[]{:S(2)}) collective-permute-start(f32[512,256]{1,0:T(8,128)S(1)} %constant_dynamic-update-slice_fusion.own_ref), channel_id=1, source_target_pairs={{0,1},{1,0},{2,3},{3,2},{4,5},{5,4},{6,7},{7,6},{8,9},{9,8},{10,11... | collective-permute-start | bytes 1572872 | tf_op jit(solution)/shard_map/ppermute | solution.py:153
  5.8 0.8 copy-start.2
  8.5 5.3 %copy-start.1 = (f32[512,256]{1,0:T(8,128)S(1)}, f32[512,256]{1,0:T(8,128)}, u32[]{:S(2)}) copy-start(f32[512,256]{1,0:T(8,128)} %copy-done) | copy-start | bytes 1572868
  8.5 2.2 %collective-permute-start.3 = (f32[256,256]{1,0:T(8,128)}, f32[256,256]{1,0:T(8,128)S(1)}, u32[]{:S(2)}, u32[]{:S(2)}) collective-permute-start(f32[256,256]{1,0:T(8,128)} %shard_map.41), channel_id=1, source_target_pairs={{0,128},{1,33}} | collective-permute-start | bytes 786440 | tf_op jit(solution)/shard_map/ppermute | solution.py:171
  9.3 1.4 %collective-permute-start.2 = (f32[256,256]{1,0:T(8,128)}, f32[256,256]{1,0:T(8,128)S(1)}, u32[]{:S(2)}, u32[]{:S(2)}) collective-permute-start(f32[256,256]{1,0:T(8,128)} %shard_map.41), channel_id=1, source_target_pairs={{0,384},{1,97}} | collective-permute-start | bytes 786440 | tf_op jit(solution)/shard_map/ppermute | solution.py:171
  10.0 0.7 collective-permute-start.1
  11.8 6.8 %collective-permute-start.6 = (f32[256,256]{1,0:T(8,128)S(1)}, f32[256,256]{1,0:T(8,128)S(1)}, u32[]{:S(2)}, u32[]{:S(2)}) collective-permute-start(f32[256,256]{1,0:T(8,128)S(1)} %add_add_fusion.3), channel_id=1, source_target_pairs={{0,32},{256,288},{384,416},{128,160},{1,5},{65,69},{97,101},{33,37}} | collective-permute-start | bytes 786440 | tf_op jit(solution)/shard_map/ppermute | solution.py:171
  12.4 6.1 %collective-permute-start.5 = (f32[256,256]{1,0:T(8,128)S(1)}, f32[256,256]{1,0:T(8,128)S(1)}, u32[]{:S(2)}, u32[]{:S(2)}) collective-permute-start(f32[256,256]{1,0:T(8,128)S(1)} %add_add_fusion.3), channel_id=1, source_target_pairs={{0,96},{256,352},{384,480},{128,224},{1,13},{65,77},{97,109},{33,45}} | collective-permute-start | bytes 786440 | tf_op jit(solution)/shard_map/ppermute | solution.py:171
  13.1 5.4 %collective-permute-start.4 = (f32[256,256]{1,0:T(8,128)S(1)}, f32[256,256]{1,0:T(8,128)S(1)}, u32[]{:S(2)}, u32[]{:S(2)}) collective-permute-start(f32[256,256]{1,0:T(8,128)S(1)} %add_add_fusion.3), channel_id=1, source_target_pairs={{0,64},{256,320},{384,448},{128,192},{1,9},{65,73},{97,105},{33,41}} | collective-permute-start | bytes 786440 | tf_op jit(solution)/shard_map/ppermute | solution.py:171
  13.8 16.1 %collective-permute-start.10 = (f32[512,256]{1,0:T(8,128)S(1)}, f32[512,256]{1,0:T(8,128)S(1)}, u32[]{:S(2)}, u32[]{:S(2)}) collective-permute-start(f32[512,256]{1,0:T(8,128)S(1)} %copy-done.1), channel_id=1, source_target_pairs={{0,3},{1,2},{2,5},{3,4},{4,7},{5,6},{6,9},{7,8},{8,11},{9,10},{10,... | collective-permute-start | bytes 1572872 | tf_op jit(solution)/shard_map/ppermute | solution.py:156
  18.6 2.1 %collective-permute-start.9 = (f32[256,256]{1,0:T(8,128)S(1)}, f32[256,256]{1,0:T(8,128)S(1)}, u32[]{:S(2)}, u32[]{:S(2)}) collective-permute-start(f32[256,256]{1,0:T(8,128)S(1)} %add_add_fusion.2), channel_id=1, source_target_pairs={{0,4},{256,260},{384,388},{128,132},{64,68},{320,324},{448,452},{1... | collective-permute-start | bytes 786440 | tf_op jit(solution)/shard_map/ppermute | solution.py:171
  19.3 1.4 %collective-permute-start.8 = (f32[256,256]{1,0:T(8,128)S(1)}, f32[256,256]{1,0:T(8,128)S(1)}, u32[]{:S(2)}, u32[]{:S(2)}) collective-permute-start(f32[256,256]{1,0:T(8,128)S(1)} %add_add_fusion.2), channel_id=1, source_target_pairs={{0,12},{256,268},{384,396},{128,140},{64,76},{320,332},{448,460},{... | collective-permute-start | bytes 786440 | tf_op jit(solution)/shard_map/ppermute | solution.py:171
  20.0 0.7 collective-permute-start.7
  20.7 14.5 %copy-start.3 = (f32[512,256]{1,0:T(8,128)S(1)}, f32[512,256]{1,0:T(8,128)}, u32[]{:S(2)}) copy-start(f32[512,256]{1,0:T(8,128)} %copy-done.2) | copy-start | bytes 1572868
  29.9 6.2 %collective-permute-start.13 = (f32[256,256]{1,0:T(8,128)S(1)}, f32[256,256]{1,0:T(8,128)S(1)}, u32[]{:S(2)}, u32[]{:S(2)}) collective-permute-start(f32[256,256]{1,0:T(8,128)S(1)} %add_add_fusion.1), channel_id=1, source_target_pairs={{0,2},{256,258},{384,386},{128,130},{64,66},{320,322},{448,450},{1... | collective-permute-start | bytes 786440 | tf_op jit(solution)/shard_map/ppermute | solution.py:171
  30.6 5.5 %collective-permute-start.12 = (f32[256,256]{1,0:T(8,128)S(1)}, f32[256,256]{1,0:T(8,128)S(1)}, u32[]{:S(2)}, u32[]{:S(2)}) collective-permute-start(f32[256,256]{1,0:T(8,128)S(1)} %add_add_fusion.1), channel_id=1, source_target_pairs={{0,16},{256,272},{384,400},{128,144},{64,80},{320,336},{448,464},{... | collective-permute-start | bytes 786440 | tf_op jit(solution)/shard_map/ppermute | solution.py:171
  31.3 44.8 %collective-permute-start.11 = (f32[256,256]{1,0:T(8,128)S(1)}, f32[256,256]{1,0:T(8,128)S(1)}, u32[]{:S(2)}, u32[]{:S(2)}) collective-permute-start(f32[256,256]{1,0:T(8,128)S(1)} %add_add_fusion.1), channel_id=1, source_target_pairs={{0,18},{256,274},{384,402},{128,146},{64,82},{320,338},{448,466},{... | collective-permute-start | bytes 786440 | tf_op jit(solution)/shard_map/ppermute | solution.py:171
  32.6 45.9 %collective-permute-start.14 = (f32[512,256]{1,0:T(8,128)S(1)}, f32[512,256]{1,0:T(8,128)S(1)}, u32[]{:S(2)}, u32[]{:S(2)}) collective-permute-start(f32[512,256]{1,0:T(8,128)S(1)} %collective-permute-done.10), channel_id=1, source_target_pairs={{0,1},{1,0},{2,3},{3,2},{4,5},{5,4},{6,7},{7,6},{8,9},{9,8},{10,11... | collective-permute-start | bytes 1572872 | tf_op jit(solution)/shard_map/ppermute | solution.py:170
  78.5 0.8 copy-start.4

commit v2 on v1

--- a/solution.py
+++ b/solution.py
@@ -5,6 +5,7 @@
 from jax.experimental.pallas import tpu as pltpu
 from jax.sharding import PartitionSpec as P
 
+
 B = 256
 AXIS = "blk"
 
@@ -17,16 +18,16 @@
 
 TREE = (
     (
+        ((0, -2, 0), (0, -4, 0), (0, 2, 0)),
         ((2, 0, 0), (-1, 0, 0), (1, 0, 0)),
-        ((0, 4, 0), (0, -2, 0), (0, 2, 0)),
         ((0, 0, 4), (0, 0, -2), (0, 0, 2)),
-        ((0, 1, 1), (0, 1, 0), (0, 0, 1)),
+        ((0, 1, -1), (0, 1, 0), (0, 0, -1)),
     ),
     (
+        ((2, 0, 0), (-1, 0, 0), (1, 0, 0)),
+        ((0, 0, -4), (0, 0, -2), (0, 0, 2)),
         ((0, 4, 0), (0, -2, 0), (0, 2, 0)),
-        ((0, 0, 4), (0, 0, -2), (0, 0, 2)),
-        ((2, 0, 0), (-1, 0, 0), (1, 0, 0)),
-        ((0, -1, -1), (0, -1, 0), (0, 0, -1)),
+        ((0, -1, 1), (0, -1, 0), (0, 0, 1)),
     ),
 )
 
@@ -100,26 +101,37 @@
     return halves(top), halves(bottom)
 
 
-def factor_kernel(me_ref, own_ref, partner_ref, out_ref):
+def stack_kernel(p_ref, n_ref, out_ref, sems):
+    copies = [
+        pltpu.make_async_copy(p_ref, out_ref.at[:B, :], sems.at[0]),
+        pltpu.make_async_copy(n_ref, out_ref.at[B:, :], sems.at[1]),
+    ]
+    for copy in copies:
+        copy.start()
+    for copy in copies:
+        copy.wait()
+
+
+def factor_kernel(me_ref, own_ref, next_ref, k0_ref, k1_ref):
     me = me_ref[0]
 
-    @pl.when(me >= 2)
+    @pl.when(me != 0)
     def _():
-        out_ref[...] = jnp.zeros_like(out_ref)
-
-    @pl.when(me < 2)
+        k0_ref[...] = jnp.zeros_like(k0_ref)
+        k1_ref[...] = jnp.zeros_like(k1_ref)
+
+    @pl.when(me == 0)
     def _():
         identity = eye()
-        mine, other = own_ref[...], partner_ref[...]
-        first, second = jnp.where(me == 0, mine, other), jnp.where(me == 0, other, mine)
-        p0, n0, p1, n1 = first[:B, :], first[B:, :], second[:B, :], second[B:, :]
+        p0, n0 = own_ref[:B, :], own_ref[B:, :]
+        p1, n1 = next_ref[:B, :], next_ref[B:, :]
         k0 = coupling_of(p0, n0, identity)
+        k0_ref[...] = k0
         k, kt = halves(k0), halves(k0.T)
         top, bottom = roots_of(k, kt, identity)
         lead_p = dot(top, halves(p0 - dot(kt, halves(n0))))
         lead_n = dot(bottom, halves(n1 - dot(k, halves(p1))))
-        k1 = coupling_of(lead_p, lead_n, identity)
-        out_ref[...] = jnp.where(me == 0, k0, k1)
+        k1_ref[...] = coupling_of(lead_p, lead_n, identity)
 
 
 def apply_kernel(k_ref, back2_ref, back1_ref, own_ref, p_ref, n_ref):
@@ -141,37 +153,45 @@
 
 VMEM = pl.BlockSpec(memory_space=pltpu.VMEM)
 SMEM = pl.BlockSpec(memory_space=pltpu.SMEM)
-
-
-def on_device(positive_row, negative_row):
+ANY = pl.BlockSpec(memory_space=pl.ANY)
+
+
+def resident(*arrays):
+    return [pltpu.with_memory_space_constraint(a, pltpu.VMEM) for a in arrays]
+
+
+def send(array, pairs):
+    return lax.ppermute(array, AXIS, pairs)
+
+
+def steps(positive_row, negative_row):
     me = lax.axis_index(AXIS)
     devices = lax.axis_size(AXIS)
     cores = [[i, i + 1] for i in range(0, devices, 2)]
-    own = jnp.concatenate([positive_row, negative_row], axis=0)
-    odd = me % 2 == 1
-    swap = [(i, i ^ 1) for i in range(devices)]
-    partner = lax.ppermute(own, AXIS, swap)
-
-    route = [(i, i + (1 if i % 2 else 3)) for i in range(devices)]
-    crossed = lax.ppermute(own, AXIS, [(i, j) for i, j in route if j < devices])
-
-    factor = pl.pallas_call(
+    onward = [(i, i + 1) for i in range(devices - 1)]
+    own = pl.pallas_call(
+        stack_kernel,
+        out_shape=pltpu.VMEM((2 * B, B), jnp.float32),
+        in_specs=[ANY] * 2,
+        out_specs=VMEM,
+        scratch_shapes=[pltpu.SemaphoreType.DMA((2,))],
+    )(positive_row, negative_row)
+    second = send(own, [(1, 0)])
+    k0, k1 = pl.pallas_call(
         factor_kernel,
-        out_shape=jax.ShapeDtypeStruct((B, B), jnp.float32),
+        out_shape=[pltpu.VMEM((B, B), jnp.float32)] * 2,
         in_specs=[SMEM, VMEM, VMEM],
-        out_specs=VMEM,
-    )(jnp.reshape(me, (1,)).astype(jnp.int32), own, partner)
-
-    held = factor
+        out_specs=[VMEM] * 2,
+    )(jnp.reshape(me, (1,)).astype(jnp.int32), *resident(own, second))
+
+    held = k0 + send(k1, [(0, 1)])
     rounds = tree_rounds()
-    for number, permutes in enumerate(rounds):
-        if number == len(rounds) - 1:
-            held, crossed = lax.optimization_barrier((held, crossed))
-            back2 = lax.ppermute(crossed, AXIS, swap)
-        arrived = [lax.ppermute(held, AXIS, pairs) for pairs in permutes]
+    back1 = send(own, onward)
+    back2 = send(back1, onward)
+    for permutes in rounds:
+        arrived = [send(held, pairs) for pairs in permutes]
         for block in arrived:
             held = held + block
-    back1 = jnp.where(odd, partner, crossed)
 
     both = lax.all_gather(held, AXIS, axis=0, axis_index_groups=cores)
     return pl.pallas_call(
@@ -179,11 +199,11 @@
         out_shape=[jax.ShapeDtypeStruct((B, B), jnp.float32)] * 2,
         in_specs=[VMEM] * 4,
         out_specs=[VMEM] * 2,
-    )(both, back2, back1, own)
+    )(*resident(both, back2, back1, own))
 
 
 def solution(mesh):
     spec = P(None, AXIS)
     return jax.shard_map(
-        on_device, mesh=mesh, in_specs=(spec, spec), out_specs=(spec, spec), check_vma=False
+        steps, mesh=mesh, in_specs=(spec, spec), out_specs=(spec, spec), check_vma=False
     )

time: 86.2 us -> 82.9 us (0.962)
  the two profiles are of different devices: /device:TPU:221 before, /device:TPU:2 now
where the time goes in v2:
time: 82.9 us; the launch traced here: 82.5 us
  waiting for transfers between devices  55.4 us (67%)
  starting transfers between devices  17.7 us (21%)
  Pallas kernels  6.01 us (7%)
  blocking collectives  2.18 us (3%)
  between operations  0.87 us (1%)
    ppermute x16, waiting for transfers between devices, send(): return lax.ppermute(array, AXIS, pairs)  55.4 us
    ppermute x16, starting transfers between devices, send(): return lax.ppermute(array, AXIS, pairs)  17.7 us
    pallas_call x1, Pallas kernels, steps(): pl.pallas_call(apply_kernel, out_shape=[jax.ShapeDtypeStruct((B, B), jnp....  4.92 us
    all_gather x1, blocking collectives, steps(): both = lax.all_gather(held, AXIS, axis=0, axis_index_groups=cores)  2.18 us
  transfers between devices with their start and end apart: 16, of which 6 were waited for; matrix products, arithmetic and copies ran while one was open for 0% of the time, Pallas kernels for 0%

profile of v2, /device:TPU:2, one launch (start us, length us, event | category | flops | bytes accessed | tf_op | source)
XLA Modules:
  0.0 82.5 jit_solution(9915446421711624477)
XLA Ops:
  0.6 1.0 %shard_map.41.own_ref = f32[512,256]{1,0:T(8,128)S(1)} custom-call(f32[256,256]{1,0:T(8,128)} %p_ref.1, f32[256,256]{1,0:T(8,128)} %n_ref.1), custom_call_target="tpu_custom_call" | custom-call | tf_op jit(solution)/shard_map/pallas_call | solution.py:172
  1.7 0.7 collective-permute-start
  2.4 0.0 collective-permute-done.next_ref
  2.5 0.7 collective-permute-start.1
  3.1 0.0 collective-permute-done.1
  3.2 0.7 collective-permute-start.2
  3.9 0.7 collective-permute-start.3
  4.6 0.7 collective-permute-start.4
  5.3 0.0 collective-permute-done.3
  5.3 0.1 add_add_fusion.3
  5.4 0.7 collective-permute-start.5
  6.0 0.7 collective-permute-start.6
  6.7 1.3 %collective-permute-start.7 = (f32[256,256]{1,0:T(8,128)S(1)}, f32[256,256]{1,0:T(8,128)S(1)}, u32[]{:S(2)}, u32[]{:S(2)}) collective-permute-start(f32[256,256]{1,0:T(8,128)S(1)} %add_add_fusion.3), channel_id=1, source_target_pairs={{0,128},{96,224},{64,192},{32,160},{1,5},{257,261},{385,389},{129,... | collective-permute-start | bytes 786440 | tf_op jit(solution)/shard_map/ppermute | solution.py:164
  8.0 36.0 %collective-permute-done.7 = f32[256,256]{1,0:T(8,128)S(1)} collective-permute-done((f32[256,256]{1,0:T(8,128)S(1)}, f32[256,256]{1,0:T(8,128)S(1)}, u32[]{:S(2)}, u32[]{:S(2)}) %collective-permute-start.7) | collective-permute-done | bytes 262176 | tf_op jit(solution)/shard_map/ppermute | solution.py:164
  44.1 0.1 add_add_fusion.2
  44.2 1.3 %collective-permute-start.10 = (f32[256,256]{1,0:T(8,128)S(1)}, f32[256,256]{1,0:T(8,128)S(1)}, u32[]{:S(2)}, u32[]{:S(2)}) collective-permute-start(f32[256,256]{1,0:T(8,128)S(1)} %add_add_fusion.2), channel_id=1, source_target_pairs={{0,4},{96,100},{64,68},{32,36},{256,260},{352,356},{320,324},{288,... | collective-permute-start | bytes 786440 | tf_op jit(solution)/shard_map/ppermute | solution.py:164
  45.5 1.3 %collective-permute-start.8 = (f32[256,256]{1,0:T(8,128)S(1)}, f32[256,256]{1,0:T(8,128)S(1)}, u32[]{:S(2)}, u32[]{:S(2)}) collective-permute-start(f32[256,256]{1,0:T(8,128)S(1)} %add_add_fusion.2), channel_id=1, source_target_pairs={{0,8},{96,104},{64,72},{32,40},{256,264},{352,360},{320,328},{288,... | collective-permute-start | bytes 786440 | tf_op jit(solution)/shard_map/ppermute | solution.py:164
  46.8 1.3 %collective-permute-start.9 = (f32[256,256]{1,0:T(8,128)S(1)}, f32[256,256]{1,0:T(8,128)S(1)}, u32[]{:S(2)}, u32[]{:S(2)}) collective-permute-start(f32[256,256]{1,0:T(8,128)S(1)} %add_add_fusion.2), channel_id=1, source_target_pairs={{0,12},{96,108},{64,76},{32,44},{256,268},{352,364},{320,332},{288... | collective-permute-start | bytes 786440 | tf_op jit(solution)/shard_map/ppermute | solution.py:164
  48.1 1.9 %collective-permute-start.14 = (f32[512,256]{1,0:T(8,128)S(1)}, f32[512,256]{1,0:T(8,128)S(1)}, u32[]{:S(2)}, u32[]{:S(2)}) collective-permute-start(f32[512,256]{1,0:T(8,128)S(1)} %shard_map.41.own_ref), channel_id=1, source_target_pairs={{0,1},{1,2},{2,3},{3,4},{4,5},{5,6},{6,7},{7,8},{8,9},{9,10},{10,1... | collective-permute-start | bytes 1572872 | tf_op jit(solution)/shard_map/ppermute | solution.py:164
  50.0 2.1 %collective-permute-done.10 = f32[256,256]{1,0:T(8,128)S(1)} collective-permute-done((f32[256,256]{1,0:T(8,128)S(1)}, f32[256,256]{1,0:T(8,128)S(1)}, u32[]{:S(2)}, u32[]{:S(2)}) %collective-permute-start.10) | collective-permute-done | bytes 262176 | tf_op jit(solution)/shard_map/ppermute | solution.py:164
  52.1 5.6 %collective-permute-done.8 = f32[256,256]{1,0:T(8,128)S(1)} collective-permute-done((f32[256,256]{1,0:T(8,128)S(1)}, f32[256,256]{1,0:T(8,128)S(1)}, u32[]{:S(2)}, u32[]{:S(2)}) %collective-permute-start.8) | collective-permute-done | bytes 262176 | tf_op jit(solution)/shard_map/ppermute | solution.py:164
  57.8 0.1 add_add_fusion.1
  57.8 1.3 %collective-permute-start.11 = (f32[256,256]{1,0:T(8,128)S(1)}, f32[256,256]{1,0:T(8,128)S(1)}, u32[]{:S(2)}, u32[]{:S(2)}) collective-permute-start(f32[256,256]{1,0:T(8,128)S(1)} %add_add_fusion.1), channel_id=1, source_target_pairs={{0,30},{96,126},{64,94},{32,62},{256,286},{352,382},{320,350},{288... | collective-permute-start | bytes 786440 | tf_op jit(solution)/shard_map/ppermute | solution.py:164
  59.2 1.3 %collective-permute-start.12 = (f32[256,256]{1,0:T(8,128)S(1)}, f32[256,256]{1,0:T(8,128)S(1)}, u32[]{:S(2)}, u32[]{:S(2)}) collective-permute-start(f32[256,256]{1,0:T(8,128)S(1)} %add_add_fusion.1), channel_id=1, source_target_pairs={{0,16},{96,112},{64,80},{32,48},{256,272},{352,368},{320,336},{288... | collective-permute-start | bytes 786440 | tf_op jit(solution)/shard_map/ppermute | solution.py:164
  60.5 1.3 %collective-permute-start.13 = (f32[256,256]{1,0:T(8,128)S(1)}, f32[256,256]{1,0:T(8,128)S(1)}, u32[]{:S(2)}, u32[]{:S(2)}) collective-permute-start(f32[256,256]{1,0:T(8,128)S(1)} %add_add_fusion.1), channel_id=1, source_target_pairs={{0,14},{96,110},{64,78},{32,46},{256,270},{352,366},{320,334},{288... | collective-permute-start | bytes 786440 | tf_op jit(solution)/shard_map/ppermute | solution.py:164
  61.8 1.0 %collective-permute-done.14.back1_ref = f32[512,256]{1,0:T(8,128)S(1)} collective-permute-done((f32[512,256]{1,0:T(8,128)S(1)}, f32[512,256]{1,0:T(8,128)S(1)}, u32[]{:S(2)}, u32[]{:S(2)}) %collective-permute-start.14) | collective-permute-done | bytes 524320 | tf_op jit(solution)/shard_map/ppermute | solution.py:164
  62.8 1.9 %collective-permute-start.15 = (f32[512,256]{1,0:T(8,128)S(1)}, f32[512,256]{1,0:T(8,128)S(1)}, u32[]{:S(2)}, u32[]{:S(2)}) collective-permute-start(f32[512,256]{1,0:T(8,128)S(1)} %collective-permute-done.14.back1_ref), channel_id=1, source_target_pairs={{0,1},{1,2},{2,3},{3,4},{4,5},{5,6},{6,7},{7,8},{8,9},{9,10},{10,1... | collective-permute-start | bytes 1572872 | tf_op jit(solution)/shard_map/ppermute | solution.py:164
  64.8 1.1 %collective-permute-done.13 = f32[256,256]{1,0:T(8,128)S(1)} collective-permute-done((f32[256,256]{1,0:T(8,128)S(1)}, f32[256,256]{1,0:T(8,128)S(1)}, u32[]{:S(2)}, u32[]{:S(2)}) %collective-permute-start.13) | collective-permute-done | bytes 262176 | tf_op jit(solution)/shard_map/ppermute | solution.py:164
  65.8 0.1 add_add_fusion
  65.9 2.2 %all-gather = f32[512,256]{1,0:T(8,128)S(1)} all-gather(f32[256,256]{1,0:T(8,128)S(1)} %add_add_fusion), channel_id=2, replica_groups={{0,1},{2,3},{4,5},{6,7},{8,9},{10,11},{12,13},{14,15},{16,17},{18,19},{..., dimensions={0}, use_global_device_ids=true | all-gather | bytes 786432 | tf_op jit(solution)/shard_map/all_gather | solution.py:196
  68.1 9.5 %collective-permute-done.15.back2_ref = f32[512,256]{1,0:T(8,128)S(1)} collective-permute-done((f32[512,256]{1,0:T(8,128)S(1)}, f32[512,256]{1,0:T(8,128)S(1)}, u32[]{:S(2)}, u32[]{:S(2)}) %collective-permute-start.15) | collective-permute-done | bytes 524320 | tf_op jit(solution)/shard_map/ppermute | solution.py:164
  77.5 4.9 %shard_map.43 = (f32[256,256]{1,0:T(8,128)}, f32[256,256]{1,0:T(8,128)}) custom-call(f32[2,256,256]{2,1,0:T(8,128)S(1)} %bitcast.2, f32[512,256]{1,0:T(8,128)S(1)} %collective-permute-done.15.back2_ref, f32[512,256]{1,0:T(8,128)S(1)} %collective-permute-done.14.back1_ref, f32[512,256]{1,0:T(8,128)S(1)} %shard_map.41.own_ref), custom_call_target="tpu_custom_call" | custom-call | tf_op jit(solution)/shard_map/pallas_call | solution.py:197
  (9 shorter events, 0.1 us)
Async XLA Ops:
  1.7 0.7 collective-permute-start
  2.5 0.7 collective-permute-start.1
  3.2 2.1 %collective-permute-start.2 = (f32[256,256]{1,0:T(8,128)S(1)}, f32[256,256]{1,0:T(8,128)S(1)}, u32[]{:S(2)}, u32[]{:S(2)}) collective-permute-start(f32[256,256]{1,0:T(8,128)S(1)} %add.39), channel_id=1, source_target_pairs={{0,96},{1,257}} | collective-permute-start | bytes 786440 | tf_op jit(solution)/shard_map/ppermute | solution.py:164
  3.9 1.4 %collective-permute-start.3 = (f32[256,256]{1,0:T(8,128)S(1)}, f32[256,256]{1,0:T(8,128)S(1)}, u32[]{:S(2)}, u32[]{:S(2)}) collective-permute-start(f32[256,256]{1,0:T(8,128)S(1)} %add.39), channel_id=1, source_target_pairs={{0,64},{1,385}} | collective-permute-start | bytes 786440 | tf_op jit(solution)/shard_map/ppermute | solution.py:164
  4.6 0.7 collective-permute-start.4
  5.4 2.7 %collective-permute-start.5 = (f32[256,256]{1,0:T(8,128)S(1)}, f32[256,256]{1,0:T(8,128)S(1)}, u32[]{:S(2)}, u32[]{:S(2)}) collective-permute-start(f32[256,256]{1,0:T(8,128)S(1)} %add_add_fusion.3), channel_id=1, source_target_pairs={{0,256},{96,352},{64,320},{32,288},{1,9},{257,265},{385,393},{129,... | collective-permute-start | bytes 786440 | tf_op jit(solution)/shard_map/ppermute | solution.py:164
  6.0 2.0 %collective-permute-start.6 = (f32[256,256]{1,0:T(8,128)S(1)}, f32[256,256]{1,0:T(8,128)S(1)}, u32[]{:S(2)}, u32[]{:S(2)}) collective-permute-start(f32[256,256]{1,0:T(8,128)S(1)} %add_add_fusion.3), channel_id=1, source_target_pairs={{0,384},{96,480},{64,448},{32,416},{1,13},{257,269},{385,397},{129... | collective-permute-start | bytes 786440 | tf_op jit(solution)/shard_map/ppermute | solution.py:164
  6.7 37.4 %collective-permute-start.7 = (f32[256,256]{1,0:T(8,128)S(1)}, f32[256,256]{1,0:T(8,128)S(1)}, u32[]{:S(2)}, u32[]{:S(2)}) collective-permute-start(f32[256,256]{1,0:T(8,128)S(1)} %add_add_fusion.3), channel_id=1, source_target_pairs={{0,128},{96,224},{64,192},{32,160},{1,5},{257,261},{385,389},{129,... | collective-permute-start | bytes 786440 | tf_op jit(solution)/shard_map/ppermute | solution.py:164
  44.2 8.0 %collective-permute-start.10 = (f32[256,256]{1,0:T(8,128)S(1)}, f32[256,256]{1,0:T(8,128)S(1)}, u32[]{:S(2)}, u32[]{:S(2)}) collective-permute-start(f32[256,256]{1,0:T(8,128)S(1)} %add_add_fusion.2), channel_id=1, source_target_pairs={{0,4},{96,100},{64,68},{32,36},{256,260},{352,356},{320,324},{288,... | collective-permute-start | bytes 786440 | tf_op jit(solution)/shard_map/ppermute | solution.py:164
  45.5 12.3 %collective-permute-start.8 = (f32[256,256]{1,0:T(8,128)S(1)}, f32[256,256]{1,0:T(8,128)S(1)}, u32[]{:S(2)}, u32[]{:S(2)}) collective-permute-start(f32[256,256]{1,0:T(8,128)S(1)} %add_add_fusion.2), channel_id=1, source_target_pairs={{0,8},{96,104},{64,72},{32,40},{256,264},{352,360},{320,328},{288,... | collective-permute-start | bytes 786440 | tf_op jit(solution)/shard_map/ppermute | solution.py:164
  46.8 11.0 %collective-permute-start.9 = (f32[256,256]{1,0:T(8,128)S(1)}, f32[256,256]{1,0:T(8,128)S(1)}, u32[]{:S(2)}, u32[]{:S(2)}) collective-permute-start(f32[256,256]{1,0:T(8,128)S(1)} %add_add_fusion.2), channel_id=1, source_target_pairs={{0,12},{96,108},{64,76},{32,44},{256,268},{352,364},{320,332},{288... | collective-permute-start | bytes 786440 | tf_op jit(solution)/shard_map/ppermute | solution.py:164
  48.1 14.7 %collective-permute-start.14 = (f32[512,256]{1,0:T(8,128)S(1)}, f32[512,256]{1,0:T(8,128)S(1)}, u32[]{:S(2)}, u32[]{:S(2)}) collective-permute-start(f32[512,256]{1,0:T(8,128)S(1)} %shard_map.41.own_ref), channel_id=1, source_target_pairs={{0,1},{1,2},{2,3},{3,4},{4,5},{5,6},{6,7},{7,8},{8,9},{9,10},{10,1... | collective-permute-start | bytes 1572872 | tf_op jit(solution)/shard_map/ppermute | solution.py:164
  57.8 6.9 %collective-permute-start.11 = (f32[256,256]{1,0:T(8,128)S(1)}, f32[256,256]{1,0:T(8,128)S(1)}, u32[]{:S(2)}, u32[]{:S(2)}) collective-permute-start(f32[256,256]{1,0:T(8,128)S(1)} %add_add_fusion.1), channel_id=1, source_target_pairs={{0,30},{96,126},{64,94},{32,62},{256,286},{352,382},{320,350},{288... | collective-permute-start | bytes 786440 | tf_op jit(solution)/shard_map/ppermute | solution.py:164
  59.2 5.6 %collective-permute-start.12 = (f32[256,256]{1,0:T(8,128)S(1)}, f32[256,256]{1,0:T(8,128)S(1)}, u32[]{:S(2)}, u32[]{:S(2)}) collective-permute-start(f32[256,256]{1,0:T(8,128)S(1)} %add_add_fusion.1), channel_id=1, source_target_pairs={{0,16},{96,112},{64,80},{32,48},{256,272},{352,368},{320,336},{288... | collective-permute-start | bytes 786440 | tf_op jit(solution)/shard_map/ppermute | solution.py:164
  60.5 5.4 %collective-permute-start.13 = (f32[256,256]{1,0:T(8,128)S(1)}, f32[256,256]{1,0:T(8,128)S(1)}, u32[]{:S(2)}, u32[]{:S(2)}) collective-permute-start(f32[256,256]{1,0:T(8,128)S(1)} %add_add_fusion.1), channel_id=1, source_target_pairs={{0,14},{96,110},{64,78},{32,46},{256,270},{352,366},{320,334},{288... | collective-permute-start | bytes 786440 | tf_op jit(solution)/shard_map/ppermute | solution.py:164
  62.8 14.7 %collective-permute-start.15 = (f32[512,256]{1,0:T(8,128)S(1)}, f32[512,256]{1,0:T(8,128)S(1)}, u32[]{:S(2)}, u32[]{:S(2)}) collective-permute-start(f32[512,256]{1,0:T(8,128)S(1)} %collective-permute-done.14.back1_ref), channel_id=1, source_target_pairs={{0,1},{1,2},{2,3},{3,4},{4,5},{5,6},{6,7},{7,8},{8,9},{9,10},{10,1... | collective-permute-start | bytes 1572872 | tf_op jit(solution)/shard_map/ppermute | solution.py:164

commit v3 on v2

--- a/solution.py
+++ b/solution.py
@@ -168,7 +168,7 @@
     me = lax.axis_index(AXIS)
     devices = lax.axis_size(AXIS)
     cores = [[i, i + 1] for i in range(0, devices, 2)]
-    onward = [(i, i + 1) for i in range(devices - 1)]
+    onward = [(i, i + 1) for i in range(1, devices - 1)]
     own = pl.pallas_call(
         stack_kernel,
         out_shape=pltpu.VMEM((2 * B, B), jnp.float32),
@@ -176,7 +176,8 @@
         out_specs=VMEM,
         scratch_shapes=[pltpu.SemaphoreType.DMA((2,))],
     )(positive_row, negative_row)
-    second = send(own, [(1, 0)])
+    second = send(own, [(0, 1), (1, 0)])
+    back1 = send(own, onward)
     k0, k1 = pl.pallas_call(
         factor_kernel,
         out_shape=[pltpu.VMEM((B, B), jnp.float32)] * 2,
@@ -185,9 +186,9 @@
     )(jnp.reshape(me, (1,)).astype(jnp.int32), *resident(own, second))
 
     held = k0 + send(k1, [(0, 1)])
+    back1 = jnp.where(me == 1, second, back1)
+    back2 = send(back1, onward)
     rounds = tree_rounds()
-    back1 = send(own, onward)
-    back2 = send(back1, onward)
     for permutes in rounds:
         arrived = [send(held, pairs) for pairs in permutes]
         for block in arrived:

time: 82.9 us -> 78.9 us (0.952)
  the two profiles are of different devices: /device:TPU:2 before, /device:TPU:4 now
where the time goes in v3:
time: 78.9 us; the launch traced here: 78.5 us
  starting transfers between devices  48.9 us (62%)
  waiting for transfers between devices  20.2 us (26%)
  Pallas kernels  6.01 us (8%)
  blocking collectives  2.18 us (3%)
  between operations  0.9 us (1%)
    ppermute x16, starting transfers between devices, send(): return lax.ppermute(array, AXIS, pairs)  48.9 us
    ppermute x16, waiting for transfers between devices, send(): return lax.ppermute(array, AXIS, pairs)  20.2 us
    pallas_call x1, Pallas kernels, steps(): pl.pallas_call(apply_kernel, out_shape=[jax.ShapeDtypeStruct((B, B), jnp....  4.92 us
    all_gather x1, blocking collectives, steps(): both = lax.all_gather(held, AXIS, axis=0, axis_index_groups=cores)  2.18 us
  transfers between devices with their start and end apart: 16, of which 5 were waited for; matrix products, arithmetic and copies ran while one was open for 0% of the time, Pallas kernels for 0%

profile of v3, /device:TPU:4, one launch (start us, length us, event | category | flops | bytes accessed | tf_op | source)
XLA Modules:
  0.0 78.5 jit_solution(6608836073931563722)
XLA Ops:
  0.6 1.0 %shard_map.41.own_ref = f32[512,256]{1,0:T(8,128)S(1)} custom-call(f32[256,256]{1,0:T(8,128)} %p_ref.1, f32[256,256]{1,0:T(8,128)} %n_ref.1), custom_call_target="tpu_custom_call" | custom-call | tf_op jit(solution)/shard_map/pallas_call | solution.py:172
  1.7 0.7 collective-permute-start
  2.4 0.0 collective-permute-done.next_ref
  2.5 0.7 collective-permute-start.1
  3.2 0.7 collective-permute-start.4
  3.9 0.7 collective-permute-start.3
  4.6 0.7 collective-permute-start.2
  5.3 0.0 collective-permute-done.3
  5.3 0.1 add_add_fusion.3
  5.4 0.7 collective-permute-start.7
  6.0 0.7 collective-permute-start.6
  6.7 1.3 %collective-permute-start.5 = (f32[256,256]{1,0:T(8,128)S(1)}, f32[256,256]{1,0:T(8,128)S(1)}, u32[]{:S(2)}, u32[]{:S(2)}) collective-permute-start(f32[256,256]{1,0:T(8,128)S(1)} %add_add_fusion.3), channel_id=1, source_target_pairs={{0,256},{96,352},{64,320},{32,288},{1,9},{257,265},{385,393},{129,... | collective-permute-start | bytes 786440 | tf_op jit(solution)/shard_map/ppermute | solution.py:164
  8.0 33.1 %collective-permute-start.14 = (f32[512,256]{1,0:T(8,128)S(1)}, f32[512,256]{1,0:T(8,128)S(1)}, u32[]{:S(2)}, u32[]{:S(2)}) collective-permute-start(f32[512,256]{1,0:T(8,128)S(1)} %shard_map.41.own_ref), channel_id=1, source_target_pairs={{1,2},{2,3},{3,4},{4,5},{5,6},{6,7},{7,8},{8,9},{9,10},{10,11},{11... | collective-permute-start | bytes 1572872 | tf_op jit(solution)/shard_map/ppermute | solution.py:164
  41.1 0.0 collective-permute-done.7
  41.1 0.1 add_add_fusion.2
  41.2 1.3 %collective-permute-start.10 = (f32[256,256]{1,0:T(8,128)S(1)}, f32[256,256]{1,0:T(8,128)S(1)}, u32[]{:S(2)}, u32[]{:S(2)}) collective-permute-start(f32[256,256]{1,0:T(8,128)S(1)} %add_add_fusion.2), channel_id=1, source_target_pairs={{0,4},{96,100},{64,68},{32,36},{256,260},{352,356},{320,324},{288,... | collective-permute-start | bytes 786440 | tf_op jit(solution)/shard_map/ppermute | solution.py:164
  42.5 1.3 %collective-permute-start.9 = (f32[256,256]{1,0:T(8,128)S(1)}, f32[256,256]{1,0:T(8,128)S(1)}, u32[]{:S(2)}, u32[]{:S(2)}) collective-permute-start(f32[256,256]{1,0:T(8,128)S(1)} %add_add_fusion.2), channel_id=1, source_target_pairs={{0,12},{96,108},{64,76},{32,44},{256,268},{352,364},{320,332},{288... | collective-permute-start | bytes 786440 | tf_op jit(solution)/shard_map/ppermute | solution.py:164
  43.8 1.3 %collective-permute-start.8 = (f32[256,256]{1,0:T(8,128)S(1)}, f32[256,256]{1,0:T(8,128)S(1)}, u32[]{:S(2)}, u32[]{:S(2)}) collective-permute-start(f32[256,256]{1,0:T(8,128)S(1)} %add_add_fusion.2), channel_id=1, source_target_pairs={{0,8},{96,104},{64,72},{32,40},{256,264},{352,360},{320,328},{288,... | collective-permute-start | bytes 786440 | tf_op jit(solution)/shard_map/ppermute | solution.py:164
  45.1 4.0 %collective-permute-done.10 = f32[256,256]{1,0:T(8,128)S(1)} collective-permute-done((f32[256,256]{1,0:T(8,128)S(1)}, f32[256,256]{1,0:T(8,128)S(1)}, u32[]{:S(2)}, u32[]{:S(2)}) %collective-permute-start.10) | collective-permute-done | bytes 262176 | tf_op jit(solution)/shard_map/ppermute | solution.py:164
  49.2 5.6 %collective-permute-done.8 = f32[256,256]{1,0:T(8,128)S(1)} collective-permute-done((f32[256,256]{1,0:T(8,128)S(1)}, f32[256,256]{1,0:T(8,128)S(1)}, u32[]{:S(2)}, u32[]{:S(2)}) %collective-permute-start.8) | collective-permute-done | bytes 262176 | tf_op jit(solution)/shard_map/ppermute | solution.py:164
  54.8 0.1 add_add_fusion.1
  54.9 1.3 %collective-permute-start.13 = (f32[256,256]{1,0:T(8,128)S(1)}, f32[256,256]{1,0:T(8,128)S(1)}, u32[]{:S(2)}, u32[]{:S(2)}) collective-permute-start(f32[256,256]{1,0:T(8,128)S(1)} %add_add_fusion.1), channel_id=1, source_target_pairs={{0,14},{96,110},{64,78},{32,46},{256,270},{352,366},{320,334},{288... | collective-permute-start | bytes 786440 | tf_op jit(solution)/shard_map/ppermute | solution.py:164
  56.2 1.3 %collective-permute-start.12 = (f32[256,256]{1,0:T(8,128)S(1)}, f32[256,256]{1,0:T(8,128)S(1)}, u32[]{:S(2)}, u32[]{:S(2)}) collective-permute-start(f32[256,256]{1,0:T(8,128)S(1)} %add_add_fusion.1), channel_id=1, source_target_pairs={{0,16},{96,112},{64,80},{32,48},{256,272},{352,368},{320,336},{288... | collective-permute-start | bytes 786440 | tf_op jit(solution)/shard_map/ppermute | solution.py:164
  57.5 1.3 %collective-permute-start.11 = (f32[256,256]{1,0:T(8,128)S(1)}, f32[256,256]{1,0:T(8,128)S(1)}, u32[]{:S(2)}, u32[]{:S(2)}) collective-permute-start(f32[256,256]{1,0:T(8,128)S(1)} %add_add_fusion.1), channel_id=1, source_target_pairs={{0,30},{96,126},{64,94},{32,62},{256,286},{352,382},{320,350},{288... | collective-permute-start | bytes 786440 | tf_op jit(solution)/shard_map/ppermute | solution.py:164
  58.8 0.1 broadcast_select_fusion.back1_ref
  58.9 1.9 %collective-permute-start.15 = (f32[512,256]{1,0:T(8,128)S(1)}, f32[512,256]{1,0:T(8,128)S(1)}, u32[]{:S(2)}, u32[]{:S(2)}) collective-permute-start(f32[512,256]{1,0:T(8,128)S(1)} %broadcast_select_fusion.back1_ref), channel_id=1, source_target_pairs={{1,2},{2,3},{3,4},{4,5},{5,6},{6,7},{7,8},{8,9},{9,10},{10,11},{11... | collective-permute-start | bytes 1572872 | tf_op jit(solution)/shard_map/ppermute | solution.py:164
  60.8 0.5 collective-permute-done.12
  61.3 1.5 %collective-permute-done.11 = f32[256,256]{1,0:T(8,128)S(1)} collective-permute-done((f32[256,256]{1,0:T(8,128)S(1)}, f32[256,256]{1,0:T(8,128)S(1)}, u32[]{:S(2)}, u32[]{:S(2)}) %collective-permute-start.11) | collective-permute-done | bytes 262176 | tf_op jit(solution)/shard_map/ppermute | solution.py:164
  62.8 0.1 add_add_fusion
  62.9 2.2 %all-gather = f32[512,256]{1,0:T(8,128)S(1)} all-gather(f32[256,256]{1,0:T(8,128)S(1)} %add_add_fusion), channel_id=2, replica_groups={{0,1},{2,3},{4,5},{6,7},{8,9},{10,11},{12,13},{14,15},{16,17},{18,19},{..., dimensions={0}, use_global_device_ids=true | all-gather | bytes 786432 | tf_op jit(solution)/shard_map/all_gather | solution.py:197
  65.1 8.5 %collective-permute-done.15.back2_ref = f32[512,256]{1,0:T(8,128)S(1)} collective-permute-done((f32[512,256]{1,0:T(8,128)S(1)}, f32[512,256]{1,0:T(8,128)S(1)}, u32[]{:S(2)}, u32[]{:S(2)}) %collective-permute-start.15) | collective-permute-done | bytes 524320 | tf_op jit(solution)/shard_map/ppermute | solution.py:164
  73.6 4.9 %shard_map.43 = (f32[256,256]{1,0:T(8,128)}, f32[256,256]{1,0:T(8,128)}) custom-call(f32[2,256,256]{2,1,0:T(8,128)S(1)} %bitcast.2, f32[512,256]{1,0:T(8,128)S(1)} %collective-permute-done.15.back2_ref, f32[512,256]{1,0:T(8,128)S(1)} %broadcast_select_fusion.back1_ref, f32[512,256]{1,0:T(8,128)S(1)} %shard_map.41.own_ref), custom_call_target="tpu_custom_call" | custom-call | tf_op jit(solution)/shard_map/pallas_call | solution.py:198
  (10 shorter events, 0.1 us)
Async XLA Ops:
  1.7 0.7 collective-permute-start
  2.5 0.7 collective-permute-start.1
  3.2 2.1 %collective-permute-start.4 = (f32[256,256]{1,0:T(8,128)S(1)}, f32[256,256]{1,0:T(8,128)S(1)}, u32[]{:S(2)}, u32[]{:S(2)}) collective-permute-start(f32[256,256]{1,0:T(8,128)S(1)} %add.39), channel_id=1, source_target_pairs={{0,32},{1,129}} | collective-permute-start | bytes 786440 | tf_op jit(solution)/shard_map/ppermute | solution.py:164
  3.9 1.4 %collective-permute-start.3 = (f32[256,256]{1,0:T(8,128)S(1)}, f32[256,256]{1,0:T(8,128)S(1)}, u32[]{:S(2)}, u32[]{:S(2)}) collective-permute-start(f32[256,256]{1,0:T(8,128)S(1)} %add.39), channel_id=1, source_target_pairs={{0,64},{1,385}} | collective-permute-start | bytes 786440 | tf_op jit(solution)/shard_map/ppermute | solution.py:164
  4.6 0.7 collective-permute-start.2
  5.4 35.7 %collective-permute-start.7 = (f32[256,256]{1,0:T(8,128)S(1)}, f32[256,256]{1,0:T(8,128)S(1)}, u32[]{:S(2)}, u32[]{:S(2)}) collective-permute-start(f32[256,256]{1,0:T(8,128)S(1)} %add_add_fusion.3), channel_id=1, source_target_pairs={{0,128},{96,224},{64,192},{32,160},{1,5},{257,261},{385,389},{129,... | collective-permute-start | bytes 786440 | tf_op jit(solution)/shard_map/ppermute | solution.py:164
  6.0 35.1 %collective-permute-start.6 = (f32[256,256]{1,0:T(8,128)S(1)}, f32[256,256]{1,0:T(8,128)S(1)}, u32[]{:S(2)}, u32[]{:S(2)}) collective-permute-start(f32[256,256]{1,0:T(8,128)S(1)} %add_add_fusion.3), channel_id=1, source_target_pairs={{0,384},{96,480},{64,448},{32,416},{1,13},{257,269},{385,397},{129... | collective-permute-start | bytes 786440 | tf_op jit(solution)/shard_map/ppermute | solution.py:164
  6.7 34.4 %collective-permute-start.5 = (f32[256,256]{1,0:T(8,128)S(1)}, f32[256,256]{1,0:T(8,128)S(1)}, u32[]{:S(2)}, u32[]{:S(2)}) collective-permute-start(f32[256,256]{1,0:T(8,128)S(1)} %add_add_fusion.3), channel_id=1, source_target_pairs={{0,256},{96,352},{64,320},{32,288},{1,9},{257,265},{385,393},{129,... | collective-permute-start | bytes 786440 | tf_op jit(solution)/shard_map/ppermute | solution.py:164
  8.0 50.8 %collective-permute-start.14 = (f32[512,256]{1,0:T(8,128)S(1)}, f32[512,256]{1,0:T(8,128)S(1)}, u32[]{:S(2)}, u32[]{:S(2)}) collective-permute-start(f32[512,256]{1,0:T(8,128)S(1)} %shard_map.41.own_ref), channel_id=1, source_target_pairs={{1,2},{2,3},{3,4},{4,5},{5,6},{6,7},{7,8},{8,9},{9,10},{10,11},{11... | collective-permute-start | bytes 1572872 | tf_op jit(solution)/shard_map/ppermute | solution.py:164
  41.2 8.0 %collective-permute-start.10 = (f32[256,256]{1,0:T(8,128)S(1)}, f32[256,256]{1,0:T(8,128)S(1)}, u32[]{:S(2)}, u32[]{:S(2)}) collective-permute-start(f32[256,256]{1,0:T(8,128)S(1)} %add_add_fusion.2), channel_id=1, source_target_pairs={{0,4},{96,100},{64,68},{32,36},{256,260},{352,356},{320,324},{288,... | collective-permute-start | bytes 786440 | tf_op jit(solution)/shard_map/ppermute | solution.py:164
  42.5 6.7 %collective-permute-start.9 = (f32[256,256]{1,0:T(8,128)S(1)}, f32[256,256]{1,0:T(8,128)S(1)}, u32[]{:S(2)}, u32[]{:S(2)}) collective-permute-start(f32[256,256]{1,0:T(8,128)S(1)} %add_add_fusion.2), channel_id=1, source_target_pairs={{0,12},{96,108},{64,76},{32,44},{256,268},{352,364},{320,332},{288... | collective-permute-start | bytes 786440 | tf_op jit(solution)/shard_map/ppermute | solution.py:164
  43.8 11.0 %collective-permute-start.8 = (f32[256,256]{1,0:T(8,128)S(1)}, f32[256,256]{1,0:T(8,128)S(1)}, u32[]{:S(2)}, u32[]{:S(2)}) collective-permute-start(f32[256,256]{1,0:T(8,128)S(1)} %add_add_fusion.2), channel_id=1, source_target_pairs={{0,8},{96,104},{64,72},{32,40},{256,264},{352,360},{320,328},{288,... | collective-permute-start | bytes 786440 | tf_op jit(solution)/shard_map/ppermute | solution.py:164
  54.9 6.0 %collective-permute-start.13 = (f32[256,256]{1,0:T(8,128)S(1)}, f32[256,256]{1,0:T(8,128)S(1)}, u32[]{:S(2)}, u32[]{:S(2)}) collective-permute-start(f32[256,256]{1,0:T(8,128)S(1)} %add_add_fusion.1), channel_id=1, source_target_pairs={{0,14},{96,110},{64,78},{32,46},{256,270},{352,366},{320,334},{288... | collective-permute-start | bytes 786440 | tf_op jit(solution)/shard_map/ppermute | solution.py:164
  56.2 5.2 %collective-permute-start.12 = (f32[256,256]{1,0:T(8,128)S(1)}, f32[256,256]{1,0:T(8,128)S(1)}, u32[]{:S(2)}, u32[]{:S(2)}) collective-permute-start(f32[256,256]{1,0:T(8,128)S(1)} %add_add_fusion.1), channel_id=1, source_target_pairs={{0,16},{96,112},{64,80},{32,48},{256,272},{352,368},{320,336},{288... | collective-permute-start | bytes 786440 | tf_op jit(solution)/shard_map/ppermute | solution.py:164
  57.5 5.4 %collective-permute-start.11 = (f32[256,256]{1,0:T(8,128)S(1)}, f32[256,256]{1,0:T(8,128)S(1)}, u32[]{:S(2)}, u32[]{:S(2)}) collective-permute-start(f32[256,256]{1,0:T(8,128)S(1)} %add_add_fusion.1), channel_id=1, source_target_pairs={{0,30},{96,126},{64,94},{32,62},{256,286},{352,382},{320,350},{288... | collective-permute-start | bytes 786440 | tf_op jit(solution)/shard_map/ppermute | solution.py:164
  58.9 14.7 %collective-permute-start.15 = (f32[512,256]{1,0:T(8,128)S(1)}, f32[512,256]{1,0:T(8,128)S(1)}, u32[]{:S(2)}, u32[]{:S(2)}) collective-permute-start(f32[512,256]{1,0:T(8,128)S(1)} %broadcast_select_fusion.back1_ref), channel_id=1, source_target_pairs={{1,2},{2,3},{3,4},{4,5},{5,6},{6,7},{7,8},{8,9},{9,10},{10,11},{11... | collective-permute-start | bytes 1572872 | tf_op jit(solution)/shard_map/ppermute | solution.py:164

commit v4 on v3

--- a/solution.py
+++ b/solution.py
@@ -18,15 +18,15 @@
 
 TREE = (
     (
-        ((0, -2, 0), (0, -4, 0), (0, 2, 0)),
-        ((2, 0, 0), (-1, 0, 0), (1, 0, 0)),
-        ((0, 0, 4), (0, 0, -2), (0, 0, 2)),
+        ((0, 0, -4), (0, 0, -2), (0, 0, 2)),
+        ((-2, 0, 0), (-1, 0, 0), (1, 0, 0)),
+        ((0, 4, 0), (0, -2, 0), (0, 2, 0)),
         ((0, 1, -1), (0, 1, 0), (0, 0, -1)),
     ),
     (
-        ((2, 0, 0), (-1, 0, 0), (1, 0, 0)),
-        ((0, 0, -4), (0, 0, -2), (0, 0, 2)),
-        ((0, 4, 0), (0, -2, 0), (0, 2, 0)),
+        ((0, -4, 0), (0, -2, 0), (0, 2, 0)),
+        ((0, 0, 4), (0, 0, -2), (0, 0, 2)),
+        ((-2, 0, 0), (-1, 0, 0), (1, 0, 0)),
         ((0, -1, 1), (0, -1, 0), (0, 0, 1)),
     ),
 )
@@ -112,26 +112,26 @@
         copy.wait()
 
 
-def factor_kernel(me_ref, own_ref, next_ref, k0_ref, k1_ref):
+def factor_kernel(me_ref, own_ref, other_ref, out_ref):
     me = me_ref[0]
 
-    @pl.when(me != 0)
+    @pl.when(me >= 2)
     def _():
-        k0_ref[...] = jnp.zeros_like(k0_ref)
-        k1_ref[...] = jnp.zeros_like(k1_ref)
-
-    @pl.when(me == 0)
+        out_ref[...] = jnp.zeros_like(out_ref)
+
+    @pl.when(me < 2)
     def _():
         identity = eye()
-        p0, n0 = own_ref[:B, :], own_ref[B:, :]
-        p1, n1 = next_ref[:B, :], next_ref[B:, :]
+        mine, other = own_ref[...], other_ref[...]
+        first, second = jnp.where(me == 0, mine, other), jnp.where(me == 0, other, mine)
+        p0, n0, p1, n1 = first[:B, :], first[B:, :], second[:B, :], second[B:, :]
         k0 = coupling_of(p0, n0, identity)
-        k0_ref[...] = k0
         k, kt = halves(k0), halves(k0.T)
         top, bottom = roots_of(k, kt, identity)
         lead_p = dot(top, halves(p0 - dot(kt, halves(n0))))
         lead_n = dot(bottom, halves(n1 - dot(k, halves(p1))))
-        k1_ref[...] = coupling_of(lead_p, lead_n, identity)
+        k1 = coupling_of(lead_p, lead_n, identity)
+        out_ref[...] = jnp.where(me == 0, k0, k1)
 
 
 def apply_kernel(k_ref, back2_ref, back1_ref, own_ref, p_ref, n_ref):
@@ -178,14 +178,13 @@
     )(positive_row, negative_row)
     second = send(own, [(0, 1), (1, 0)])
     back1 = send(own, onward)
-    k0, k1 = pl.pallas_call(
+    held = pl.pallas_call(
         factor_kernel,
-        out_shape=[pltpu.VMEM((B, B), jnp.float32)] * 2,
+        out_shape=pltpu.VMEM((B, B), jnp.float32),
         in_specs=[SMEM, VMEM, VMEM],
-        out_specs=[VMEM] * 2,
+        out_specs=VMEM,
     )(jnp.reshape(me, (1,)).astype(jnp.int32), *resident(own, second))
 
-    held = k0 + send(k1, [(0, 1)])
     back1 = jnp.where(me == 1, second, back1)
     back2 = send(back1, onward)
     rounds = tree_rounds()

time: 78.9 us -> 66 us (0.84)
  the two profiles are of different devices: /device:TPU:4 before, /device:TPU:256 now
where the time goes in v4:
time: 66 us; the launch traced here: 65.6 us
  starting transfers between devices  35.6 us (54%)
  waiting for transfers between devices  20.6 us (31%)
  Pallas kernels  5.99 us (9%)
  blocking collectives  2.18 us (3%)
  between operations  0.89 us (1%)
    ppermute x15, starting transfers between devices, send(): return lax.ppermute(array, AXIS, pairs)  35.6 us
    ppermute x15, waiting for transfers between devices, send(): return lax.ppermute(array, AXIS, pairs)  20.6 us
    pallas_call x1, Pallas kernels, steps(): pl.pallas_call(apply_kernel, out_shape=[jax.ShapeDtypeStruct((B, B), jnp....  4.92 us
    all_gather x1, blocking collectives, steps(): both = lax.all_gather(held, AXIS, axis=0, axis_index_groups=cores)  2.18 us
  transfers between devices with their start and end apart: 15, of which 4 were waited for; matrix products, arithmetic and copies ran while one was open for 0% of the time, Pallas kernels for 0%

profile of v4, /device:TPU:256, one launch (start us, length us, event | category | flops | bytes accessed | tf_op | source)
XLA Modules:
  0.0 65.6 jit_solution(15454387258968184810)
XLA Ops:
  0.6 1.0 %shard_map.41.own_ref = f32[512,256]{1,0:T(8,128)S(1)} custom-call(f32[256,256]{1,0:T(8,128)} %p_ref.1, f32[256,256]{1,0:T(8,128)} %n_ref.1), custom_call_target="tpu_custom_call" | custom-call | tf_op jit(solution)/shard_map/pallas_call | solution.py:172
  1.7 0.7 %collective-permute-start = (f32[512,256]{1,0:T(8,128)S(1)}, f32[512,256]{1,0:T(8,128)S(1)}, u32[]{:S(2)}, u32[]{:S(2)}) collective-permute-start(f32[512,256]{1,0:T(8,128)S(1)} %shard_map.41.own_ref), channel_id=1, source_target_pairs={{0,1},{1,0}} | collective-permute-start | bytes 1572872 | tf_op jit(solution)/shard_map/ppermute | solution.py:164
  2.4 0.0 collective-permute-done.other_ref
  2.4 0.7 %collective-permute-start.3 = (f32[256,256]{1,0:T(8,128)S(1)}, f32[256,256]{1,0:T(8,128)S(1)}, u32[]{:S(2)}, u32[]{:S(2)}) collective-permute-start(f32[256,256]{1,0:T(8,128)S(1)} %shard_map.42), channel_id=1, source_target_pairs={{0,4},{1,33}} | collective-permute-start | bytes 786440 | tf_op jit(solution)/shard_map/ppermute | solution.py:164
  3.1 0.7 %collective-permute-start.2 = (f32[256,256]{1,0:T(8,128)S(1)}, f32[256,256]{1,0:T(8,128)S(1)}, u32[]{:S(2)}, u32[]{:S(2)}) collective-permute-start(f32[256,256]{1,0:T(8,128)S(1)} %shard_map.42), channel_id=1, source_target_pairs={{0,12},{1,97}} | collective-permute-start | bytes 786440 | tf_op jit(solution)/shard_map/ppermute | solution.py:164
  3.8 0.7 %collective-permute-start.1 = (f32[256,256]{1,0:T(8,128)S(1)}, f32[256,256]{1,0:T(8,128)S(1)}, u32[]{:S(2)}, u32[]{:S(2)}) collective-permute-start(f32[256,256]{1,0:T(8,128)S(1)} %shard_map.42), channel_id=1, source_target_pairs={{0,8},{1,65}} | collective-permute-start | bytes 786440 | tf_op jit(solution)/shard_map/ppermute | solution.py:164
  4.5 0.0 collective-permute-done.2
  4.5 0.1 add_add_fusion.3
  4.6 0.7 %collective-permute-start.6 = (f32[256,256]{1,0:T(8,128)S(1)}, f32[256,256]{1,0:T(8,128)S(1)}, u32[]{:S(2)}, u32[]{:S(2)}) collective-permute-start(f32[256,256]{1,0:T(8,128)S(1)} %add_add_fusion.3), channel_id=1, source_target_pairs={{0,128},{8,136},{12,140},{4,132},{1,5},{65,69},{97,101},{33,37}} | collective-permute-start | bytes 786440 | tf_op jit(solution)/shard_map/ppermute | solution.py:164
  5.3 0.7 %collective-permute-start.5 = (f32[256,256]{1,0:T(8,128)S(1)}, f32[256,256]{1,0:T(8,128)S(1)}, u32[]{:S(2)}, u32[]{:S(2)}) collective-permute-start(f32[256,256]{1,0:T(8,128)S(1)} %add_add_fusion.3), channel_id=1, source_target_pairs={{0,384},{8,392},{12,396},{4,388},{1,13},{65,77},{97,109},{33,45}} | collective-permute-start | bytes 786440 | tf_op jit(solution)/shard_map/ppermute | solution.py:164
  6.0 0.7 %collective-permute-start.4 = (f32[256,256]{1,0:T(8,128)S(1)}, f32[256,256]{1,0:T(8,128)S(1)}, u32[]{:S(2)}, u32[]{:S(2)}) collective-permute-start(f32[256,256]{1,0:T(8,128)S(1)} %add_add_fusion.3), channel_id=1, source_target_pairs={{0,256},{8,264},{12,268},{4,260},{1,9},{65,73},{97,105},{33,41}} | collective-permute-start | bytes 786440 | tf_op jit(solution)/shard_map/ppermute | solution.py:164
  6.7 22.4 %collective-permute-start.13 = (f32[512,256]{1,0:T(8,128)S(1)}, f32[512,256]{1,0:T(8,128)S(1)}, u32[]{:S(2)}, u32[]{:S(2)}) collective-permute-start(f32[512,256]{1,0:T(8,128)S(1)} %shard_map.41.own_ref), channel_id=1, source_target_pairs={{1,2},{2,3},{3,4},{4,5},{5,6},{6,7},{7,8},{8,9},{9,10},{10,11},{11... | collective-permute-start | bytes 1572872 | tf_op jit(solution)/shard_map/ppermute | solution.py:164
  29.0 0.0 collective-permute-done.5
  29.1 0.0 collective-permute-done.4
  29.1 0.1 add_add_fusion.2
  29.1 0.7 %collective-permute-start.9 = (f32[256,256]{1,0:T(8,128)S(1)}, f32[256,256]{1,0:T(8,128)S(1)}, u32[]{:S(2)}, u32[]{:S(2)}) collective-permute-start(f32[256,256]{1,0:T(8,128)S(1)} %add_add_fusion.2), channel_id=1, source_target_pairs={{0,32},{8,40},{12,44},{4,36},{256,288},{264,296},{268,300},{260,29... | collective-permute-start | bytes 786440 | tf_op jit(solution)/shard_map/ppermute | solution.py:164
  29.8 0.7 %collective-permute-start.8 = (f32[256,256]{1,0:T(8,128)S(1)}, f32[256,256]{1,0:T(8,128)S(1)}, u32[]{:S(2)}, u32[]{:S(2)}) collective-permute-start(f32[256,256]{1,0:T(8,128)S(1)} %add_add_fusion.2), channel_id=1, source_target_pairs={{0,96},{8,104},{12,108},{4,100},{256,352},{264,360},{268,364},{260... | collective-permute-start | bytes 786440 | tf_op jit(solution)/shard_map/ppermute | solution.py:164
  30.5 1.3 %collective-permute-start.7 = (f32[256,256]{1,0:T(8,128)S(1)}, f32[256,256]{1,0:T(8,128)S(1)}, u32[]{:S(2)}, u32[]{:S(2)}) collective-permute-start(f32[256,256]{1,0:T(8,128)S(1)} %add_add_fusion.2), channel_id=1, source_target_pairs={{0,64},{8,72},{12,76},{4,68},{256,320},{264,328},{268,332},{260,32... | collective-permute-start | bytes 786440 | tf_op jit(solution)/shard_map/ppermute | solution.py:164
  31.8 0.0 collective-permute-done.8
  31.8 10.9 %collective-permute-done.7 = f32[256,256]{1,0:T(8,128)S(1)} collective-permute-done((f32[256,256]{1,0:T(8,128)S(1)}, f32[256,256]{1,0:T(8,128)S(1)}, u32[]{:S(2)}, u32[]{:S(2)}) %collective-permute-start.7) | collective-permute-done | bytes 262176 | tf_op jit(solution)/shard_map/ppermute | solution.py:164
  42.8 0.1 add_add_fusion.1
  42.9 1.3 %collective-permute-start.12 = (f32[256,256]{1,0:T(8,128)S(1)}, f32[256,256]{1,0:T(8,128)S(1)}, u32[]{:S(2)}, u32[]{:S(2)}) collective-permute-start(f32[256,256]{1,0:T(8,128)S(1)} %add_add_fusion.1), channel_id=1, source_target_pairs={{0,14},{8,6},{12,10},{4,2},{256,270},{264,262},{268,266},{260,258}... | collective-permute-start | bytes 786440 | tf_op jit(solution)/shard_map/ppermute | solution.py:164
  44.2 1.3 %collective-permute-start.11 = (f32[256,256]{1,0:T(8,128)S(1)}, f32[256,256]{1,0:T(8,128)S(1)}, u32[]{:S(2)}, u32[]{:S(2)}) collective-permute-start(f32[256,256]{1,0:T(8,128)S(1)} %add_add_fusion.1), channel_id=1, source_target_pairs={{0,16},{8,24},{12,28},{4,20},{256,272},{264,280},{268,284},{260,27... | collective-permute-start | bytes 786440 | tf_op jit(solution)/shard_map/ppermute | solution.py:164
  45.5 1.3 %collective-permute-start.10 = (f32[256,256]{1,0:T(8,128)S(1)}, f32[256,256]{1,0:T(8,128)S(1)}, u32[]{:S(2)}, u32[]{:S(2)}) collective-permute-start(f32[256,256]{1,0:T(8,128)S(1)} %add_add_fusion.1), channel_id=1, source_target_pairs={{0,30},{8,22},{12,26},{4,18},{256,286},{264,278},{268,282},{260,27... | collective-permute-start | bytes 786440 | tf_op jit(solution)/shard_map/ppermute | solution.py:164
  46.8 0.1 broadcast_select_fusion.back1_ref
  46.9 1.9 %collective-permute-start.14 = (f32[512,256]{1,0:T(8,128)S(1)}, f32[512,256]{1,0:T(8,128)S(1)}, u32[]{:S(2)}, u32[]{:S(2)}) collective-permute-start(f32[512,256]{1,0:T(8,128)S(1)} %broadcast_select_fusion.back1_ref), channel_id=1, source_target_pairs={{1,2},{2,3},{3,4},{4,5},{5,6},{6,7},{7,8},{8,9},{9,10},{10,11},{11... | collective-permute-start | bytes 1572872 | tf_op jit(solution)/shard_map/ppermute | solution.py:164
  48.8 0.5 collective-permute-done.11
  49.3 1.5 %collective-permute-done.10 = f32[256,256]{1,0:T(8,128)S(1)} collective-permute-done((f32[256,256]{1,0:T(8,128)S(1)}, f32[256,256]{1,0:T(8,128)S(1)}, u32[]{:S(2)}, u32[]{:S(2)}) %collective-permute-start.10) | collective-permute-done | bytes 262176 | tf_op jit(solution)/shard_map/ppermute | solution.py:164
  50.8 0.1 add_add_fusion
  50.9 2.2 %all-gather = f32[512,256]{1,0:T(8,128)S(1)} all-gather(f32[256,256]{1,0:T(8,128)S(1)} %add_add_fusion), channel_id=2, replica_groups={{0,1},{2,3},{4,5},{6,7},{8,9},{10,11},{12,13},{14,15},{16,17},{18,19},{..., dimensions={0}, use_global_device_ids=true | all-gather | bytes 786432 | tf_op jit(solution)/shard_map/all_gather | solution.py:196
  53.1 7.6 %collective-permute-done.14.back2_ref = f32[512,256]{1,0:T(8,128)S(1)} collective-permute-done((f32[512,256]{1,0:T(8,128)S(1)}, f32[512,256]{1,0:T(8,128)S(1)}, u32[]{:S(2)}, u32[]{:S(2)}) %collective-permute-start.14) | collective-permute-done | bytes 524320 | tf_op jit(solution)/shard_map/ppermute | solution.py:164
  60.7 4.9 %shard_map.43 = (f32[256,256]{1,0:T(8,128)}, f32[256,256]{1,0:T(8,128)}) custom-call(f32[2,256,256]{2,1,0:T(8,128)S(1)} %bitcast.2, f32[512,256]{1,0:T(8,128)S(1)} %collective-permute-done.14.back2_ref, f32[512,256]{1,0:T(8,128)S(1)} %broadcast_select_fusion.back1_ref, f32[512,256]{1,0:T(8,128)S(1)} %shard_map.41.own_ref), custom_call_target="tpu_custom_call" | custom-call | tf_op jit(solution)/shard_map/pallas_call | solution.py:197
  (7 shorter events, 0.0 us)
Async XLA Ops:
  1.7 0.7 %collective-permute-start = (f32[512,256]{1,0:T(8,128)S(1)}, f32[512,256]{1,0:T(8,128)S(1)}, u32[]{:S(2)}, u32[]{:S(2)}) collective-permute-start(f32[512,256]{1,0:T(8,128)S(1)} %shard_map.41.own_ref), channel_id=1, source_target_pairs={{0,1},{1,0}} | collective-permute-start | bytes 1572872 | tf_op jit(solution)/shard_map/ppermute | solution.py:164
  2.4 2.1 %collective-permute-start.3 = (f32[256,256]{1,0:T(8,128)S(1)}, f32[256,256]{1,0:T(8,128)S(1)}, u32[]{:S(2)}, u32[]{:S(2)}) collective-permute-start(f32[256,256]{1,0:T(8,128)S(1)} %shard_map.42), channel_id=1, source_target_pairs={{0,4},{1,33}} | collective-permute-start | bytes 786440 | tf_op jit(solution)/shard_map/ppermute | solution.py:164
  3.1 1.4 %collective-permute-start.2 = (f32[256,256]{1,0:T(8,128)S(1)}, f32[256,256]{1,0:T(8,128)S(1)}, u32[]{:S(2)}, u32[]{:S(2)}) collective-permute-start(f32[256,256]{1,0:T(8,128)S(1)} %shard_map.42), channel_id=1, source_target_pairs={{0,12},{1,97}} | collective-permute-start | bytes 786440 | tf_op jit(solution)/shard_map/ppermute | solution.py:164
  3.8 0.7 %collective-permute-start.1 = (f32[256,256]{1,0:T(8,128)S(1)}, f32[256,256]{1,0:T(8,128)S(1)}, u32[]{:S(2)}, u32[]{:S(2)}) collective-permute-start(f32[256,256]{1,0:T(8,128)S(1)} %shard_map.42), channel_id=1, source_target_pairs={{0,8},{1,65}} | collective-permute-start | bytes 786440 | tf_op jit(solution)/shard_map/ppermute | solution.py:164
  4.6 24.4 %collective-permute-start.6 = (f32[256,256]{1,0:T(8,128)S(1)}, f32[256,256]{1,0:T(8,128)S(1)}, u32[]{:S(2)}, u32[]{:S(2)}) collective-permute-start(f32[256,256]{1,0:T(8,128)S(1)} %add_add_fusion.3), channel_id=1, source_target_pairs={{0,128},{8,136},{12,140},{4,132},{1,5},{65,69},{97,101},{33,37}} | collective-permute-start | bytes 786440 | tf_op jit(solution)/shard_map/ppermute | solution.py:164
  5.3 23.8 %collective-permute-start.5 = (f32[256,256]{1,0:T(8,128)S(1)}, f32[256,256]{1,0:T(8,128)S(1)}, u32[]{:S(2)}, u32[]{:S(2)}) collective-permute-start(f32[256,256]{1,0:T(8,128)S(1)} %add_add_fusion.3), channel_id=1, source_target_pairs={{0,384},{8,392},{12,396},{4,388},{1,13},{65,77},{97,109},{33,45}} | collective-permute-start | bytes 786440 | tf_op jit(solution)/shard_map/ppermute | solution.py:164
  6.0 23.1 %collective-permute-start.4 = (f32[256,256]{1,0:T(8,128)S(1)}, f32[256,256]{1,0:T(8,128)S(1)}, u32[]{:S(2)}, u32[]{:S(2)}) collective-permute-start(f32[256,256]{1,0:T(8,128)S(1)} %add_add_fusion.3), channel_id=1, source_target_pairs={{0,256},{8,264},{12,268},{4,260},{1,9},{65,73},{97,105},{33,41}} | collective-permute-start | bytes 786440 | tf_op jit(solution)/shard_map/ppermute | solution.py:164
  6.7 40.1 %collective-permute-start.13 = (f32[512,256]{1,0:T(8,128)S(1)}, f32[512,256]{1,0:T(8,128)S(1)}, u32[]{:S(2)}, u32[]{:S(2)}) collective-permute-start(f32[512,256]{1,0:T(8,128)S(1)} %shard_map.41.own_ref), channel_id=1, source_target_pairs={{1,2},{2,3},{3,4},{4,5},{5,6},{6,7},{7,8},{8,9},{9,10},{10,11},{11... | collective-permute-start | bytes 1572872 | tf_op jit(solution)/shard_map/ppermute | solution.py:164
  29.1 2.7 %collective-permute-start.9 = (f32[256,256]{1,0:T(8,128)S(1)}, f32[256,256]{1,0:T(8,128)S(1)}, u32[]{:S(2)}, u32[]{:S(2)}) collective-permute-start(f32[256,256]{1,0:T(8,128)S(1)} %add_add_fusion.2), channel_id=1, source_target_pairs={{0,32},{8,40},{12,44},{4,36},{256,288},{264,296},{268,300},{260,29... | collective-permute-start | bytes 786440 | tf_op jit(solution)/shard_map/ppermute | solution.py:164
  29.8 2.0 %collective-permute-start.8 = (f32[256,256]{1,0:T(8,128)S(1)}, f32[256,256]{1,0:T(8,128)S(1)}, u32[]{:S(2)}, u32[]{:S(2)}) collective-permute-start(f32[256,256]{1,0:T(8,128)S(1)} %add_add_fusion.2), channel_id=1, source_target_pairs={{0,96},{8,104},{12,108},{4,100},{256,352},{264,360},{268,364},{260... | collective-permute-start | bytes 786440 | tf_op jit(solution)/shard_map/ppermute | solution.py:164
  30.5 12.3 %collective-permute-start.7 = (f32[256,256]{1,0:T(8,128)S(1)}, f32[256,256]{1,0:T(8,128)S(1)}, u32[]{:S(2)}, u32[]{:S(2)}) collective-permute-start(f32[256,256]{1,0:T(8,128)S(1)} %add_add_fusion.2), channel_id=1, source_target_pairs={{0,64},{8,72},{12,76},{4,68},{256,320},{264,328},{268,332},{260,32... | collective-permute-start | bytes 786440 | tf_op jit(solution)/shard_map/ppermute | solution.py:164
  42.9 6.0 %collective-permute-start.12 = (f32[256,256]{1,0:T(8,128)S(1)}, f32[256,256]{1,0:T(8,128)S(1)}, u32[]{:S(2)}, u32[]{:S(2)}) collective-permute-start(f32[256,256]{1,0:T(8,128)S(1)} %add_add_fusion.1), channel_id=1, source_target_pairs={{0,14},{8,6},{12,10},{4,2},{256,270},{264,262},{268,266},{260,258}... | collective-permute-start | bytes 786440 | tf_op jit(solution)/shard_map/ppermute | solution.py:164
  44.2 5.2 %collective-permute-start.11 = (f32[256,256]{1,0:T(8,128)S(1)}, f32[256,256]{1,0:T(8,128)S(1)}, u32[]{:S(2)}, u32[]{:S(2)}) collective-permute-start(f32[256,256]{1,0:T(8,128)S(1)} %add_add_fusion.1), channel_id=1, source_target_pairs={{0,16},{8,24},{12,28},{4,20},{256,272},{264,280},{268,284},{260,27... | collective-permute-start | bytes 786440 | tf_op jit(solution)/shard_map/ppermute | solution.py:164
  45.5 5.4 %collective-permute-start.10 = (f32[256,256]{1,0:T(8,128)S(1)}, f32[256,256]{1,0:T(8,128)S(1)}, u32[]{:S(2)}, u32[]{:S(2)}) collective-permute-start(f32[256,256]{1,0:T(8,128)S(1)} %add_add_fusion.1), channel_id=1, source_target_pairs={{0,30},{8,22},{12,26},{4,18},{256,286},{264,278},{268,282},{260,27... | collective-permute-start | bytes 786440 | tf_op jit(solution)/shard_map/ppermute | solution.py:164
  46.9 13.8 %collective-permute-start.14 = (f32[512,256]{1,0:T(8,128)S(1)}, f32[512,256]{1,0:T(8,128)S(1)}, u32[]{:S(2)}, u32[]{:S(2)}) collective-permute-start(f32[512,256]{1,0:T(8,128)S(1)} %broadcast_select_fusion.back1_ref), channel_id=1, source_target_pairs={{1,2},{2,3},{3,4},{4,5},{5,6},{6,7},{7,8},{8,9},{9,10},{10,11},{11... | collective-permute-start | bytes 1572872 | tf_op jit(solution)/shard_map/ppermute | solution.py:164

commit v5 on v4

--- a/solution.py
+++ b/solution.py
@@ -18,16 +18,16 @@
 
 TREE = (
     (
-        ((0, 0, -4), (0, 0, -2), (0, 0, 2)),
-        ((-2, 0, 0), (-1, 0, 0), (1, 0, 0)),
-        ((0, 4, 0), (0, -2, 0), (0, 2, 0)),
-        ((0, 1, -1), (0, 1, 0), (0, 0, -1)),
+        ((0, 2, 0), (0, -2, 0), (0, -4, 0)),
+        ((0, 0, 4), (0, 0, -2), (0, 0, 2)),
+        ((2, 0, 0), (-1, 0, 0), (1, 0, 0)),
+        ((0, -1, -1), (0, -1, 0), (0, 0, -1)),
     ),
     (
-        ((0, -4, 0), (0, -2, 0), (0, 2, 0)),
-        ((0, 0, 4), (0, 0, -2), (0, 0, 2)),
-        ((-2, 0, 0), (-1, 0, 0), (1, 0, 0)),
-        ((0, -1, 1), (0, -1, 0), (0, 0, 1)),
+        ((0, 0, -4), (0, 0, -2), (0, 0, 2)),
+        ((0, 2, 0), (0, -2, 0), (0, -4, 0)),
+        ((0, -1, -1), (0, -1, 0), (0, 0, -1)),
+        ((2, 0, 0), (-1, 0, 0), (1, 0, 0)),
     ),
 )
 

time: 66 us -> 78.6 us (1.19)
  the two profiles are of different devices: /device:TPU:256 before, /device:TPU:4 now
where the time goes in v5:
time: 78.6 us; the launch traced here: 78.2 us
  waiting for transfers between devices  53.6 us (68%)
  starting transfers between devices  15.2 us (19%)
  Pallas kernels  5.99 us (8%)
  blocking collectives  2.18 us (3%)
  between operations  0.89 us (1%)
    ppermute x15, waiting for transfers between devices, send(): return lax.ppermute(array, AXIS, pairs)  53.6 us
    ppermute x15, starting transfers between devices, send(): return lax.ppermute(array, AXIS, pairs)  15.2 us
    pallas_call x1, Pallas kernels, steps(): pl.pallas_call(apply_kernel, out_shape=[jax.ShapeDtypeStruct((B, B), jnp....  4.92 us
    all_gather x1, blocking collectives, steps(): both = lax.all_gather(held, AXIS, axis=0, axis_index_groups=cores)  2.18 us
  transfers between devices with their start and end apart: 15, of which 4 were waited for; matrix products, arithmetic and copies ran while one was open for 0% of the time, Pallas kernels for 0%

profile of v5, /device:TPU:4, one launch (start us, length us, event | category | flops | bytes accessed | tf_op | source)
XLA Modules:
  0.0 78.2 jit_solution(11498866781837820609)
XLA Ops:
  0.6 1.0 %shard_map.41.own_ref = f32[512,256]{1,0:T(8,128)S(1)} custom-call(f32[256,256]{1,0:T(8,128)} %p_ref.1, f32[256,256]{1,0:T(8,128)} %n_ref.1), custom_call_target="tpu_custom_call" | custom-call | tf_op jit(solution)/shard_map/pallas_call | solution.py:172
  1.7 0.7 collective-permute-start
  2.4 0.0 collective-permute-done.other_ref
  2.4 0.7 collective-permute-start.3
  3.1 0.7 collective-permute-start.2
  3.8 0.7 collective-permute-start.1
  4.5 0.0 collective-permute-done.2
  4.5 0.0 collective-permute-done.1
  4.5 0.1 add_add_fusion.3
  4.6 0.7 collective-permute-start.6
  5.3 0.7 collective-permute-start.5
  6.0 0.7 collective-permute-start.4
  6.7 1.9 %collective-permute-start.13 = (f32[512,256]{1,0:T(8,128)S(1)}, f32[512,256]{1,0:T(8,128)S(1)}, u32[]{:S(2)}, u32[]{:S(2)}) collective-permute-start(f32[512,256]{1,0:T(8,128)S(1)} %shard_map.41.own_ref), channel_id=1, source_target_pairs={{1,2},{2,3},{3,4},{4,5},{5,6},{6,7},{7,8},{8,9},{9,10},{10,11},{11... | collective-permute-start | bytes 1572872 | tf_op jit(solution)/shard_map/ppermute | solution.py:164
  8.6 0.0 collective-permute-done.5
  8.6 0.0 collective-permute-done.4
  8.6 0.1 add_add_fusion.2
  8.7 0.7 collective-permute-start.9
  9.4 0.7 collective-permute-start.8
  10.1 1.3 %collective-permute-start.7 = (f32[256,256]{1,0:T(8,128)S(1)}, f32[256,256]{1,0:T(8,128)S(1)}, u32[]{:S(2)}, u32[]{:S(2)}) collective-permute-start(f32[256,256]{1,0:T(8,128)S(1)} %add_add_fusion.2), channel_id=1, source_target_pairs={{0,256},{32,288},{96,352},{64,320},{8,264},{40,296},{104,360},{72,... | collective-permute-start | bytes 786440 | tf_op jit(solution)/shard_map/ppermute | solution.py:164
  11.4 43.0 %collective-permute-done.7 = f32[256,256]{1,0:T(8,128)S(1)} collective-permute-done((f32[256,256]{1,0:T(8,128)S(1)}, f32[256,256]{1,0:T(8,128)S(1)}, u32[]{:S(2)}, u32[]{:S(2)}) %collective-permute-start.7) | collective-permute-done | bytes 262176 | tf_op jit(solution)/shard_map/ppermute | solution.py:164
  54.4 0.1 add_add_fusion.1
  54.5 1.3 %collective-permute-start.12 = (f32[256,256]{1,0:T(8,128)S(1)}, f32[256,256]{1,0:T(8,128)S(1)}, u32[]{:S(2)}, u32[]{:S(2)}) collective-permute-start(f32[256,256]{1,0:T(8,128)S(1)} %add_add_fusion.1), channel_id=1, source_target_pairs={{0,14},{32,46},{96,110},{64,78},{8,6},{40,38},{104,102},{72,70},{1... | collective-permute-start | bytes 786440 | tf_op jit(solution)/shard_map/ppermute | solution.py:164
  55.8 1.3 %collective-permute-start.11 = (f32[256,256]{1,0:T(8,128)S(1)}, f32[256,256]{1,0:T(8,128)S(1)}, u32[]{:S(2)}, u32[]{:S(2)}) collective-permute-start(f32[256,256]{1,0:T(8,128)S(1)} %add_add_fusion.1), channel_id=1, source_target_pairs={{0,112},{32,16},{96,80},{64,48},{8,120},{40,24},{104,88},{72,56},{... | collective-permute-start | bytes 786440 | tf_op jit(solution)/shard_map/ppermute | solution.py:164
  57.1 1.3 %collective-permute-start.10 = (f32[256,256]{1,0:T(8,128)S(1)}, f32[256,256]{1,0:T(8,128)S(1)}, u32[]{:S(2)}, u32[]{:S(2)}) collective-permute-start(f32[256,256]{1,0:T(8,128)S(1)} %add_add_fusion.1), channel_id=1, source_target_pairs={{0,126},{32,30},{96,94},{64,62},{8,118},{40,22},{104,86},{72,54},{... | collective-permute-start | bytes 786440 | tf_op jit(solution)/shard_map/ppermute | solution.py:164
  58.5 0.1 broadcast_select_fusion.back1_ref
  58.5 1.9 %collective-permute-start.14 = (f32[512,256]{1,0:T(8,128)S(1)}, f32[512,256]{1,0:T(8,128)S(1)}, u32[]{:S(2)}, u32[]{:S(2)}) collective-permute-start(f32[512,256]{1,0:T(8,128)S(1)} %broadcast_select_fusion.back1_ref), channel_id=1, source_target_pairs={{1,2},{2,3},{3,4},{4,5},{5,6},{6,7},{7,8},{8,9},{9,10},{10,11},{11... | collective-permute-start | bytes 1572872 | tf_op jit(solution)/shard_map/ppermute | solution.py:164
  60.5 0.5 collective-permute-done.11
  61.0 1.5 %collective-permute-done.10 = f32[256,256]{1,0:T(8,128)S(1)} collective-permute-done((f32[256,256]{1,0:T(8,128)S(1)}, f32[256,256]{1,0:T(8,128)S(1)}, u32[]{:S(2)}, u32[]{:S(2)}) %collective-permute-start.10) | collective-permute-done | bytes 262176 | tf_op jit(solution)/shard_map/ppermute | solution.py:164
  62.5 0.1 add_add_fusion
  62.6 2.2 %all-gather = f32[512,256]{1,0:T(8,128)S(1)} all-gather(f32[256,256]{1,0:T(8,128)S(1)} %add_add_fusion), channel_id=2, replica_groups={{0,1},{2,3},{4,5},{6,7},{8,9},{10,11},{12,13},{14,15},{16,17},{18,19},{..., dimensions={0}, use_global_device_ids=true | all-gather | bytes 786432 | tf_op jit(solution)/shard_map/all_gather | solution.py:196
  64.7 8.5 %collective-permute-done.14.back2_ref = f32[512,256]{1,0:T(8,128)S(1)} collective-permute-done((f32[512,256]{1,0:T(8,128)S(1)}, f32[512,256]{1,0:T(8,128)S(1)}, u32[]{:S(2)}, u32[]{:S(2)}) %collective-permute-start.14) | collective-permute-done | bytes 524320 | tf_op jit(solution)/shard_map/ppermute | solution.py:164
  73.3 4.9 %shard_map.43 = (f32[256,256]{1,0:T(8,128)}, f32[256,256]{1,0:T(8,128)}) custom-call(f32[2,256,256]{2,1,0:T(8,128)S(1)} %bitcast.2, f32[512,256]{1,0:T(8,128)S(1)} %collective-permute-done.14.back2_ref, f32[512,256]{1,0:T(8,128)S(1)} %broadcast_select_fusion.back1_ref, f32[512,256]{1,0:T(8,128)S(1)} %shard_map.41.own_ref), custom_call_target="tpu_custom_call" | custom-call | tf_op jit(solution)/shard_map/pallas_call | solution.py:197
  (7 shorter events, 0.0 us)
Async XLA Ops:
  1.7 0.7 collective-permute-start
  2.4 2.1 %collective-permute-start.3 = (f32[256,256]{1,0:T(8,128)S(1)}, f32[256,256]{1,0:T(8,128)S(1)}, u32[]{:S(2)}, u32[]{:S(2)}) collective-permute-start(f32[256,256]{1,0:T(8,128)S(1)} %shard_map.42), channel_id=1, source_target_pairs={{0,64},{1,5}} | collective-permute-start | bytes 786440 | tf_op jit(solution)/shard_map/ppermute | solution.py:164
  3.1 1.4 %collective-permute-start.2 = (f32[256,256]{1,0:T(8,128)S(1)}, f32[256,256]{1,0:T(8,128)S(1)}, u32[]{:S(2)}, u32[]{:S(2)}) collective-permute-start(f32[256,256]{1,0:T(8,128)S(1)} %shard_map.42), channel_id=1, source_target_pairs={{0,96},{1,13}} | collective-permute-start | bytes 786440 | tf_op jit(solution)/shard_map/ppermute | solution.py:164
  3.8 0.7 collective-permute-start.1
  4.6 4.0 %collective-permute-start.6 = (f32[256,256]{1,0:T(8,128)S(1)}, f32[256,256]{1,0:T(8,128)S(1)}, u32[]{:S(2)}, u32[]{:S(2)}) collective-permute-start(f32[256,256]{1,0:T(8,128)S(1)} %add_add_fusion.3), channel_id=1, source_target_pairs={{0,4},{32,36},{96,100},{64,68},{1,65},{9,73},{13,77},{5,69}} | collective-permute-start | bytes 786440 | tf_op jit(solution)/shard_map/ppermute | solution.py:164
  5.3 3.3 %collective-permute-start.5 = (f32[256,256]{1,0:T(8,128)S(1)}, f32[256,256]{1,0:T(8,128)S(1)}, u32[]{:S(2)}, u32[]{:S(2)}) collective-permute-start(f32[256,256]{1,0:T(8,128)S(1)} %add_add_fusion.3), channel_id=1, source_target_pairs={{0,12},{32,44},{96,108},{64,76},{1,97},{9,105},{13,109},{5,101}} | collective-permute-start | bytes 786440 | tf_op jit(solution)/shard_map/ppermute | solution.py:164
  6.0 2.6 %collective-permute-start.4 = (f32[256,256]{1,0:T(8,128)S(1)}, f32[256,256]{1,0:T(8,128)S(1)}, u32[]{:S(2)}, u32[]{:S(2)}) collective-permute-start(f32[256,256]{1,0:T(8,128)S(1)} %add_add_fusion.3), channel_id=1, source_target_pairs={{0,8},{32,40},{96,104},{64,72},{1,33},{9,41},{13,45},{5,37}} | collective-permute-start | bytes 786440 | tf_op jit(solution)/shard_map/ppermute | solution.py:164
  6.7 51.8 %collective-permute-start.13 = (f32[512,256]{1,0:T(8,128)S(1)}, f32[512,256]{1,0:T(8,128)S(1)}, u32[]{:S(2)}, u32[]{:S(2)}) collective-permute-start(f32[512,256]{1,0:T(8,128)S(1)} %shard_map.41.own_ref), channel_id=1, source_target_pairs={{1,2},{2,3},{3,4},{4,5},{5,6},{6,7},{7,8},{8,9},{9,10},{10,11},{11... | collective-permute-start | bytes 1572872 | tf_op jit(solution)/shard_map/ppermute | solution.py:164
  8.7 2.7 %collective-permute-start.9 = (f32[256,256]{1,0:T(8,128)S(1)}, f32[256,256]{1,0:T(8,128)S(1)}, u32[]{:S(2)}, u32[]{:S(2)}) collective-permute-start(f32[256,256]{1,0:T(8,128)S(1)} %add_add_fusion.2), channel_id=1, source_target_pairs={{0,128},{32,160},{96,224},{64,192},{8,136},{40,168},{104,232},{72,... | collective-permute-start | bytes 786440 | tf_op jit(solution)/shard_map/ppermute | solution.py:164
  9.4 2.0 %collective-permute-start.8 = (f32[256,256]{1,0:T(8,128)S(1)}, f32[256,256]{1,0:T(8,128)S(1)}, u32[]{:S(2)}, u32[]{:S(2)}) collective-permute-start(f32[256,256]{1,0:T(8,128)S(1)} %add_add_fusion.2), channel_id=1, source_target_pairs={{0,384},{32,416},{96,480},{64,448},{8,392},{40,424},{104,488},{72,... | collective-permute-start | bytes 786440 | tf_op jit(solution)/shard_map/ppermute | solution.py:164
  10.1 44.4 %collective-permute-start.7 = (f32[256,256]{1,0:T(8,128)S(1)}, f32[256,256]{1,0:T(8,128)S(1)}, u32[]{:S(2)}, u32[]{:S(2)}) collective-permute-start(f32[256,256]{1,0:T(8,128)S(1)} %add_add_fusion.2), channel_id=1, source_target_pairs={{0,256},{32,288},{96,352},{64,320},{8,264},{40,296},{104,360},{72,... | collective-permute-start | bytes 786440 | tf_op jit(solution)/shard_map/ppermute | solution.py:164
  54.5 6.0 %collective-permute-start.12 = (f32[256,256]{1,0:T(8,128)S(1)}, f32[256,256]{1,0:T(8,128)S(1)}, u32[]{:S(2)}, u32[]{:S(2)}) collective-permute-start(f32[256,256]{1,0:T(8,128)S(1)} %add_add_fusion.1), channel_id=1, source_target_pairs={{0,14},{32,46},{96,110},{64,78},{8,6},{40,38},{104,102},{72,70},{1... | collective-permute-start | bytes 786440 | tf_op jit(solution)/shard_map/ppermute | solution.py:164
  55.8 5.2 %collective-permute-start.11 = (f32[256,256]{1,0:T(8,128)S(1)}, f32[256,256]{1,0:T(8,128)S(1)}, u32[]{:S(2)}, u32[]{:S(2)}) collective-permute-start(f32[256,256]{1,0:T(8,128)S(1)} %add_add_fusion.1), channel_id=1, source_target_pairs={{0,112},{32,16},{96,80},{64,48},{8,120},{40,24},{104,88},{72,56},{... | collective-permute-start | bytes 786440 | tf_op jit(solution)/shard_map/ppermute | solution.py:164
  57.1 5.4 %collective-permute-start.10 = (f32[256,256]{1,0:T(8,128)S(1)}, f32[256,256]{1,0:T(8,128)S(1)}, u32[]{:S(2)}, u32[]{:S(2)}) collective-permute-start(f32[256,256]{1,0:T(8,128)S(1)} %add_add_fusion.1), channel_id=1, source_target_pairs={{0,126},{32,30},{96,94},{64,62},{8,118},{40,22},{104,86},{72,54},{... | collective-permute-start | bytes 786440 | tf_op jit(solution)/shard_map/ppermute | solution.py:164
  58.5 14.7 %collective-permute-start.14 = (f32[512,256]{1,0:T(8,128)S(1)}, f32[512,256]{1,0:T(8,128)S(1)}, u32[]{:S(2)}, u32[]{:S(2)}) collective-permute-start(f32[512,256]{1,0:T(8,128)S(1)} %broadcast_select_fusion.back1_ref), channel_id=1, source_target_pairs={{1,2},{2,3},{3,4},{4,5},{5,6},{6,7},{7,8},{8,9},{9,10},{10,11},{11... | collective-permute-start | bytes 1572872 | tf_op jit(solution)/shard_map/ppermute | solution.py:164

commit v6 on v4

--- a/solution.py
+++ b/solution.py
@@ -18,15 +18,15 @@
 
 TREE = (
     (
-        ((0, 0, -4), (0, 0, -2), (0, 0, 2)),
-        ((-2, 0, 0), (-1, 0, 0), (1, 0, 0)),
-        ((0, 4, 0), (0, -2, 0), (0, 2, 0)),
+        ((0, 0, 2), (0, 0, -2), (0, 0, 4)),
+        ((0, 2, 0), (0, -2, 0), (0, 4, 0)),
+        ((1, 0, 0), (-1, 0, 0), (2, 0, 0)),
         ((0, 1, -1), (0, 1, 0), (0, 0, -1)),
     ),
     (
-        ((0, -4, 0), (0, -2, 0), (0, 2, 0)),
-        ((0, 0, 4), (0, 0, -2), (0, 0, 2)),
-        ((-2, 0, 0), (-1, 0, 0), (1, 0, 0)),
+        ((1, 0, 0), (-1, 0, 0), (2, 0, 0)),
+        ((0, 0, 2), (0, 0, -2), (0, 0, 4)),
+        ((0, 2, 0), (0, -2, 0), (0, 4, 0)),
         ((0, -1, 1), (0, -1, 0), (0, 0, 1)),
     ),
 )
@@ -185,8 +185,8 @@
         out_specs=VMEM,
     )(jnp.reshape(me, (1,)).astype(jnp.int32), *resident(own, second))
 
+    back2 = send(jnp.where(me == 0, own, back1), [(0, 2)] + onward[1:])
     back1 = jnp.where(me == 1, second, back1)
-    back2 = send(back1, onward)
     rounds = tree_rounds()
     for permutes in rounds:
         arrived = [send(held, pairs) for pairs in permutes]

time: 66 us -> 72.4 us (1.097)
  the two profiles are of different devices: /device:TPU:256 before, /device:TPU:2 now
where the time goes in v6:
time: 72.4 us; the launch traced here: 72 us
  starting transfers between devices  41.8 us (58%)
  waiting for transfers between devices  20.8 us (29%)
  Pallas kernels  5.99 us (8%)
  blocking collectives  2.18 us (3%)
  between operations  0.89 us (1%)
    ppermute x15, starting transfers between devices, send(): return lax.ppermute(array, AXIS, pairs)  41.8 us
    ppermute x15, waiting for transfers between devices, send(): return lax.ppermute(array, AXIS, pairs)  20.8 us
    pallas_call x1, Pallas kernels, steps(): pl.pallas_call(apply_kernel, out_shape=[jax.ShapeDtypeStruct((B, B), jnp....  4.92 us
    all_gather x1, blocking collectives, steps(): both = lax.all_gather(held, AXIS, axis=0, axis_index_groups=cores)  2.18 us
  transfers between devices with their start and end apart: 15, of which 4 were waited for; matrix products, arithmetic and copies ran while one was open for 0% of the time, Pallas kernels for 0%

profile of v6, /device:TPU:2, one launch (start us, length us, event | category | flops | bytes accessed | tf_op | source)
XLA Modules:
  0.0 72.0 jit_solution(15184698569224195533)
XLA Ops:
  0.6 1.0 %shard_map.41.own_ref = f32[512,256]{1,0:T(8,128)S(1)} custom-call(f32[256,256]{1,0:T(8,128)} %p_ref.1, f32[256,256]{1,0:T(8,128)} %n_ref.1), custom_call_target="tpu_custom_call" | custom-call | tf_op jit(solution)/shard_map/pallas_call | solution.py:172
  1.7 0.7 collective-permute-start
  2.4 0.0 collective-permute-done.other_ref
  2.4 0.7 collective-permute-start.3
  3.1 0.7 collective-permute-start.2
  3.8 0.7 collective-permute-start.1
  4.5 0.0 collective-permute-done.3
  4.5 0.0 collective-permute-done.2
  4.5 0.1 add_add_fusion.3
  4.6 0.7 collective-permute-start.6
  5.3 0.7 collective-permute-start.5
  6.0 0.7 collective-permute-start.4
  6.7 28.6 %collective-permute-start.13 = (f32[512,256]{1,0:T(8,128)S(1)}, f32[512,256]{1,0:T(8,128)S(1)}, u32[]{:S(2)}, u32[]{:S(2)}) collective-permute-start(f32[512,256]{1,0:T(8,128)S(1)} %shard_map.41.own_ref), channel_id=1, source_target_pairs={{1,2},{2,3},{3,4},{4,5},{5,6},{6,7},{7,8},{8,9},{9,10},{10,11},{11... | collective-permute-start | bytes 1572872 | tf_op jit(solution)/shard_map/ppermute | solution.py:164
  35.2 0.0 collective-permute-done.6
  35.3 0.0 collective-permute-done.5
  35.3 0.1 add_add_fusion.2
  35.4 0.7 collective-permute-start.9
  36.0 0.7 collective-permute-start.8
  36.7 1.3 %collective-permute-start.7 = (f32[256,256]{1,0:T(8,128)S(1)}, f32[256,256]{1,0:T(8,128)S(1)}, u32[]{:S(2)}, u32[]{:S(2)}) collective-permute-start(f32[256,256]{1,0:T(8,128)S(1)} %add_add_fusion.2), channel_id=1, source_target_pairs={{0,128},{4,132},{12,140},{8,136},{32,160},{36,164},{44,172},{40,16... | collective-permute-start | bytes 786440 | tf_op jit(solution)/shard_map/ppermute | solution.py:164
  38.1 10.2 %collective-permute-done.7 = f32[256,256]{1,0:T(8,128)S(1)} collective-permute-done((f32[256,256]{1,0:T(8,128)S(1)}, f32[256,256]{1,0:T(8,128)S(1)}, u32[]{:S(2)}, u32[]{:S(2)}) %collective-permute-start.7) | collective-permute-done | bytes 262176 | tf_op jit(solution)/shard_map/ppermute | solution.py:164
  48.3 0.1 add_add_fusion.1
  48.3 1.3 %collective-permute-start.12 = (f32[256,256]{1,0:T(8,128)S(1)}, f32[256,256]{1,0:T(8,128)S(1)}, u32[]{:S(2)}, u32[]{:S(2)}) collective-permute-start(f32[256,256]{1,0:T(8,128)S(1)} %add_add_fusion.1), channel_id=1, source_target_pairs={{0,14},{4,2},{12,10},{8,6},{32,46},{36,34},{44,42},{40,38},{96,110... | collective-permute-start | bytes 786440 | tf_op jit(solution)/shard_map/ppermute | solution.py:164
  49.6 1.3 %collective-permute-start.11 = (f32[256,256]{1,0:T(8,128)S(1)}, f32[256,256]{1,0:T(8,128)S(1)}, u32[]{:S(2)}, u32[]{:S(2)}) collective-permute-start(f32[256,256]{1,0:T(8,128)S(1)} %add_add_fusion.1), channel_id=1, source_target_pairs={{0,16},{4,20},{12,28},{8,24},{32,48},{36,52},{44,60},{40,56},{96,1... | collective-permute-start | bytes 786440 | tf_op jit(solution)/shard_map/ppermute | solution.py:164
  51.0 1.3 %collective-permute-start.10 = (f32[256,256]{1,0:T(8,128)S(1)}, f32[256,256]{1,0:T(8,128)S(1)}, u32[]{:S(2)}, u32[]{:S(2)}) collective-permute-start(f32[256,256]{1,0:T(8,128)S(1)} %add_add_fusion.1), channel_id=1, source_target_pairs={{0,30},{4,18},{12,26},{8,22},{32,62},{36,50},{44,58},{40,54},{96,1... | collective-permute-start | bytes 786440 | tf_op jit(solution)/shard_map/ppermute | solution.py:164
  52.3 0.1 broadcast_select_fusion
  52.4 1.9 %collective-permute-start.14 = (f32[512,256]{1,0:T(8,128)S(1)}, f32[512,256]{1,0:T(8,128)S(1)}, u32[]{:S(2)}, u32[]{:S(2)}) collective-permute-start(f32[512,256]{1,0:T(8,128)S(1)} %get-tuple-element.3), channel_id=1, source_target_pairs={{0,2},{2,3},{3,4},{4,5},{5,6},{6,7},{7,8},{8,9},{9,10},{10,11},{11... | collective-permute-start | bytes 1572872 | tf_op jit(solution)/shard_map/ppermute | solution.py:164
  54.3 0.5 collective-permute-done.11
  54.8 1.5 %collective-permute-done.10 = f32[256,256]{1,0:T(8,128)S(1)} collective-permute-done((f32[256,256]{1,0:T(8,128)S(1)}, f32[256,256]{1,0:T(8,128)S(1)}, u32[]{:S(2)}, u32[]{:S(2)}) %collective-permute-start.10) | collective-permute-done | bytes 262176 | tf_op jit(solution)/shard_map/ppermute | solution.py:164
  56.3 0.1 add_add_fusion
  56.4 2.2 %all-gather = f32[512,256]{1,0:T(8,128)S(1)} all-gather(f32[256,256]{1,0:T(8,128)S(1)} %add_add_fusion), channel_id=2, replica_groups={{0,1},{2,3},{4,5},{6,7},{8,9},{10,11},{12,13},{14,15},{16,17},{18,19},{..., dimensions={0}, use_global_device_ids=true | all-gather | bytes 786432 | tf_op jit(solution)/shard_map/all_gather | solution.py:196
  58.6 8.5 %collective-permute-done.14.back2_ref = f32[512,256]{1,0:T(8,128)S(1)} collective-permute-done((f32[512,256]{1,0:T(8,128)S(1)}, f32[512,256]{1,0:T(8,128)S(1)}, u32[]{:S(2)}, u32[]{:S(2)}) %collective-permute-start.14) | collective-permute-done | bytes 524320 | tf_op jit(solution)/shard_map/ppermute | solution.py:164
  67.1 4.9 %shard_map.43 = (f32[256,256]{1,0:T(8,128)}, f32[256,256]{1,0:T(8,128)}) custom-call(f32[2,256,256]{2,1,0:T(8,128)S(1)} %bitcast.2, f32[512,256]{1,0:T(8,128)S(1)} %collective-permute-done.14.back2_ref, f32[512,256]{1,0:T(8,128)S(1)} %get-tuple-element.2.back1_ref, f32[512,256]{1,0:T(8,128)S(1)} %shard_map.41.own_ref), custom_call_target="tpu_custom_call" | custom-call | tf_op jit(solution)/shard_map/pallas_call | solution.py:197
  (7 shorter events, 0.0 us)
Async XLA Ops:
  1.7 0.7 collective-permute-start
  2.4 2.1 %collective-permute-start.3 = (f32[256,256]{1,0:T(8,128)S(1)}, f32[256,256]{1,0:T(8,128)S(1)}, u32[]{:S(2)}, u32[]{:S(2)}) collective-permute-start(f32[256,256]{1,0:T(8,128)S(1)} %shard_map.42), channel_id=1, source_target_pairs={{0,8},{1,257}} | collective-permute-start | bytes 786440 | tf_op jit(solution)/shard_map/ppermute | solution.py:164
  3.1 1.4 %collective-permute-start.2 = (f32[256,256]{1,0:T(8,128)S(1)}, f32[256,256]{1,0:T(8,128)S(1)}, u32[]{:S(2)}, u32[]{:S(2)}) collective-permute-start(f32[256,256]{1,0:T(8,128)S(1)} %shard_map.42), channel_id=1, source_target_pairs={{0,12},{1,385}} | collective-permute-start | bytes 786440 | tf_op jit(solution)/shard_map/ppermute | solution.py:164
  3.8 0.7 collective-permute-start.1
  4.6 30.7 %collective-permute-start.6 = (f32[256,256]{1,0:T(8,128)S(1)}, f32[256,256]{1,0:T(8,128)S(1)}, u32[]{:S(2)}, u32[]{:S(2)}) collective-permute-start(f32[256,256]{1,0:T(8,128)S(1)} %add_add_fusion.3), channel_id=1, source_target_pairs={{0,64},{4,68},{12,76},{8,72},{1,9},{129,137},{385,393},{257,265}} | collective-permute-start | bytes 786440 | tf_op jit(solution)/shard_map/ppermute | solution.py:164
  5.3 30.0 %collective-permute-start.5 = (f32[256,256]{1,0:T(8,128)S(1)}, f32[256,256]{1,0:T(8,128)S(1)}, u32[]{:S(2)}, u32[]{:S(2)}) collective-permute-start(f32[256,256]{1,0:T(8,128)S(1)} %add_add_fusion.3), channel_id=1, source_target_pairs={{0,96},{4,100},{12,108},{8,104},{1,13},{129,141},{385,397},{257,269}} | collective-permute-start | bytes 786440 | tf_op jit(solution)/shard_map/ppermute | solution.py:164
  6.0 29.3 %collective-permute-start.4 = (f32[256,256]{1,0:T(8,128)S(1)}, f32[256,256]{1,0:T(8,128)S(1)}, u32[]{:S(2)}, u32[]{:S(2)}) collective-permute-start(f32[256,256]{1,0:T(8,128)S(1)} %add_add_fusion.3), channel_id=1, source_target_pairs={{0,32},{4,36},{12,44},{8,40},{1,5},{129,133},{385,389},{257,261}} | collective-permute-start | bytes 786440 | tf_op jit(solution)/shard_map/ppermute | solution.py:164
  6.7 45.6 %collective-permute-start.13 = (f32[512,256]{1,0:T(8,128)S(1)}, f32[512,256]{1,0:T(8,128)S(1)}, u32[]{:S(2)}, u32[]{:S(2)}) collective-permute-start(f32[512,256]{1,0:T(8,128)S(1)} %shard_map.41.own_ref), channel_id=1, source_target_pairs={{1,2},{2,3},{3,4},{4,5},{5,6},{6,7},{7,8},{8,9},{9,10},{10,11},{11... | collective-permute-start | bytes 1572872 | tf_op jit(solution)/shard_map/ppermute | solution.py:164
  35.4 2.7 %collective-permute-start.9 = (f32[256,256]{1,0:T(8,128)S(1)}, f32[256,256]{1,0:T(8,128)S(1)}, u32[]{:S(2)}, u32[]{:S(2)}) collective-permute-start(f32[256,256]{1,0:T(8,128)S(1)} %add_add_fusion.2), channel_id=1, source_target_pairs={{0,256},{4,260},{12,268},{8,264},{32,288},{36,292},{44,300},{40,29... | collective-permute-start | bytes 786440 | tf_op jit(solution)/shard_map/ppermute | solution.py:164
  36.0 2.0 %collective-permute-start.8 = (f32[256,256]{1,0:T(8,128)S(1)}, f32[256,256]{1,0:T(8,128)S(1)}, u32[]{:S(2)}, u32[]{:S(2)}) collective-permute-start(f32[256,256]{1,0:T(8,128)S(1)} %add_add_fusion.2), channel_id=1, source_target_pairs={{0,384},{4,388},{12,396},{8,392},{32,416},{36,420},{44,428},{40,42... | collective-permute-start | bytes 786440 | tf_op jit(solution)/shard_map/ppermute | solution.py:164
  36.7 11.5 %collective-permute-start.7 = (f32[256,256]{1,0:T(8,128)S(1)}, f32[256,256]{1,0:T(8,128)S(1)}, u32[]{:S(2)}, u32[]{:S(2)}) collective-permute-start(f32[256,256]{1,0:T(8,128)S(1)} %add_add_fusion.2), channel_id=1, source_target_pairs={{0,128},{4,132},{12,140},{8,136},{32,160},{36,164},{44,172},{40,16... | collective-permute-start | bytes 786440 | tf_op jit(solution)/shard_map/ppermute | solution.py:164
  48.3 6.0 %collective-permute-start.12 = (f32[256,256]{1,0:T(8,128)S(1)}, f32[256,256]{1,0:T(8,128)S(1)}, u32[]{:S(2)}, u32[]{:S(2)}) collective-permute-start(f32[256,256]{1,0:T(8,128)S(1)} %add_add_fusion.1), channel_id=1, source_target_pairs={{0,14},{4,2},{12,10},{8,6},{32,46},{36,34},{44,42},{40,38},{96,110... | collective-permute-start | bytes 786440 | tf_op jit(solution)/shard_map/ppermute | solution.py:164
  49.6 5.2 %collective-permute-start.11 = (f32[256,256]{1,0:T(8,128)S(1)}, f32[256,256]{1,0:T(8,128)S(1)}, u32[]{:S(2)}, u32[]{:S(2)}) collective-permute-start(f32[256,256]{1,0:T(8,128)S(1)} %add_add_fusion.1), channel_id=1, source_target_pairs={{0,16},{4,20},{12,28},{8,24},{32,48},{36,52},{44,60},{40,56},{96,1... | collective-permute-start | bytes 786440 | tf_op jit(solution)/shard_map/ppermute | solution.py:164
  51.0 5.4 %collective-permute-start.10 = (f32[256,256]{1,0:T(8,128)S(1)}, f32[256,256]{1,0:T(8,128)S(1)}, u32[]{:S(2)}, u32[]{:S(2)}) collective-permute-start(f32[256,256]{1,0:T(8,128)S(1)} %add_add_fusion.1), channel_id=1, source_target_pairs={{0,30},{4,18},{12,26},{8,22},{32,62},{36,50},{44,58},{40,54},{96,1... | collective-permute-start | bytes 786440 | tf_op jit(solution)/shard_map/ppermute | solution.py:164
  52.4 14.7 %collective-permute-start.14 = (f32[512,256]{1,0:T(8,128)S(1)}, f32[512,256]{1,0:T(8,128)S(1)}, u32[]{:S(2)}, u32[]{:S(2)}) collective-permute-start(f32[512,256]{1,0:T(8,128)S(1)} %get-tuple-element.3), channel_id=1, source_target_pairs={{0,2},{2,3},{3,4},{4,5},{5,6},{6,7},{7,8},{8,9},{9,10},{10,11},{11... | collective-permute-start | bytes 1572872 | tf_op jit(solution)/shard_map/ppermute | solution.py:164

commit v7 on v6

--- a/solution.py
+++ b/solution.py
@@ -18,16 +18,16 @@
 
 TREE = (
     (
+        ((2, 0, 0), (-1, 0, 0), (1, 0, 0)),
+        ((0, 0, 2), (0, 0, -2), (0, 0, 4)),
+        ((0, 2, 0), (0, -2, 0), (0, 4, 0)),
+        ((0, 0, 1), (0, -1, 0), (0, -1, 1)),
+    ),
+    (
         ((0, 0, 2), (0, 0, -2), (0, 0, 4)),
         ((0, 2, 0), (0, -2, 0), (0, 4, 0)),
         ((1, 0, 0), (-1, 0, 0), (2, 0, 0)),
-        ((0, 1, -1), (0, 1, 0), (0, 0, -1)),
-    ),
-    (
-        ((1, 0, 0), (-1, 0, 0), (2, 0, 0)),
-        ((0, 0, 2), (0, 0, -2), (0, 0, 4)),
-        ((0, 2, 0), (0, -2, 0), (0, 4, 0)),
-        ((0, -1, 1), (0, -1, 0), (0, 0, 1)),
+        ((0, 0, -1), (0, 1, 0), (0, 1, -1)),
     ),
 )
 
@@ -60,9 +60,10 @@
 
 
 def dot(a, b):
-    left = jnp.concatenate([a[0], a[0], a[1]], axis=1)
-    right = jnp.concatenate([b[0], b[1], b[0]], axis=0)
-    return jnp.dot(left, right, preferred_element_type=jnp.float32)
+    rows = a[0].shape[0]
+    both = jnp.dot(jnp.concatenate([a[0], a[1]], axis=0), b[0], preferred_element_type=jnp.float32)
+    cross = jnp.dot(a[0], b[1], preferred_element_type=jnp.float32)
+    return both[:rows] + (both[rows:] + cross)
 
 
 def eye():

time: 72.4 us -> 66.6 us (0.920)
  the two profiles are of different devices: /device:TPU:2 before, /device:TPU:10 now
where the time goes in v7:
time: 66.6 us; the launch traced here: 66.2 us
  waiting for transfers between devices  43.5 us (65%)
  starting transfers between devices  13.3 us (20%)
  Pallas kernels  5.99 us (9%)
  blocking collectives  2.18 us (3%)
  between operations  0.9 us (1%)
    ppermute x15, waiting for transfers between devices, send(): return lax.ppermute(array, AXIS, pairs)  43.5 us
    ppermute x15, starting transfers between devices, send(): return lax.ppermute(array, AXIS, pairs)  13.3 us
    pallas_call x1, Pallas kernels, steps(): pl.pallas_call(apply_kernel, out_shape=[jax.ShapeDtypeStruct((B, B), jnp....  4.91 us
    all_gather x1, blocking collectives, steps(): both = lax.all_gather(held, AXIS, axis=0, axis_index_groups=cores)  2.18 us
  transfers between devices with their start and end apart: 15, of which 3 were waited for; matrix products, arithmetic and copies ran while one was open for 0% of the time, Pallas kernels for 0%

profile of v7, /device:TPU:10, one launch (start us, length us, event | category | flops | bytes accessed | tf_op | source)
XLA Modules:
  0.0 66.2 jit_solution(18137012158785238230)
XLA Ops:
  0.6 1.0 %shard_map.41.own_ref = f32[512,256]{1,0:T(8,128)S(1)} custom-call(f32[256,256]{1,0:T(8,128)} %p_ref.1, f32[256,256]{1,0:T(8,128)} %n_ref.1), custom_call_target="tpu_custom_call" | custom-call | tf_op jit(solution)/shard_map/pallas_call | solution.py:173
  1.7 0.7 %collective-permute-start = (f32[512,256]{1,0:T(8,128)S(1)}, f32[512,256]{1,0:T(8,128)S(1)}, u32[]{:S(2)}, u32[]{:S(2)}) collective-permute-start(f32[512,256]{1,0:T(8,128)S(1)} %shard_map.41.own_ref), channel_id=1, source_target_pairs={{0,1},{1,0}} | collective-permute-start | bytes 1572872 | tf_op jit(solution)/shard_map/ppermute | solution.py:165
  2.4 0.0 collective-permute-done.other_ref
  2.4 0.7 %collective-permute-start.3 = (f32[256,256]{1,0:T(8,128)S(1)}, f32[256,256]{1,0:T(8,128)S(1)}, u32[]{:S(2)}, u32[]{:S(2)}) collective-permute-start(f32[256,256]{1,0:T(8,128)S(1)} %shard_map.42), channel_id=1, source_target_pairs={{0,128},{1,9}} | collective-permute-start | bytes 786440 | tf_op jit(solution)/shard_map/ppermute | solution.py:165
  3.1 0.7 %collective-permute-start.2 = (f32[256,256]{1,0:T(8,128)S(1)}, f32[256,256]{1,0:T(8,128)S(1)}, u32[]{:S(2)}, u32[]{:S(2)}) collective-permute-start(f32[256,256]{1,0:T(8,128)S(1)} %shard_map.42), channel_id=1, source_target_pairs={{0,384},{1,13}} | collective-permute-start | bytes 786440 | tf_op jit(solution)/shard_map/ppermute | solution.py:165
  3.8 0.7 %collective-permute-start.1 = (f32[256,256]{1,0:T(8,128)S(1)}, f32[256,256]{1,0:T(8,128)S(1)}, u32[]{:S(2)}, u32[]{:S(2)}) collective-permute-start(f32[256,256]{1,0:T(8,128)S(1)} %shard_map.42), channel_id=1, source_target_pairs={{0,256},{1,5}} | collective-permute-start | bytes 786440 | tf_op jit(solution)/shard_map/ppermute | solution.py:165
  4.5 0.0 collective-permute-done.2
  4.5 0.1 add_add_fusion.3
  4.6 0.7 %collective-permute-start.6 = (f32[256,256]{1,0:T(8,128)S(1)}, f32[256,256]{1,0:T(8,128)S(1)}, u32[]{:S(2)}, u32[]{:S(2)}) collective-permute-start(f32[256,256]{1,0:T(8,128)S(1)} %add_add_fusion.3), channel_id=1, source_target_pairs={{0,8},{256,264},{384,392},{128,136},{1,65},{5,69},{13,77},{9,73}} | collective-permute-start | bytes 786440 | tf_op jit(solution)/shard_map/ppermute | solution.py:165
  5.3 0.7 %collective-permute-start.5 = (f32[256,256]{1,0:T(8,128)S(1)}, f32[256,256]{1,0:T(8,128)S(1)}, u32[]{:S(2)}, u32[]{:S(2)}) collective-permute-start(f32[256,256]{1,0:T(8,128)S(1)} %add_add_fusion.3), channel_id=1, source_target_pairs={{0,12},{256,268},{384,396},{128,140},{1,97},{5,101},{13,109},{9,105}} | collective-permute-start | bytes 786440 | tf_op jit(solution)/shard_map/ppermute | solution.py:165
  6.0 0.7 %collective-permute-start.4 = (f32[256,256]{1,0:T(8,128)S(1)}, f32[256,256]{1,0:T(8,128)S(1)}, u32[]{:S(2)}, u32[]{:S(2)}) collective-permute-start(f32[256,256]{1,0:T(8,128)S(1)} %add_add_fusion.3), channel_id=1, source_target_pairs={{0,4},{256,260},{384,388},{128,132},{1,33},{5,37},{13,45},{9,41}} | collective-permute-start | bytes 786440 | tf_op jit(solution)/shard_map/ppermute | solution.py:165
  6.7 1.9 %collective-permute-start.13 = (f32[512,256]{1,0:T(8,128)S(1)}, f32[512,256]{1,0:T(8,128)S(1)}, u32[]{:S(2)}, u32[]{:S(2)}) collective-permute-start(f32[512,256]{1,0:T(8,128)S(1)} %shard_map.41.own_ref), channel_id=1, source_target_pairs={{1,2},{2,3},{3,4},{4,5},{5,6},{6,7},{7,8},{8,9},{9,10},{10,11},{11... | collective-permute-start | bytes 1572872 | tf_op jit(solution)/shard_map/ppermute | solution.py:165
  8.6 0.0 collective-permute-done.5
  8.6 0.0 collective-permute-done.4
  8.6 0.1 add_add_fusion.2
  8.7 0.7 %collective-permute-start.9 = (f32[256,256]{1,0:T(8,128)S(1)}, f32[256,256]{1,0:T(8,128)S(1)}, u32[]{:S(2)}, u32[]{:S(2)}) collective-permute-start(f32[256,256]{1,0:T(8,128)S(1)} %add_add_fusion.2), channel_id=1, source_target_pairs={{0,64},{256,320},{384,448},{128,192},{4,68},{260,324},{388,452},{1... | collective-permute-start | bytes 786440 | tf_op jit(solution)/shard_map/ppermute | solution.py:165
  9.4 0.7 %collective-permute-start.8 = (f32[256,256]{1,0:T(8,128)S(1)}, f32[256,256]{1,0:T(8,128)S(1)}, u32[]{:S(2)}, u32[]{:S(2)}) collective-permute-start(f32[256,256]{1,0:T(8,128)S(1)} %add_add_fusion.2), channel_id=1, source_target_pairs={{0,96},{256,352},{384,480},{128,224},{4,100},{260,356},{388,484},{... | collective-permute-start | bytes 786440 | tf_op jit(solution)/shard_map/ppermute | solution.py:165
  10.1 0.7 %collective-permute-start.7 = (f32[256,256]{1,0:T(8,128)S(1)}, f32[256,256]{1,0:T(8,128)S(1)}, u32[]{:S(2)}, u32[]{:S(2)}) collective-permute-start(f32[256,256]{1,0:T(8,128)S(1)} %add_add_fusion.2), channel_id=1, source_target_pairs={{0,32},{256,288},{384,416},{128,160},{4,36},{260,292},{388,420},{1... | collective-permute-start | bytes 786440 | tf_op jit(solution)/shard_map/ppermute | solution.py:165
  10.8 0.0 collective-permute-done.9
  10.8 0.0 collective-permute-done.8
  10.8 0.1 add_add_fusion.1
  10.9 0.7 %collective-permute-start.12 = (f32[256,256]{1,0:T(8,128)S(1)}, f32[256,256]{1,0:T(8,128)S(1)}, u32[]{:S(2)}, u32[]{:S(2)}) collective-permute-start(f32[256,256]{1,0:T(8,128)S(1)} %add_add_fusion.1), channel_id=1, source_target_pairs={{0,114},{256,370},{384,498},{128,242},{4,118},{260,374},{388,502},... | collective-permute-start | bytes 786440 | tf_op jit(solution)/shard_map/ppermute | solution.py:165
  11.5 0.7 %collective-permute-start.11 = (f32[256,256]{1,0:T(8,128)S(1)}, f32[256,256]{1,0:T(8,128)S(1)}, u32[]{:S(2)}, u32[]{:S(2)}) collective-permute-start(f32[256,256]{1,0:T(8,128)S(1)} %add_add_fusion.1), channel_id=1, source_target_pairs={{0,112},{256,368},{384,496},{128,240},{4,116},{260,372},{388,500},... | collective-permute-start | bytes 786440 | tf_op jit(solution)/shard_map/ppermute | solution.py:165
  12.2 1.3 %collective-permute-start.10 = (f32[256,256]{1,0:T(8,128)S(1)}, f32[256,256]{1,0:T(8,128)S(1)}, u32[]{:S(2)}, u32[]{:S(2)}) collective-permute-start(f32[256,256]{1,0:T(8,128)S(1)} %add_add_fusion.1), channel_id=1, source_target_pairs={{0,2},{256,258},{384,386},{128,130},{4,6},{260,262},{388,390},{132... | collective-permute-start | bytes 786440 | tf_op jit(solution)/shard_map/ppermute | solution.py:165
  13.5 3.6 %collective-permute-done.13 = f32[512,256]{1,0:T(8,128)S(1)} collective-permute-done((f32[512,256]{1,0:T(8,128)S(1)}, f32[512,256]{1,0:T(8,128)S(1)}, u32[]{:S(2)}, u32[]{:S(2)}) %collective-permute-start.13) | collective-permute-done | bytes 524320 | tf_op jit(solution)/shard_map/ppermute | solution.py:165
  17.2 0.1 broadcast_select_fusion
  17.3 1.9 %collective-permute-start.14 = (f32[512,256]{1,0:T(8,128)S(1)}, f32[512,256]{1,0:T(8,128)S(1)}, u32[]{:S(2)}, u32[]{:S(2)}) collective-permute-start(f32[512,256]{1,0:T(8,128)S(1)} %get-tuple-element.3), channel_id=1, source_target_pairs={{0,2},{2,3},{3,4},{4,5},{5,6},{6,7},{7,8},{8,9},{9,10},{10,11},{11... | collective-permute-start | bytes 1572872 | tf_op jit(solution)/shard_map/ppermute | solution.py:165
  19.2 28.9 %collective-permute-done.10 = f32[256,256]{1,0:T(8,128)S(1)} collective-permute-done((f32[256,256]{1,0:T(8,128)S(1)}, f32[256,256]{1,0:T(8,128)S(1)}, u32[]{:S(2)}, u32[]{:S(2)}) %collective-permute-start.10) | collective-permute-done | bytes 262176 | tf_op jit(solution)/shard_map/ppermute | solution.py:165
  48.2 0.1 add_add_fusion
  48.2 2.2 %all-gather = f32[512,256]{1,0:T(8,128)S(1)} all-gather(f32[256,256]{1,0:T(8,128)S(1)} %add_add_fusion), channel_id=2, replica_groups={{0,1},{2,3},{4,5},{6,7},{8,9},{10,11},{12,13},{14,15},{16,17},{18,19},{..., dimensions={0}, use_global_device_ids=true | all-gather | bytes 786432 | tf_op jit(solution)/shard_map/all_gather | solution.py:197
  50.4 10.9 %collective-permute-done.14.back2_ref = f32[512,256]{1,0:T(8,128)S(1)} collective-permute-done((f32[512,256]{1,0:T(8,128)S(1)}, f32[512,256]{1,0:T(8,128)S(1)}, u32[]{:S(2)}, u32[]{:S(2)}) %collective-permute-start.14) | collective-permute-done | bytes 524320 | tf_op jit(solution)/shard_map/ppermute | solution.py:165
  61.3 4.9 %shard_map.43 = (f32[256,256]{1,0:T(8,128)}, f32[256,256]{1,0:T(8,128)}) custom-call(f32[2,256,256]{2,1,0:T(8,128)S(1)} %bitcast.2, f32[512,256]{1,0:T(8,128)S(1)} %collective-permute-done.14.back2_ref, f32[512,256]{1,0:T(8,128)S(1)} %get-tuple-element.2.back1_ref, f32[512,256]{1,0:T(8,128)S(1)} %shard_map.41.own_ref), custom_call_target="tpu_custom_call" | custom-call | tf_op jit(solution)/shard_map/pallas_call | solution.py:198
  (7 shorter events, 0.0 us)
Async XLA Ops:
  1.7 0.7 %collective-permute-start = (f32[512,256]{1,0:T(8,128)S(1)}, f32[512,256]{1,0:T(8,128)S(1)}, u32[]{:S(2)}, u32[]{:S(2)}) collective-permute-start(f32[512,256]{1,0:T(8,128)S(1)} %shard_map.41.own_ref), channel_id=1, source_target_pairs={{0,1},{1,0}} | collective-permute-start | bytes 1572872 | tf_op jit(solution)/shard_map/ppermute | solution.py:165
  2.4 2.1 %collective-permute-start.3 = (f32[256,256]{1,0:T(8,128)S(1)}, f32[256,256]{1,0:T(8,128)S(1)}, u32[]{:S(2)}, u32[]{:S(2)}) collective-permute-start(f32[256,256]{1,0:T(8,128)S(1)} %shard_map.42), channel_id=1, source_target_pairs={{0,128},{1,9}} | collective-permute-start | bytes 786440 | tf_op jit(solution)/shard_map/ppermute | solution.py:165
  3.1 1.4 %collective-permute-start.2 = (f32[256,256]{1,0:T(8,128)S(1)}, f32[256,256]{1,0:T(8,128)S(1)}, u32[]{:S(2)}, u32[]{:S(2)}) collective-permute-start(f32[256,256]{1,0:T(8,128)S(1)} %shard_map.42), channel_id=1, source_target_pairs={{0,384},{1,13}} | collective-permute-start | bytes 786440 | tf_op jit(solution)/shard_map/ppermute | solution.py:165
  3.8 0.7 %collective-permute-start.1 = (f32[256,256]{1,0:T(8,128)S(1)}, f32[256,256]{1,0:T(8,128)S(1)}, u32[]{:S(2)}, u32[]{:S(2)}) collective-permute-start(f32[256,256]{1,0:T(8,128)S(1)} %shard_map.42), channel_id=1, source_target_pairs={{0,256},{1,5}} | collective-permute-start | bytes 786440 | tf_op jit(solution)/shard_map/ppermute | solution.py:165
  4.6 4.0 %collective-permute-start.6 = (f32[256,256]{1,0:T(8,128)S(1)}, f32[256,256]{1,0:T(8,128)S(1)}, u32[]{:S(2)}, u32[]{:S(2)}) collective-permute-start(f32[256,256]{1,0:T(8,128)S(1)} %add_add_fusion.3), channel_id=1, source_target_pairs={{0,8},{256,264},{384,392},{128,136},{1,65},{5,69},{13,77},{9,73}} | collective-permute-start | bytes 786440 | tf_op jit(solution)/shard_map/ppermute | solution.py:165
  5.3 3.3 %collective-permute-start.5 = (f32[256,256]{1,0:T(8,128)S(1)}, f32[256,256]{1,0:T(8,128)S(1)}, u32[]{:S(2)}, u32[]{:S(2)}) collective-permute-start(f32[256,256]{1,0:T(8,128)S(1)} %add_add_fusion.3), channel_id=1, source_target_pairs={{0,12},{256,268},{384,396},{128,140},{1,97},{5,101},{13,109},{9,105}} | collective-permute-start | bytes 786440 | tf_op jit(solution)/shard_map/ppermute | solution.py:165
  6.0 2.6 %collective-permute-start.4 = (f32[256,256]{1,0:T(8,128)S(1)}, f32[256,256]{1,0:T(8,128)S(1)}, u32[]{:S(2)}, u32[]{:S(2)}) collective-permute-start(f32[256,256]{1,0:T(8,128)S(1)} %add_add_fusion.3), channel_id=1, source_target_pairs={{0,4},{256,260},{384,388},{128,132},{1,33},{5,37},{13,45},{9,41}} | collective-permute-start | bytes 786440 | tf_op jit(solution)/shard_map/ppermute | solution.py:165
  6.7 10.5 %collective-permute-start.13 = (f32[512,256]{1,0:T(8,128)S(1)}, f32[512,256]{1,0:T(8,128)S(1)}, u32[]{:S(2)}, u32[]{:S(2)}) collective-permute-start(f32[512,256]{1,0:T(8,128)S(1)} %shard_map.41.own_ref), channel_id=1, source_target_pairs={{1,2},{2,3},{3,4},{4,5},{5,6},{6,7},{7,8},{8,9},{9,10},{10,11},{11... | collective-permute-start | bytes 1572872 | tf_op jit(solution)/shard_map/ppermute | solution.py:165
  8.7 2.1 %collective-permute-start.9 = (f32[256,256]{1,0:T(8,128)S(1)}, f32[256,256]{1,0:T(8,128)S(1)}, u32[]{:S(2)}, u32[]{:S(2)}) collective-permute-start(f32[256,256]{1,0:T(8,128)S(1)} %add_add_fusion.2), channel_id=1, source_target_pairs={{0,64},{256,320},{384,448},{128,192},{4,68},{260,324},{388,452},{1... | collective-permute-start | bytes 786440 | tf_op jit(solution)/shard_map/ppermute | solution.py:165
  9.4 1.4 %collective-permute-start.8 = (f32[256,256]{1,0:T(8,128)S(1)}, f32[256,256]{1,0:T(8,128)S(1)}, u32[]{:S(2)}, u32[]{:S(2)}) collective-permute-start(f32[256,256]{1,0:T(8,128)S(1)} %add_add_fusion.2), channel_id=1, source_target_pairs={{0,96},{256,352},{384,480},{128,224},{4,100},{260,356},{388,484},{... | collective-permute-start | bytes 786440 | tf_op jit(solution)/shard_map/ppermute | solution.py:165
  10.1 0.7 %collective-permute-start.7 = (f32[256,256]{1,0:T(8,128)S(1)}, f32[256,256]{1,0:T(8,128)S(1)}, u32[]{:S(2)}, u32[]{:S(2)}) collective-permute-start(f32[256,256]{1,0:T(8,128)S(1)} %add_add_fusion.2), channel_id=1, source_target_pairs={{0,32},{256,288},{384,416},{128,160},{4,36},{260,292},{388,420},{1... | collective-permute-start | bytes 786440 | tf_op jit(solution)/shard_map/ppermute | solution.py:165
  10.9 8.3 %collective-permute-start.12 = (f32[256,256]{1,0:T(8,128)S(1)}, f32[256,256]{1,0:T(8,128)S(1)}, u32[]{:S(2)}, u32[]{:S(2)}) collective-permute-start(f32[256,256]{1,0:T(8,128)S(1)} %add_add_fusion.1), channel_id=1, source_target_pairs={{0,114},{256,370},{384,498},{128,242},{4,118},{260,374},{388,502},... | collective-permute-start | bytes 786440 | tf_op jit(solution)/shard_map/ppermute | solution.py:165
  11.5 7.7 %collective-permute-start.11 = (f32[256,256]{1,0:T(8,128)S(1)}, f32[256,256]{1,0:T(8,128)S(1)}, u32[]{:S(2)}, u32[]{:S(2)}) collective-permute-start(f32[256,256]{1,0:T(8,128)S(1)} %add_add_fusion.1), channel_id=1, source_target_pairs={{0,112},{256,368},{384,496},{128,240},{4,116},{260,372},{388,500},... | collective-permute-start | bytes 786440 | tf_op jit(solution)/shard_map/ppermute | solution.py:165
  12.2 35.9 %collective-permute-start.10 = (f32[256,256]{1,0:T(8,128)S(1)}, f32[256,256]{1,0:T(8,128)S(1)}, u32[]{:S(2)}, u32[]{:S(2)}) collective-permute-start(f32[256,256]{1,0:T(8,128)S(1)} %add_add_fusion.1), channel_id=1, source_target_pairs={{0,2},{256,258},{384,386},{128,130},{4,6},{260,262},{388,390},{132... | collective-permute-start | bytes 786440 | tf_op jit(solution)/shard_map/ppermute | solution.py:165
  17.3 44.0 %collective-permute-start.14 = (f32[512,256]{1,0:T(8,128)S(1)}, f32[512,256]{1,0:T(8,128)S(1)}, u32[]{:S(2)}, u32[]{:S(2)}) collective-permute-start(f32[512,256]{1,0:T(8,128)S(1)} %get-tuple-element.3), channel_id=1, source_target_pairs={{0,2},{2,3},{3,4},{4,5},{5,6},{6,7},{7,8},{8,9},{9,10},{10,11},{11... | collective-permute-start | bytes 1572872 | tf_op jit(solution)/shard_map/ppermute | solution.py:165

commit v8 on v7

--- a/solution.py
+++ b/solution.py
@@ -18,16 +18,16 @@
 
 TREE = (
     (
+        ((0, 0, 2), (0, 0, -2), (0, 0, 4)),
+        ((1, 0, 0), (2, 0, 0), (-1, 0, 0)),
+        ((0, 4, 0), (0, 0, -1), (0, 4, -1)),
+        ((0, 1, 0), (0, 2, 0), (0, -1, 0)),
+    ),
+    (
         ((2, 0, 0), (-1, 0, 0), (1, 0, 0)),
         ((0, 0, 2), (0, 0, -2), (0, 0, 4)),
-        ((0, 2, 0), (0, -2, 0), (0, 4, 0)),
+        ((0, -2, 0), (0, 2, 0), (0, 4, 0)),
         ((0, 0, 1), (0, -1, 0), (0, -1, 1)),
-    ),
-    (
-        ((0, 0, 2), (0, 0, -2), (0, 0, 4)),
-        ((0, 2, 0), (0, -2, 0), (0, 4, 0)),
-        ((1, 0, 0), (-1, 0, 0), (2, 0, 0)),
-        ((0, 0, -1), (0, 1, 0), (0, 1, -1)),
     ),
 )
 

time: 66.6 us -> 71.8 us (1.078)
  the two profiles are of different devices: /device:TPU:10 before, /device:TPU:4 now
where the time goes in v8:
time: 71.8 us; the launch traced here: 71.4 us
  starting transfers between devices  45.8 us (64%)
  waiting for transfers between devices  16.1 us (22%)
  Pallas kernels  5.99 us (8%)
  blocking collectives  2.18 us (3%)
  between operations  0.89 us (1%)
    ppermute x15, starting transfers between devices, send(): return lax.ppermute(array, AXIS, pairs)  45.8 us
    ppermute x15, waiting for transfers between devices, send(): return lax.ppermute(array, AXIS, pairs)  16.1 us
    pallas_call x1, Pallas kernels, steps(): pl.pallas_call(apply_kernel, out_shape=[jax.ShapeDtypeStruct((B, B), jnp....  4.91 us
    all_gather x1, blocking collectives, steps(): both = lax.all_gather(held, AXIS, axis=0, axis_index_groups=cores)  2.18 us
  transfers between devices with their start and end apart: 15, of which 5 were waited for; matrix products, arithmetic and copies ran while one was open for 0% of the time, Pallas kernels for 0%

profile of v8, /device:TPU:4, one launch (start us, length us, event | category | flops | bytes accessed | tf_op | source)
XLA Modules:
  0.0 71.4 jit_solution(15971090969715907342)
XLA Ops:
  0.6 1.0 %shard_map.41.own_ref = f32[512,256]{1,0:T(8,128)S(1)} custom-call(f32[256,256]{1,0:T(8,128)} %p_ref.1, f32[256,256]{1,0:T(8,128)} %n_ref.1), custom_call_target="tpu_custom_call" | custom-call | tf_op jit(solution)/shard_map/pallas_call | solution.py:173
  1.7 0.7 collective-permute-start
  2.4 0.0 collective-permute-done.other_ref
  2.4 0.7 collective-permute-start.3
  3.1 0.7 collective-permute-start.2
  3.8 0.7 collective-permute-start.1
  4.5 0.0 collective-permute-done.2
  4.5 0.0 collective-permute-done.1
  4.5 0.1 add_add_fusion.3
  4.6 0.7 collective-permute-start.6
  5.3 1.3 %collective-permute-start.5 = (f32[256,256]{1,0:T(8,128)S(1)}, f32[256,256]{1,0:T(8,128)S(1)}, u32[]{:S(2)}, u32[]{:S(2)}) collective-permute-start(f32[256,256]{1,0:T(8,128)S(1)} %add_add_fusion.3), channel_id=1, source_target_pairs={{0,256},{4,260},{12,268},{8,264},{1,13},{257,269},{385,397},{129,1... | collective-permute-start | bytes 786440 | tf_op jit(solution)/shard_map/ppermute | solution.py:165
  6.6 0.7 collective-permute-start.4
  7.3 29.6 %collective-permute-start.13 = (f32[512,256]{1,0:T(8,128)S(1)}, f32[512,256]{1,0:T(8,128)S(1)}, u32[]{:S(2)}, u32[]{:S(2)}) collective-permute-start(f32[512,256]{1,0:T(8,128)S(1)} %shard_map.41.own_ref), channel_id=1, source_target_pairs={{1,2},{2,3},{3,4},{4,5},{5,6},{6,7},{7,8},{8,9},{9,10},{10,11},{11... | collective-permute-start | bytes 1572872 | tf_op jit(solution)/shard_map/ppermute | solution.py:165
  36.9 0.0 collective-permute-done.4
  36.9 0.1 add_add_fusion.2
  37.0 1.3 %collective-permute-start.9 = (f32[256,256]{1,0:T(8,128)S(1)}, f32[256,256]{1,0:T(8,128)S(1)}, u32[]{:S(2)}, u32[]{:S(2)}) collective-permute-start(f32[256,256]{1,0:T(8,128)S(1)} %add_add_fusion.2), channel_id=1, source_target_pairs={{0,78},{4,66},{12,74},{8,70},{128,206},{132,194},{140,202},{136,19... | collective-permute-start | bytes 786440 | tf_op jit(solution)/shard_map/ppermute | solution.py:165
  38.3 1.3 %collective-permute-start.8 = (f32[256,256]{1,0:T(8,128)S(1)}, f32[256,256]{1,0:T(8,128)S(1)}, u32[]{:S(2)}, u32[]{:S(2)}) collective-permute-start(f32[256,256]{1,0:T(8,128)S(1)} %add_add_fusion.2), channel_id=1, source_target_pairs={{0,14},{4,2},{12,10},{8,6},{128,142},{132,130},{140,138},{136,134}... | collective-permute-start | bytes 786440 | tf_op jit(solution)/shard_map/ppermute | solution.py:165
  39.6 1.3 %collective-permute-start.7 = (f32[256,256]{1,0:T(8,128)S(1)}, f32[256,256]{1,0:T(8,128)S(1)}, u32[]{:S(2)}, u32[]{:S(2)}) collective-permute-start(f32[256,256]{1,0:T(8,128)S(1)} %add_add_fusion.2), channel_id=1, source_target_pairs={{0,64},{4,68},{12,76},{8,72},{128,192},{132,196},{140,204},{136,20... | collective-permute-start | bytes 786440 | tf_op jit(solution)/shard_map/ppermute | solution.py:165
  40.9 1.2 %collective-permute-done.9 = f32[256,256]{1,0:T(8,128)S(1)} collective-permute-done((f32[256,256]{1,0:T(8,128)S(1)}, f32[256,256]{1,0:T(8,128)S(1)}, u32[]{:S(2)}, u32[]{:S(2)}) %collective-permute-start.9) | collective-permute-done | bytes 262176 | tf_op jit(solution)/shard_map/ppermute | solution.py:165
  42.2 2.8 %collective-permute-done.8 = f32[256,256]{1,0:T(8,128)S(1)} collective-permute-done((f32[256,256]{1,0:T(8,128)S(1)}, f32[256,256]{1,0:T(8,128)S(1)}, u32[]{:S(2)}, u32[]{:S(2)}) %collective-permute-start.8) | collective-permute-done | bytes 262176 | tf_op jit(solution)/shard_map/ppermute | solution.py:165
  45.0 2.6 %collective-permute-done.7 = f32[256,256]{1,0:T(8,128)S(1)} collective-permute-done((f32[256,256]{1,0:T(8,128)S(1)}, f32[256,256]{1,0:T(8,128)S(1)}, u32[]{:S(2)}, u32[]{:S(2)}) %collective-permute-start.7) | collective-permute-done | bytes 262176 | tf_op jit(solution)/shard_map/ppermute | solution.py:165
  47.6 0.1 add_add_fusion.1
  47.7 1.3 %collective-permute-start.12 = (f32[256,256]{1,0:T(8,128)S(1)}, f32[256,256]{1,0:T(8,128)S(1)}, u32[]{:S(2)}, u32[]{:S(2)}) collective-permute-start(f32[256,256]{1,0:T(8,128)S(1)} %add_add_fusion.1), channel_id=1, source_target_pairs={{0,112},{4,116},{12,124},{8,120},{128,240},{132,244},{140,252},{13... | collective-permute-start | bytes 786440 | tf_op jit(solution)/shard_map/ppermute | solution.py:165
  49.0 1.3 %collective-permute-start.11 = (f32[256,256]{1,0:T(8,128)S(1)}, f32[256,256]{1,0:T(8,128)S(1)}, u32[]{:S(2)}, u32[]{:S(2)}) collective-permute-start(f32[256,256]{1,0:T(8,128)S(1)} %add_add_fusion.1), channel_id=1, source_target_pairs={{0,32},{4,36},{12,44},{8,40},{128,160},{132,164},{140,172},{136,16... | collective-permute-start | bytes 786440 | tf_op jit(solution)/shard_map/ppermute | solution.py:165
  50.3 1.3 %collective-permute-start.10 = (f32[256,256]{1,0:T(8,128)S(1)}, f32[256,256]{1,0:T(8,128)S(1)}, u32[]{:S(2)}, u32[]{:S(2)}) collective-permute-start(f32[256,256]{1,0:T(8,128)S(1)} %add_add_fusion.1), channel_id=1, source_target_pairs={{0,16},{4,20},{12,28},{8,24},{128,144},{132,148},{140,156},{136,15... | collective-permute-start | bytes 786440 | tf_op jit(solution)/shard_map/ppermute | solution.py:165
  51.6 0.1 broadcast_select_fusion
  51.7 3.0 %collective-permute-start.14 = (f32[512,256]{1,0:T(8,128)S(1)}, f32[512,256]{1,0:T(8,128)S(1)}, u32[]{:S(2)}, u32[]{:S(2)}) collective-permute-start(f32[512,256]{1,0:T(8,128)S(1)} %get-tuple-element.3), channel_id=1, source_target_pairs={{0,2},{2,3},{3,4},{4,5},{5,6},{6,7},{7,8},{8,9},{9,10},{10,11},{11... | collective-permute-start | bytes 1572872 | tf_op jit(solution)/shard_map/ppermute | solution.py:165
  54.8 2.2 %collective-permute-done.10 = f32[256,256]{1,0:T(8,128)S(1)} collective-permute-done((f32[256,256]{1,0:T(8,128)S(1)}, f32[256,256]{1,0:T(8,128)S(1)}, u32[]{:S(2)}, u32[]{:S(2)}) %collective-permute-start.10) | collective-permute-done | bytes 262176 | tf_op jit(solution)/shard_map/ppermute | solution.py:165
  57.0 0.1 add_add_fusion
  57.0 2.2 %all-gather = f32[512,256]{1,0:T(8,128)S(1)} all-gather(f32[256,256]{1,0:T(8,128)S(1)} %add_add_fusion), channel_id=2, replica_groups={{0,1},{2,3},{4,5},{6,7},{8,9},{10,11},{12,13},{14,15},{16,17},{18,19},{..., dimensions={0}, use_global_device_ids=true | all-gather | bytes 786432 | tf_op jit(solution)/shard_map/all_gather | solution.py:197
  59.2 7.2 %collective-permute-done.14.back2_ref = f32[512,256]{1,0:T(8,128)S(1)} collective-permute-done((f32[512,256]{1,0:T(8,128)S(1)}, f32[512,256]{1,0:T(8,128)S(1)}, u32[]{:S(2)}, u32[]{:S(2)}) %collective-permute-start.14) | collective-permute-done | bytes 524320 | tf_op jit(solution)/shard_map/ppermute | solution.py:165
  66.5 4.9 %shard_map.43 = (f32[256,256]{1,0:T(8,128)}, f32[256,256]{1,0:T(8,128)}) custom-call(f32[2,256,256]{2,1,0:T(8,128)S(1)} %bitcast.2, f32[512,256]{1,0:T(8,128)S(1)} %collective-permute-done.14.back2_ref, f32[512,256]{1,0:T(8,128)S(1)} %get-tuple-element.2.back1_ref, f32[512,256]{1,0:T(8,128)S(1)} %shard_map.41.own_ref), custom_call_target="tpu_custom_call" | custom-call | tf_op jit(solution)/shard_map/pallas_call | solution.py:198
  (7 shorter events, 0.0 us)
Async XLA Ops:
  1.7 0.7 collective-permute-start
  2.4 2.1 %collective-permute-start.3 = (f32[256,256]{1,0:T(8,128)S(1)}, f32[256,256]{1,0:T(8,128)S(1)}, u32[]{:S(2)}, u32[]{:S(2)}) collective-permute-start(f32[256,256]{1,0:T(8,128)S(1)} %shard_map.42), channel_id=1, source_target_pairs={{0,8},{1,129}} | collective-permute-start | bytes 786440 | tf_op jit(solution)/shard_map/ppermute | solution.py:165
  3.1 1.4 %collective-permute-start.2 = (f32[256,256]{1,0:T(8,128)S(1)}, f32[256,256]{1,0:T(8,128)S(1)}, u32[]{:S(2)}, u32[]{:S(2)}) collective-permute-start(f32[256,256]{1,0:T(8,128)S(1)} %shard_map.42), channel_id=1, source_target_pairs={{0,12},{1,385}} | collective-permute-start | bytes 786440 | tf_op jit(solution)/shard_map/ppermute | solution.py:165
  3.8 0.7 collective-permute-start.1
  4.6 32.3 %collective-permute-start.6 = (f32[256,256]{1,0:T(8,128)S(1)}, f32[256,256]{1,0:T(8,128)S(1)}, u32[]{:S(2)}, u32[]{:S(2)}) collective-permute-start(f32[256,256]{1,0:T(8,128)S(1)} %add_add_fusion.3), channel_id=1, source_target_pairs={{0,384},{4,388},{12,396},{8,392},{1,9},{257,265},{385,393},{129,137}} | collective-permute-start | bytes 786440 | tf_op jit(solution)/shard_map/ppermute | solution.py:165
  5.3 31.6 %collective-permute-start.5 = (f32[256,256]{1,0:T(8,128)S(1)}, f32[256,256]{1,0:T(8,128)S(1)}, u32[]{:S(2)}, u32[]{:S(2)}) collective-permute-start(f32[256,256]{1,0:T(8,128)S(1)} %add_add_fusion.3), channel_id=1, source_target_pairs={{0,256},{4,260},{12,268},{8,264},{1,13},{257,269},{385,397},{129,1... | collective-permute-start | bytes 786440 | tf_op jit(solution)/shard_map/ppermute | solution.py:165
  6.6 30.3 %collective-permute-start.4 = (f32[256,256]{1,0:T(8,128)S(1)}, f32[256,256]{1,0:T(8,128)S(1)}, u32[]{:S(2)}, u32[]{:S(2)}) collective-permute-start(f32[256,256]{1,0:T(8,128)S(1)} %add_add_fusion.3), channel_id=1, source_target_pairs={{0,128},{4,132},{12,140},{8,136},{1,5},{257,261},{385,389},{129,133}} | collective-permute-start | bytes 786440 | tf_op jit(solution)/shard_map/ppermute | solution.py:165
  7.3 44.3 %collective-permute-start.13 = (f32[512,256]{1,0:T(8,128)S(1)}, f32[512,256]{1,0:T(8,128)S(1)}, u32[]{:S(2)}, u32[]{:S(2)}) collective-permute-start(f32[512,256]{1,0:T(8,128)S(1)} %shard_map.41.own_ref), channel_id=1, source_target_pairs={{1,2},{2,3},{3,4},{4,5},{5,6},{6,7},{7,8},{8,9},{9,10},{10,11},{11... | collective-permute-start | bytes 1572872 | tf_op jit(solution)/shard_map/ppermute | solution.py:165
  37.0 5.2 %collective-permute-start.9 = (f32[256,256]{1,0:T(8,128)S(1)}, f32[256,256]{1,0:T(8,128)S(1)}, u32[]{:S(2)}, u32[]{:S(2)}) collective-permute-start(f32[256,256]{1,0:T(8,128)S(1)} %add_add_fusion.2), channel_id=1, source_target_pairs={{0,78},{4,66},{12,74},{8,70},{128,206},{132,194},{140,202},{136,19... | collective-permute-start | bytes 786440 | tf_op jit(solution)/shard_map/ppermute | solution.py:165
  38.3 6.7 %collective-permute-start.8 = (f32[256,256]{1,0:T(8,128)S(1)}, f32[256,256]{1,0:T(8,128)S(1)}, u32[]{:S(2)}, u32[]{:S(2)}) collective-permute-start(f32[256,256]{1,0:T(8,128)S(1)} %add_add_fusion.2), channel_id=1, source_target_pairs={{0,14},{4,2},{12,10},{8,6},{128,142},{132,130},{140,138},{136,134}... | collective-permute-start | bytes 786440 | tf_op jit(solution)/shard_map/ppermute | solution.py:165
  39.6 8.0 %collective-permute-start.7 = (f32[256,256]{1,0:T(8,128)S(1)}, f32[256,256]{1,0:T(8,128)S(1)}, u32[]{:S(2)}, u32[]{:S(2)}) collective-permute-start(f32[256,256]{1,0:T(8,128)S(1)} %add_add_fusion.2), channel_id=1, source_target_pairs={{0,64},{4,68},{12,76},{8,72},{128,192},{132,196},{140,204},{136,20... | collective-permute-start | bytes 786440 | tf_op jit(solution)/shard_map/ppermute | solution.py:165
  47.7 7.1 %collective-permute-start.12 = (f32[256,256]{1,0:T(8,128)S(1)}, f32[256,256]{1,0:T(8,128)S(1)}, u32[]{:S(2)}, u32[]{:S(2)}) collective-permute-start(f32[256,256]{1,0:T(8,128)S(1)} %add_add_fusion.1), channel_id=1, source_target_pairs={{0,112},{4,116},{12,124},{8,120},{128,240},{132,244},{140,252},{13... | collective-permute-start | bytes 786440 | tf_op jit(solution)/shard_map/ppermute | solution.py:165
  49.0 5.8 %collective-permute-start.11 = (f32[256,256]{1,0:T(8,128)S(1)}, f32[256,256]{1,0:T(8,128)S(1)}, u32[]{:S(2)}, u32[]{:S(2)}) collective-permute-start(f32[256,256]{1,0:T(8,128)S(1)} %add_add_fusion.1), channel_id=1, source_target_pairs={{0,32},{4,36},{12,44},{8,40},{128,160},{132,164},{140,172},{136,16... | collective-permute-start | bytes 786440 | tf_op jit(solution)/shard_map/ppermute | solution.py:165
  50.3 6.7 %collective-permute-start.10 = (f32[256,256]{1,0:T(8,128)S(1)}, f32[256,256]{1,0:T(8,128)S(1)}, u32[]{:S(2)}, u32[]{:S(2)}) collective-permute-start(f32[256,256]{1,0:T(8,128)S(1)} %add_add_fusion.1), channel_id=1, source_target_pairs={{0,16},{4,20},{12,28},{8,24},{128,144},{132,148},{140,156},{136,15... | collective-permute-start | bytes 786440 | tf_op jit(solution)/shard_map/ppermute | solution.py:165
  51.7 14.7 %collective-permute-start.14 = (f32[512,256]{1,0:T(8,128)S(1)}, f32[512,256]{1,0:T(8,128)S(1)}, u32[]{:S(2)}, u32[]{:S(2)}) collective-permute-start(f32[512,256]{1,0:T(8,128)S(1)} %get-tuple-element.3), channel_id=1, source_target_pairs={{0,2},{2,3},{3,4},{4,5},{5,6},{6,7},{7,8},{8,9},{9,10},{10,11},{11... | collective-permute-start | bytes 1572872 | tf_op jit(solution)/shard_map/ppermute | solution.py:165

commit v9 on v5

--- a/solution.py
+++ b/solution.py
@@ -18,16 +18,16 @@
 
 TREE = (
     (
-        ((0, 2, 0), (0, -2, 0), (0, -4, 0)),
         ((0, 0, 4), (0, 0, -2), (0, 0, 2)),
-        ((2, 0, 0), (-1, 0, 0), (1, 0, 0)),
-        ((0, -1, -1), (0, -1, 0), (0, 0, -1)),
+        ((0, 2, 0), (0, 4, 0), (0, -2, 0)),
+        ((1, 0, 0), (-1, 0, 0), (2, 0, 0)),
+        ((0, 0, -1), (0, 1, 0), (0, 1, -1)),
     ),
     (
-        ((0, 0, -4), (0, 0, -2), (0, 0, 2)),
-        ((0, 2, 0), (0, -2, 0), (0, -4, 0)),
-        ((0, -1, -1), (0, -1, 0), (0, 0, -1)),
         ((2, 0, 0), (-1, 0, 0), (1, 0, 0)),
+        ((0, 0, 2), (0, 0, -2), (0, 0, 4)),
+        ((0, 2, 0), (0, -2, 0), (0, 4, 0)),
+        ((0, 0, 1), (0, -1, 0), (0, -1, 1)),
     ),
 )
 
@@ -185,8 +185,8 @@
         out_specs=VMEM,
     )(jnp.reshape(me, (1,)).astype(jnp.int32), *resident(own, second))
 
+    back2 = send(jnp.where(me == 0, own, back1), [(0, 2)] + onward[1:])
     back1 = jnp.where(me == 1, second, back1)
-    back2 = send(back1, onward)
     rounds = tree_rounds()
     for permutes in rounds:
         arrived = [send(held, pairs) for pairs in permutes]

time: 78.6 us -> 73.5 us (0.935)
  the two profiles are of different devices: /device:TPU:4 before, /device:TPU:2 now
where the time goes in v9:
time: 73.5 us; the launch traced here: 73.1 us
  starting transfers between devices  33.4 us (45%)
  waiting for transfers between devices  30.3 us (41%)
  Pallas kernels  5.99 us (8%)
  blocking collectives  2.18 us (3%)
  between operations  0.89 us (1%)
    ppermute x15, starting transfers between devices, send(): return lax.ppermute(array, AXIS, pairs)  33.4 us
    ppermute x15, waiting for transfers between devices, send(): return lax.ppermute(array, AXIS, pairs)  30.3 us
    pallas_call x1, Pallas kernels, steps(): pl.pallas_call(apply_kernel, out_shape=[jax.ShapeDtypeStruct((B, B), jnp....  4.92 us
    all_gather x1, blocking collectives, steps(): both = lax.all_gather(held, AXIS, axis=0, axis_index_groups=cores)  2.18 us
  transfers between devices with their start and end apart: 15, of which 4 were waited for; matrix products, arithmetic and copies ran while one was open for 0% of the time, Pallas kernels for 0%

profile of v9, /device:TPU:2, one launch (start us, length us, event | category | flops | bytes accessed | tf_op | source)
XLA Modules:
  0.0 73.1 jit_solution(10421610390886014876)
XLA Ops:
  0.6 1.0 %shard_map.41.own_ref = f32[512,256]{1,0:T(8,128)S(1)} custom-call(f32[256,256]{1,0:T(8,128)} %p_ref.1, f32[256,256]{1,0:T(8,128)} %n_ref.1), custom_call_target="tpu_custom_call" | custom-call | tf_op jit(solution)/shard_map/pallas_call | solution.py:172
  1.7 0.7 collective-permute-start
  2.4 0.0 collective-permute-done.other_ref
  2.4 0.7 collective-permute-start.3
  3.1 0.7 collective-permute-start.2
  3.8 0.7 collective-permute-start.1
  4.5 0.0 collective-permute-done.3
  4.5 0.0 collective-permute-done.2
  4.5 0.1 add_add_fusion.3
  4.6 0.7 collective-permute-start.6
  5.3 0.7 collective-permute-start.5
  6.0 0.7 collective-permute-start.4
  6.7 20.2 %collective-permute-start.13 = (f32[512,256]{1,0:T(8,128)S(1)}, f32[512,256]{1,0:T(8,128)S(1)}, u32[]{:S(2)}, u32[]{:S(2)}) collective-permute-start(f32[512,256]{1,0:T(8,128)S(1)} %shard_map.41.own_ref), channel_id=1, source_target_pairs={{1,2},{2,3},{3,4},{4,5},{5,6},{6,7},{7,8},{8,9},{9,10},{10,11},{11... | collective-permute-start | bytes 1572872 | tf_op jit(solution)/shard_map/ppermute | solution.py:164
  26.8 0.0 collective-permute-done.6
  26.8 0.0 collective-permute-done.5
  26.9 0.1 add_add_fusion.2
  26.9 0.7 collective-permute-start.9
  27.6 0.7 collective-permute-start.8
  28.3 1.3 %collective-permute-start.7 = (f32[256,256]{1,0:T(8,128)S(1)}, f32[256,256]{1,0:T(8,128)S(1)}, u32[]{:S(2)}, u32[]{:S(2)}) collective-permute-start(f32[256,256]{1,0:T(8,128)S(1)} %add_add_fusion.2), channel_id=1, source_target_pairs={{0,128},{8,136},{12,140},{4,132},{32,160},{40,168},{44,172},{36,16... | collective-permute-start | bytes 786440 | tf_op jit(solution)/shard_map/ppermute | solution.py:164
  29.6 19.7 %collective-permute-done.7 = f32[256,256]{1,0:T(8,128)S(1)} collective-permute-done((f32[256,256]{1,0:T(8,128)S(1)}, f32[256,256]{1,0:T(8,128)S(1)}, u32[]{:S(2)}, u32[]{:S(2)}) %collective-permute-start.7) | collective-permute-done | bytes 262176 | tf_op jit(solution)/shard_map/ppermute | solution.py:164
  49.4 0.1 add_add_fusion.1
  49.4 1.3 %collective-permute-start.12 = (f32[256,256]{1,0:T(8,128)S(1)}, f32[256,256]{1,0:T(8,128)S(1)}, u32[]{:S(2)}, u32[]{:S(2)}) collective-permute-start(f32[256,256]{1,0:T(8,128)S(1)} %add_add_fusion.1), channel_id=1, source_target_pairs={{0,30},{8,22},{12,26},{4,18},{32,62},{40,54},{44,58},{36,50},{64,9... | collective-permute-start | bytes 786440 | tf_op jit(solution)/shard_map/ppermute | solution.py:164
  50.8 1.3 %collective-permute-start.11 = (f32[256,256]{1,0:T(8,128)S(1)}, f32[256,256]{1,0:T(8,128)S(1)}, u32[]{:S(2)}, u32[]{:S(2)}) collective-permute-start(f32[256,256]{1,0:T(8,128)S(1)} %add_add_fusion.1), channel_id=1, source_target_pairs={{0,16},{8,24},{12,28},{4,20},{32,48},{40,56},{44,60},{36,52},{64,8... | collective-permute-start | bytes 786440 | tf_op jit(solution)/shard_map/ppermute | solution.py:164
  52.1 1.3 %collective-permute-start.10 = (f32[256,256]{1,0:T(8,128)S(1)}, f32[256,256]{1,0:T(8,128)S(1)}, u32[]{:S(2)}, u32[]{:S(2)}) collective-permute-start(f32[256,256]{1,0:T(8,128)S(1)} %add_add_fusion.1), channel_id=1, source_target_pairs={{0,14},{8,6},{12,10},{4,2},{32,46},{40,38},{44,42},{36,34},{64,78}... | collective-permute-start | bytes 786440 | tf_op jit(solution)/shard_map/ppermute | solution.py:164
  53.4 0.1 broadcast_select_fusion
  53.5 1.9 %collective-permute-start.14 = (f32[512,256]{1,0:T(8,128)S(1)}, f32[512,256]{1,0:T(8,128)S(1)}, u32[]{:S(2)}, u32[]{:S(2)}) collective-permute-start(f32[512,256]{1,0:T(8,128)S(1)} %get-tuple-element.3), channel_id=1, source_target_pairs={{0,2},{2,3},{3,4},{4,5},{5,6},{6,7},{7,8},{8,9},{9,10},{10,11},{11... | collective-permute-start | bytes 1572872 | tf_op jit(solution)/shard_map/ppermute | solution.py:164
  55.4 0.5 collective-permute-done.11
  55.9 1.5 %collective-permute-done.10 = f32[256,256]{1,0:T(8,128)S(1)} collective-permute-done((f32[256,256]{1,0:T(8,128)S(1)}, f32[256,256]{1,0:T(8,128)S(1)}, u32[]{:S(2)}, u32[]{:S(2)}) %collective-permute-start.10) | collective-permute-done | bytes 262176 | tf_op jit(solution)/shard_map/ppermute | solution.py:164
  57.4 0.1 add_add_fusion
  57.5 2.2 %all-gather = f32[512,256]{1,0:T(8,128)S(1)} all-gather(f32[256,256]{1,0:T(8,128)S(1)} %add_add_fusion), channel_id=2, replica_groups={{0,1},{2,3},{4,5},{6,7},{8,9},{10,11},{12,13},{14,15},{16,17},{18,19},{..., dimensions={0}, use_global_device_ids=true | all-gather | bytes 786432 | tf_op jit(solution)/shard_map/all_gather | solution.py:196
  59.7 8.5 %collective-permute-done.14.back2_ref = f32[512,256]{1,0:T(8,128)S(1)} collective-permute-done((f32[512,256]{1,0:T(8,128)S(1)}, f32[512,256]{1,0:T(8,128)S(1)}, u32[]{:S(2)}, u32[]{:S(2)}) %collective-permute-start.14) | collective-permute-done | bytes 524320 | tf_op jit(solution)/shard_map/ppermute | solution.py:164
  68.2 4.9 %shard_map.43 = (f32[256,256]{1,0:T(8,128)}, f32[256,256]{1,0:T(8,128)}) custom-call(f32[2,256,256]{2,1,0:T(8,128)S(1)} %bitcast.2, f32[512,256]{1,0:T(8,128)S(1)} %collective-permute-done.14.back2_ref, f32[512,256]{1,0:T(8,128)S(1)} %get-tuple-element.2.back1_ref, f32[512,256]{1,0:T(8,128)S(1)} %shard_map.41.own_ref), custom_call_target="tpu_custom_call" | custom-call | tf_op jit(solution)/shard_map/pallas_call | solution.py:197
  (7 shorter events, 0.0 us)
Async XLA Ops:
  1.7 0.7 collective-permute-start
  2.4 2.1 %collective-permute-start.3 = (f32[256,256]{1,0:T(8,128)S(1)}, f32[256,256]{1,0:T(8,128)S(1)}, u32[]{:S(2)}, u32[]{:S(2)}) collective-permute-start(f32[256,256]{1,0:T(8,128)S(1)} %shard_map.42), channel_id=1, source_target_pairs={{0,4},{1,129}} | collective-permute-start | bytes 786440 | tf_op jit(solution)/shard_map/ppermute | solution.py:164
  3.1 1.4 %collective-permute-start.2 = (f32[256,256]{1,0:T(8,128)S(1)}, f32[256,256]{1,0:T(8,128)S(1)}, u32[]{:S(2)}, u32[]{:S(2)}) collective-permute-start(f32[256,256]{1,0:T(8,128)S(1)} %shard_map.42), channel_id=1, source_target_pairs={{0,12},{1,385}} | collective-permute-start | bytes 786440 | tf_op jit(solution)/shard_map/ppermute | solution.py:164
  3.8 0.7 collective-permute-start.1
  4.6 22.2 %collective-permute-start.6 = (f32[256,256]{1,0:T(8,128)S(1)}, f32[256,256]{1,0:T(8,128)S(1)}, u32[]{:S(2)}, u32[]{:S(2)}) collective-permute-start(f32[256,256]{1,0:T(8,128)S(1)} %add_add_fusion.3), channel_id=1, source_target_pairs={{0,96},{8,104},{12,108},{4,100},{1,9},{257,265},{385,393},{129,137}} | collective-permute-start | bytes 786440 | tf_op jit(solution)/shard_map/ppermute | solution.py:164
  5.3 21.6 %collective-permute-start.5 = (f32[256,256]{1,0:T(8,128)S(1)}, f32[256,256]{1,0:T(8,128)S(1)}, u32[]{:S(2)}, u32[]{:S(2)}) collective-permute-start(f32[256,256]{1,0:T(8,128)S(1)} %add_add_fusion.3), channel_id=1, source_target_pairs={{0,64},{8,72},{12,76},{4,68},{1,13},{257,269},{385,397},{129,141}} | collective-permute-start | bytes 786440 | tf_op jit(solution)/shard_map/ppermute | solution.py:164
  6.0 20.9 %collective-permute-start.4 = (f32[256,256]{1,0:T(8,128)S(1)}, f32[256,256]{1,0:T(8,128)S(1)}, u32[]{:S(2)}, u32[]{:S(2)}) collective-permute-start(f32[256,256]{1,0:T(8,128)S(1)} %add_add_fusion.3), channel_id=1, source_target_pairs={{0,32},{8,40},{12,44},{4,36},{1,5},{257,261},{385,389},{129,133}} | collective-permute-start | bytes 786440 | tf_op jit(solution)/shard_map/ppermute | solution.py:164
  6.7 46.7 %collective-permute-start.13 = (f32[512,256]{1,0:T(8,128)S(1)}, f32[512,256]{1,0:T(8,128)S(1)}, u32[]{:S(2)}, u32[]{:S(2)}) collective-permute-start(f32[512,256]{1,0:T(8,128)S(1)} %shard_map.41.own_ref), channel_id=1, source_target_pairs={{1,2},{2,3},{3,4},{4,5},{5,6},{6,7},{7,8},{8,9},{9,10},{10,11},{11... | collective-permute-start | bytes 1572872 | tf_op jit(solution)/shard_map/ppermute | solution.py:164
  26.9 2.7 %collective-permute-start.9 = (f32[256,256]{1,0:T(8,128)S(1)}, f32[256,256]{1,0:T(8,128)S(1)}, u32[]{:S(2)}, u32[]{:S(2)}) collective-permute-start(f32[256,256]{1,0:T(8,128)S(1)} %add_add_fusion.2), channel_id=1, source_target_pairs={{0,256},{8,264},{12,268},{4,260},{32,288},{40,296},{44,300},{36,29... | collective-permute-start | bytes 786440 | tf_op jit(solution)/shard_map/ppermute | solution.py:164
  27.6 2.0 %collective-permute-start.8 = (f32[256,256]{1,0:T(8,128)S(1)}, f32[256,256]{1,0:T(8,128)S(1)}, u32[]{:S(2)}, u32[]{:S(2)}) collective-permute-start(f32[256,256]{1,0:T(8,128)S(1)} %add_add_fusion.2), channel_id=1, source_target_pairs={{0,384},{8,392},{12,396},{4,388},{32,416},{40,424},{44,428},{36,42... | collective-permute-start | bytes 786440 | tf_op jit(solution)/shard_map/ppermute | solution.py:164
  28.3 21.1 %collective-permute-start.7 = (f32[256,256]{1,0:T(8,128)S(1)}, f32[256,256]{1,0:T(8,128)S(1)}, u32[]{:S(2)}, u32[]{:S(2)}) collective-permute-start(f32[256,256]{1,0:T(8,128)S(1)} %add_add_fusion.2), channel_id=1, source_target_pairs={{0,128},{8,136},{12,140},{4,132},{32,160},{40,168},{44,172},{36,16... | collective-permute-start | bytes 786440 | tf_op jit(solution)/shard_map/ppermute | solution.py:164
  49.4 6.0 %collective-permute-start.12 = (f32[256,256]{1,0:T(8,128)S(1)}, f32[256,256]{1,0:T(8,128)S(1)}, u32[]{:S(2)}, u32[]{:S(2)}) collective-permute-start(f32[256,256]{1,0:T(8,128)S(1)} %add_add_fusion.1), channel_id=1, source_target_pairs={{0,30},{8,22},{12,26},{4,18},{32,62},{40,54},{44,58},{36,50},{64,9... | collective-permute-start | bytes 786440 | tf_op jit(solution)/shard_map/ppermute | solution.py:164
  50.8 5.2 %collective-permute-start.11 = (f32[256,256]{1,0:T(8,128)S(1)}, f32[256,256]{1,0:T(8,128)S(1)}, u32[]{:S(2)}, u32[]{:S(2)}) collective-permute-start(f32[256,256]{1,0:T(8,128)S(1)} %add_add_fusion.1), channel_id=1, source_target_pairs={{0,16},{8,24},{12,28},{4,20},{32,48},{40,56},{44,60},{36,52},{64,8... | collective-permute-start | bytes 786440 | tf_op jit(solution)/shard_map/ppermute | solution.py:164
  52.1 5.4 %collective-permute-start.10 = (f32[256,256]{1,0:T(8,128)S(1)}, f32[256,256]{1,0:T(8,128)S(1)}, u32[]{:S(2)}, u32[]{:S(2)}) collective-permute-start(f32[256,256]{1,0:T(8,128)S(1)} %add_add_fusion.1), channel_id=1, source_target_pairs={{0,14},{8,6},{12,10},{4,2},{32,46},{40,38},{44,42},{36,34},{64,78}... | collective-permute-start | bytes 786440 | tf_op jit(solution)/shard_map/ppermute | solution.py:164
  53.5 14.7 %collective-permute-start.14 = (f32[512,256]{1,0:T(8,128)S(1)}, f32[512,256]{1,0:T(8,128)S(1)}, u32[]{:S(2)}, u32[]{:S(2)}) collective-permute-start(f32[512,256]{1,0:T(8,128)S(1)} %get-tuple-element.3), channel_id=1, source_target_pairs={{0,2},{2,3},{3,4},{4,5},{5,6},{6,7},{7,8},{8,9},{9,10},{10,11},{11... | collective-permute-start | bytes 1572872 | tf_op jit(solution)/shard_map/ppermute | solution.py:164

commit v10 on v9

--- a/solution.py
+++ b/solution.py
@@ -60,9 +60,10 @@
 
 
 def dot(a, b):
-    left = jnp.concatenate([a[0], a[0], a[1]], axis=1)
-    right = jnp.concatenate([b[0], b[1], b[0]], axis=0)
-    return jnp.dot(left, right, preferred_element_type=jnp.float32)
+    rows = a[0].shape[0]
+    both = jnp.dot(jnp.concatenate([a[0], a[1]], axis=0), b[0], preferred_element_type=jnp.float32)
+    cross = jnp.dot(a[0], b[1], preferred_element_type=jnp.float32)
+    return both[:rows] + (both[rows:] + cross)
 
 
 def eye():
@@ -134,7 +135,7 @@
         out_ref[...] = jnp.where(me == 0, k0, k1)
 
 
-def apply_kernel(k_ref, back2_ref, back1_ref, own_ref, p_ref, n_ref):
+def apply_kernel(k_ref, back2_ref, back1_ref, own_ref, p_ref, n_ref, p_buf, n_buf, sems):
     identity = eye()
     k0, k1 = k_ref[0], k_ref[1]
     h0, t0 = halves(k0), halves(k0.T)
@@ -147,8 +148,14 @@
     cat = lambda a, b: jnp.concatenate([a, b], axis=1)
     first_p = dot(top0, halves(cat(p2, p1) - dot(t0, halves(cat(n2, n1)))))
     first_n = dot(bottom0, halves(cat(n1, n0) - dot(h0, halves(cat(p1, p0)))))
-    p_ref[...] = dot(top1, halves(first_p[:, :B] - dot(t1, halves(first_n[:, :B]))))
-    n_ref[...] = dot(bottom1, halves(first_n[:, B:] - dot(h1, halves(first_p[:, B:]))))
+    n_buf[...] = dot(bottom1, halves(first_n[:, B:] - dot(h1, halves(first_p[:, B:]))))
+    n_copy = pltpu.make_async_copy(n_buf, n_ref, sems.at[0])
+    n_copy.start()
+    p_buf[...] = dot(top1, halves(first_p[:, :B] - dot(t1, halves(first_n[:, :B]))))
+    p_copy = pltpu.make_async_copy(p_buf, p_ref, sems.at[1])
+    p_copy.start()
+    n_copy.wait()
+    p_copy.wait()
 
 
 VMEM = pl.BlockSpec(memory_space=pltpu.VMEM)
@@ -198,7 +205,8 @@
         apply_kernel,
         out_shape=[jax.ShapeDtypeStruct((B, B), jnp.float32)] * 2,
         in_specs=[VMEM] * 4,
-        out_specs=[VMEM] * 2,
+        out_specs=[ANY] * 2,
+        scratch_shapes=[pltpu.VMEM((B, B), jnp.float32)] * 2 + [pltpu.SemaphoreType.DMA((2,))],
     )(*resident(both, back2, back1, own))
 
 

time: 73.5 us -> 73.5 us (level)
  no operation moved by 1% of the time
where the time goes in v10:
time: 73.5 us; the launch traced here: 73.1 us
  starting transfers between devices  33.5 us (46%)
  waiting for transfers between devices  30.2 us (41%)
  Pallas kernels  5.99 us (8%)
  blocking collectives  2.18 us (3%)
  between operations  0.89 us (1%)
    ppermute x15, starting transfers between devices, send(): return lax.ppermute(array, AXIS, pairs)  33.5 us
    ppermute x15, waiting for transfers between devices, send(): return lax.ppermute(array, AXIS, pairs)  30.2 us
    pallas_call x1, Pallas kernels, steps(): pl.pallas_call(apply_kernel, out_shape=[jax.ShapeDtypeStruct((B, B), jnp....  4.91 us
    all_gather x1, blocking collectives, steps(): both = lax.all_gather(held, AXIS, axis=0, axis_index_groups=cores)  2.18 us
  transfers between devices with their start and end apart: 15, of which 4 were waited for; matrix products, arithmetic and copies ran while one was open for 0% of the time, Pallas kernels for 0%

profile of v10, /device:TPU:2, one launch (start us, length us, event | category | flops | bytes accessed | tf_op | source)
XLA Modules:
  0.0 73.1 jit_solution(15331246757354075479)
XLA Ops:
  0.6 1.0 %shard_map.41.own_ref = f32[512,256]{1,0:T(8,128)S(1)} custom-call(f32[256,256]{1,0:T(8,128)} %p_ref.1, f32[256,256]{1,0:T(8,128)} %n_ref.1), custom_call_target="tpu_custom_call" | custom-call | tf_op jit(solution)/shard_map/pallas_call | solution.py:179
  1.7 0.7 collective-permute-start
  2.4 0.0 collective-permute-done.other_ref
  2.4 0.7 collective-permute-start.3
  3.1 0.7 collective-permute-start.2
  3.8 0.7 collective-permute-start.1
  4.5 0.0 collective-permute-done.3
  4.5 0.0 collective-permute-done.2
  4.5 0.1 add_add_fusion.3
  4.6 0.7 collective-permute-start.6
  5.3 0.7 collective-permute-start.5
  6.0 0.7 collective-permute-start.4
  6.7 20.2 %collective-permute-start.13 = (f32[512,256]{1,0:T(8,128)S(1)}, f32[512,256]{1,0:T(8,128)S(1)}, u32[]{:S(2)}, u32[]{:S(2)}) collective-permute-start(f32[512,256]{1,0:T(8,128)S(1)} %shard_map.41.own_ref), channel_id=1, source_target_pairs={{1,2},{2,3},{3,4},{4,5},{5,6},{6,7},{7,8},{8,9},{9,10},{10,11},{11... | collective-permute-start | bytes 1572872 | tf_op jit(solution)/shard_map/ppermute | solution.py:171
  26.9 0.0 collective-permute-done.4
  26.9 0.1 add_add_fusion.2
  27.0 0.7 collective-permute-start.9
  27.7 0.7 collective-permute-start.8
  28.4 1.3 %collective-permute-start.7 = (f32[256,256]{1,0:T(8,128)S(1)}, f32[256,256]{1,0:T(8,128)S(1)}, u32[]{:S(2)}, u32[]{:S(2)}) collective-permute-start(f32[256,256]{1,0:T(8,128)S(1)} %add_add_fusion.2), channel_id=1, source_target_pairs={{0,128},{8,136},{12,140},{4,132},{32,160},{40,168},{44,172},{36,16... | collective-permute-start | bytes 786440 | tf_op jit(solution)/shard_map/ppermute | solution.py:171
  29.7 0.0 collective-permute-done.8
  29.7 19.6 %collective-permute-done.7 = f32[256,256]{1,0:T(8,128)S(1)} collective-permute-done((f32[256,256]{1,0:T(8,128)S(1)}, f32[256,256]{1,0:T(8,128)S(1)}, u32[]{:S(2)}, u32[]{:S(2)}) %collective-permute-start.7) | collective-permute-done | bytes 262176 | tf_op jit(solution)/shard_map/ppermute | solution.py:171
  49.3 0.1 add_add_fusion.1
  49.4 1.3 %collective-permute-start.12 = (f32[256,256]{1,0:T(8,128)S(1)}, f32[256,256]{1,0:T(8,128)S(1)}, u32[]{:S(2)}, u32[]{:S(2)}) collective-permute-start(f32[256,256]{1,0:T(8,128)S(1)} %add_add_fusion.1), channel_id=1, source_target_pairs={{0,30},{8,22},{12,26},{4,18},{32,62},{40,54},{44,58},{36,50},{64,9... | collective-permute-start | bytes 786440 | tf_op jit(solution)/shard_map/ppermute | solution.py:171
  50.7 1.3 %collective-permute-start.11 = (f32[256,256]{1,0:T(8,128)S(1)}, f32[256,256]{1,0:T(8,128)S(1)}, u32[]{:S(2)}, u32[]{:S(2)}) collective-permute-start(f32[256,256]{1,0:T(8,128)S(1)} %add_add_fusion.1), channel_id=1, source_target_pairs={{0,16},{8,24},{12,28},{4,20},{32,48},{40,56},{44,60},{36,52},{64,8... | collective-permute-start | bytes 786440 | tf_op jit(solution)/shard_map/ppermute | solution.py:171
  52.0 1.3 %collective-permute-start.10 = (f32[256,256]{1,0:T(8,128)S(1)}, f32[256,256]{1,0:T(8,128)S(1)}, u32[]{:S(2)}, u32[]{:S(2)}) collective-permute-start(f32[256,256]{1,0:T(8,128)S(1)} %add_add_fusion.1), channel_id=1, source_target_pairs={{0,14},{8,6},{12,10},{4,2},{32,46},{40,38},{44,42},{36,34},{64,78}... | collective-permute-start | bytes 786440 | tf_op jit(solution)/shard_map/ppermute | solution.py:171
  53.4 0.1 broadcast_select_fusion
  53.5 1.9 %collective-permute-start.14 = (f32[512,256]{1,0:T(8,128)S(1)}, f32[512,256]{1,0:T(8,128)S(1)}, u32[]{:S(2)}, u32[]{:S(2)}) collective-permute-start(f32[512,256]{1,0:T(8,128)S(1)} %get-tuple-element.3), channel_id=1, source_target_pairs={{0,2},{2,3},{3,4},{4,5},{5,6},{6,7},{7,8},{8,9},{9,10},{10,11},{11... | collective-permute-start | bytes 1572872 | tf_op jit(solution)/shard_map/ppermute | solution.py:171
  55.4 0.5 collective-permute-done.11
  55.9 1.5 %collective-permute-done.10 = f32[256,256]{1,0:T(8,128)S(1)} collective-permute-done((f32[256,256]{1,0:T(8,128)S(1)}, f32[256,256]{1,0:T(8,128)S(1)}, u32[]{:S(2)}, u32[]{:S(2)}) %collective-permute-start.10) | collective-permute-done | bytes 262176 | tf_op jit(solution)/shard_map/ppermute | solution.py:171
  57.4 0.1 add_add_fusion
  57.5 2.2 %all-gather = f32[512,256]{1,0:T(8,128)S(1)} all-gather(f32[256,256]{1,0:T(8,128)S(1)} %add_add_fusion), channel_id=2, replica_groups={{0,1},{2,3},{4,5},{6,7},{8,9},{10,11},{12,13},{14,15},{16,17},{18,19},{..., dimensions={0}, use_global_device_ids=true | all-gather | bytes 786432 | tf_op jit(solution)/shard_map/all_gather | solution.py:203
  59.6 8.5 %collective-permute-done.14.back2_ref = f32[512,256]{1,0:T(8,128)S(1)} collective-permute-done((f32[512,256]{1,0:T(8,128)S(1)}, f32[512,256]{1,0:T(8,128)S(1)}, u32[]{:S(2)}, u32[]{:S(2)}) %collective-permute-start.14) | collective-permute-done | bytes 524320 | tf_op jit(solution)/shard_map/ppermute | solution.py:171
  68.2 4.9 %shard_map.43 = (f32[256,256]{1,0:T(8,128)}, f32[256,256]{1,0:T(8,128)}) custom-call(f32[2,256,256]{2,1,0:T(8,128)S(1)} %bitcast.2, f32[512,256]{1,0:T(8,128)S(1)} %collective-permute-done.14.back2_ref, f32[512,256]{1,0:T(8,128)S(1)} %get-tuple-element.2.back1_ref, f32[512,256]{1,0:T(8,128)S(1)} %shard_map.41.own_ref), custom_call_target="tpu_custom_call" | custom-call | tf_op jit(solution)/shard_map/pallas_call | solution.py:204
  (7 shorter events, 0.0 us)
Async XLA Ops:
  1.7 0.7 collective-permute-start
  2.4 2.1 %collective-permute-start.3 = (f32[256,256]{1,0:T(8,128)S(1)}, f32[256,256]{1,0:T(8,128)S(1)}, u32[]{:S(2)}, u32[]{:S(2)}) collective-permute-start(f32[256,256]{1,0:T(8,128)S(1)} %shard_map.42), channel_id=1, source_target_pairs={{0,4},{1,129}} | collective-permute-start | bytes 786440 | tf_op jit(solution)/shard_map/ppermute | solution.py:171
  3.1 1.4 %collective-permute-start.2 = (f32[256,256]{1,0:T(8,128)S(1)}, f32[256,256]{1,0:T(8,128)S(1)}, u32[]{:S(2)}, u32[]{:S(2)}) collective-permute-start(f32[256,256]{1,0:T(8,128)S(1)} %shard_map.42), channel_id=1, source_target_pairs={{0,12},{1,385}} | collective-permute-start | bytes 786440 | tf_op jit(solution)/shard_map/ppermute | solution.py:171
  3.8 0.7 collective-permute-start.1
  4.6 22.3 %collective-permute-start.6 = (f32[256,256]{1,0:T(8,128)S(1)}, f32[256,256]{1,0:T(8,128)S(1)}, u32[]{:S(2)}, u32[]{:S(2)}) collective-permute-start(f32[256,256]{1,0:T(8,128)S(1)} %add_add_fusion.3), channel_id=1, source_target_pairs={{0,96},{8,104},{12,108},{4,100},{1,9},{257,265},{385,393},{129,137}} | collective-permute-start | bytes 786440 | tf_op jit(solution)/shard_map/ppermute | solution.py:171
  5.3 21.6 %collective-permute-start.5 = (f32[256,256]{1,0:T(8,128)S(1)}, f32[256,256]{1,0:T(8,128)S(1)}, u32[]{:S(2)}, u32[]{:S(2)}) collective-permute-start(f32[256,256]{1,0:T(8,128)S(1)} %add_add_fusion.3), channel_id=1, source_target_pairs={{0,64},{8,72},{12,76},{4,68},{1,13},{257,269},{385,397},{129,141}} | collective-permute-start | bytes 786440 | tf_op jit(solution)/shard_map/ppermute | solution.py:171
  6.0 20.9 %collective-permute-start.4 = (f32[256,256]{1,0:T(8,128)S(1)}, f32[256,256]{1,0:T(8,128)S(1)}, u32[]{:S(2)}, u32[]{:S(2)}) collective-permute-start(f32[256,256]{1,0:T(8,128)S(1)} %add_add_fusion.3), channel_id=1, source_target_pairs={{0,32},{8,40},{12,44},{4,36},{1,5},{257,261},{385,389},{129,133}} | collective-permute-start | bytes 786440 | tf_op jit(solution)/shard_map/ppermute | solution.py:171
  6.7 46.7 %collective-permute-start.13 = (f32[512,256]{1,0:T(8,128)S(1)}, f32[512,256]{1,0:T(8,128)S(1)}, u32[]{:S(2)}, u32[]{:S(2)}) collective-permute-start(f32[512,256]{1,0:T(8,128)S(1)} %shard_map.41.own_ref), channel_id=1, source_target_pairs={{1,2},{2,3},{3,4},{4,5},{5,6},{6,7},{7,8},{8,9},{9,10},{10,11},{11... | collective-permute-start | bytes 1572872 | tf_op jit(solution)/shard_map/ppermute | solution.py:171
  27.0 2.7 %collective-permute-start.9 = (f32[256,256]{1,0:T(8,128)S(1)}, f32[256,256]{1,0:T(8,128)S(1)}, u32[]{:S(2)}, u32[]{:S(2)}) collective-permute-start(f32[256,256]{1,0:T(8,128)S(1)} %add_add_fusion.2), channel_id=1, source_target_pairs={{0,256},{8,264},{12,268},{4,260},{32,288},{40,296},{44,300},{36,29... | collective-permute-start | bytes 786440 | tf_op jit(solution)/shard_map/ppermute | solution.py:171
  27.7 2.0 %collective-permute-start.8 = (f32[256,256]{1,0:T(8,128)S(1)}, f32[256,256]{1,0:T(8,128)S(1)}, u32[]{:S(2)}, u32[]{:S(2)}) collective-permute-start(f32[256,256]{1,0:T(8,128)S(1)} %add_add_fusion.2), channel_id=1, source_target_pairs={{0,384},{8,392},{12,396},{4,388},{32,416},{40,424},{44,428},{36,42... | collective-permute-start | bytes 786440 | tf_op jit(solution)/shard_map/ppermute | solution.py:171
  28.4 21.0 %collective-permute-start.7 = (f32[256,256]{1,0:T(8,128)S(1)}, f32[256,256]{1,0:T(8,128)S(1)}, u32[]{:S(2)}, u32[]{:S(2)}) collective-permute-start(f32[256,256]{1,0:T(8,128)S(1)} %add_add_fusion.2), channel_id=1, source_target_pairs={{0,128},{8,136},{12,140},{4,132},{32,160},{40,168},{44,172},{36,16... | collective-permute-start | bytes 786440 | tf_op jit(solution)/shard_map/ppermute | solution.py:171
  49.4 6.0 %collective-permute-start.12 = (f32[256,256]{1,0:T(8,128)S(1)}, f32[256,256]{1,0:T(8,128)S(1)}, u32[]{:S(2)}, u32[]{:S(2)}) collective-permute-start(f32[256,256]{1,0:T(8,128)S(1)} %add_add_fusion.1), channel_id=1, source_target_pairs={{0,30},{8,22},{12,26},{4,18},{32,62},{40,54},{44,58},{36,50},{64,9... | collective-permute-start | bytes 786440 | tf_op jit(solution)/shard_map/ppermute | solution.py:171
  50.7 5.2 %collective-permute-start.11 = (f32[256,256]{1,0:T(8,128)S(1)}, f32[256,256]{1,0:T(8,128)S(1)}, u32[]{:S(2)}, u32[]{:S(2)}) collective-permute-start(f32[256,256]{1,0:T(8,128)S(1)} %add_add_fusion.1), channel_id=1, source_target_pairs={{0,16},{8,24},{12,28},{4,20},{32,48},{40,56},{44,60},{36,52},{64,8... | collective-permute-start | bytes 786440 | tf_op jit(solution)/shard_map/ppermute | solution.py:171
  52.0 5.4 %collective-permute-start.10 = (f32[256,256]{1,0:T(8,128)S(1)}, f32[256,256]{1,0:T(8,128)S(1)}, u32[]{:S(2)}, u32[]{:S(2)}) collective-permute-start(f32[256,256]{1,0:T(8,128)S(1)} %add_add_fusion.1), channel_id=1, source_target_pairs={{0,14},{8,6},{12,10},{4,2},{32,46},{40,38},{44,42},{36,34},{64,78}... | collective-permute-start | bytes 786440 | tf_op jit(solution)/shard_map/ppermute | solution.py:171
  53.5 14.7 %collective-permute-start.14 = (f32[512,256]{1,0:T(8,128)S(1)}, f32[512,256]{1,0:T(8,128)S(1)}, u32[]{:S(2)}, u32[]{:S(2)}) collective-permute-start(f32[512,256]{1,0:T(8,128)S(1)} %get-tuple-element.3), channel_id=1, source_target_pairs={{0,2},{2,3},{3,4},{4,5},{5,6},{6,7},{7,8},{8,9},{9,10},{10,11},{11... | collective-permute-start | bytes 1572872 | tf_op jit(solution)/shard_map/ppermute | solution.py:171
